TPU v7x, 512 devices: a whole 4x8x8 slice. The times are simulated.
512 devices in a mesh: seq: 32 (over y, x), head: 16 (over z, core).
Axes of the slice: x: 4, y: 8, z: 8, core: 2. Of those that a mesh axis runs over, the one named last changes fastest.
Arguments:
- queries: bfloat16 [65536, 2048], P('seq', 'head'), may hold values from -4.5 to 4.5
- key_vectors: bfloat16 [65536, 2048], P('seq', 'head'), may hold values from -4.5 to 4.5
- value_vectors: bfloat16 [65536, 2048], P('seq', 'head'), may hold values from -18 to 18
- w_out: bfloat16 [2048, 2048], P('seq'), may hold values from -0.125 to 0.125
Outputs:
- projected: bfloat16 [65536, 2048], P(('seq', 'head'))
All inputs are finite; a program needn't handle non-finite values.
Results may differ from a plain program's by a relative error of at most 0.0053.
Values may be sent and summed in bfloat16 or wider, within the bound.
No kernel may reach another device: no remote copies, remote signals or barrier semaphores. Data moves between devices by JAX's collectives and lax.ppermute only.
A program may use at most 64 MiB of HBM per device.

v0:
```python
import math

import jax
import jax.numpy as jnp
from jax import lax
from jax.sharding import PartitionSpec as P

HD = 128
W = 1024


norm_eps = 1e-06


def passed_along(shard, axis, by):
    count = lax.axis_size(axis)
    pairs = [(i, i + by) for i in range(count) if 0 <= i + by < count]
    return lax.ppermute(shard, axis, pairs)


def carried_in(part, axis, combine, identity):
    place = lax.axis_index(axis)
    gathered = lax.all_gather(part, axis)
    state = jnp.zeros_like(part) + jnp.asarray(identity, part.dtype)

    def one(lap, state):
        return combine(state, lax.dynamic_index_in_dim(gathered, lap, 0, False))

    return lax.fori_loop(0, place, one, state)


def normalize(branch):
    return branch * lax.rsqrt(jnp.mean(branch * branch, axis=-1, keepdims=True) + norm_eps)


def add_states(earlier, later):
    return earlier + later


def split_pair(values):
    upper = lax.optimization_barrier(values.astype(jnp.bfloat16))
    lower = (values - upper.astype(jnp.float32)).astype(jnp.bfloat16)
    return (upper, lower)


def window_branch(query_heads, window_keys, window_values, offset):
    tok_rows, heads_here, head_width = query_heads.shape
    block_rows = min(512, tok_rows)
    key_span = block_rows + W
    score_scale = 1.0 / math.sqrt(head_width)

    def one_block(block_start):
        query_block = lax.dynamic_slice_in_dim(query_heads, block_start, block_rows, 0)
        key_block = lax.dynamic_slice_in_dim(window_keys, block_start, key_span, 0)
        value_block = lax.dynamic_slice_in_dim(window_values, block_start, key_span, 0)
        scores = (
            jnp.einsum("qhd,khd->hqk", query_block, key_block, preferred_element_type=jnp.float32)
            * score_scale
        )
        row_index = block_start + jnp.arange(block_rows, dtype=jnp.int32)[:, None]
        col_index = block_start + jnp.arange(key_span, dtype=jnp.int32)[None, :]
        allowed = (
            (col_index > row_index) & (col_index <= row_index + W) & (col_index - W + offset >= 0)
        )
        scores = jnp.where(allowed[None], scores, -jnp.inf)
        row_top = jnp.max(scores, axis=-1, keepdims=True)
        weights = jnp.where(allowed[None], jnp.exp(scores - row_top), 0.0).astype(jnp.bfloat16)
        return jnp.einsum("hqk,khd->qhd", weights, value_block, preferred_element_type=jnp.float32)

    starts = jnp.arange(tok_rows // block_rows, dtype=jnp.int32) * block_rows
    return lax.map(one_block, starts).reshape(tok_rows, heads_here, head_width)


def on_device(queries, key_vectors, value_vectors, w_out):
    tok_rows = queries.shape[0]
    heads_here = queries.shape[1] // HD
    head_shape = (tok_rows, heads_here, HD)
    query_heads = queries.reshape(head_shape)
    key_heads = key_vectors.reshape(head_shape)
    value_heads = value_vectors.reshape(head_shape)
    window_rim = jnp.stack([key_heads[tok_rows - W :], value_heads[tok_rows - W :]])
    earlier = passed_along(window_rim, "seq", 1)
    window_keys = jnp.concatenate([earlier[0], key_heads], axis=0)
    window_values = jnp.concatenate([earlier[1], value_heads], axis=0)
    offset = lax.axis_index("seq") * tok_rows
    soft_heads = window_branch(query_heads, window_keys, window_values, offset)
    block_rows = min(512, tok_rows)
    block_count = tok_rows // block_rows
    block_shape = (block_count, block_rows, heads_here, HD)
    blocked_queries = query_heads.reshape(block_shape)
    blocked_keys = key_heads.reshape(block_shape)
    blocked_values = value_heads.reshape(block_shape)
    state_increments = jnp.einsum(
        "bkhd,bkhe->bhde", blocked_keys, blocked_values, preferred_element_type=jnp.float32
    )
    own_total = jnp.sum(state_increments, axis=0)
    prior_state = carried_in(own_total, "seq", add_states, jnp.zeros_like(own_total))
    running = jnp.cumsum(state_increments, axis=0)
    preceding_state = prior_state[None] + jnp.concatenate(
        [jnp.zeros_like(state_increments[:1]), running[:-1]], axis=0
    )
    intra_block_scores = jnp.einsum(
        "bqhd,bkhd->bhqk", blocked_queries, blocked_keys, preferred_element_type=jnp.float32
    )
    causal = (
        jnp.arange(block_rows, dtype=jnp.int32)[:, None]
        >= jnp.arange(block_rows, dtype=jnp.int32)[None, :]
    )
    intra_block_scores = jnp.where(causal, intra_block_scores, 0.0)
    score_upper, score_lower = split_pair(intra_block_scores)
    local_block_terms = jnp.einsum(
        "bhqk,bkhd->bqhd", score_upper, blocked_values, preferred_element_type=jnp.float32
    )
    local_block_terms = local_block_terms + jnp.einsum(
        "bhqk,bkhd->bqhd", score_lower, blocked_values, preferred_element_type=jnp.float32
    )
    state_upper, state_lower = split_pair(preceding_state)
    carried_state_sum = jnp.einsum(
        "bqhd,bhde->bqhe", blocked_queries, state_upper, preferred_element_type=jnp.float32
    )
    carried_state_sum = carried_state_sum + jnp.einsum(
        "bqhd,bhde->bqhe", blocked_queries, state_lower, preferred_element_type=jnp.float32
    )
    linear = (local_block_terms + carried_state_sum).reshape(head_shape)
    mixed_heads = (0.5 * (normalize(soft_heads) + normalize(linear))).astype(jnp.bfloat16)
    mixed_heads = mixed_heads.reshape(tok_rows, heads_here * HD)
    regrouped = lax.all_to_all(mixed_heads, "head", split_axis=0, concat_axis=1, tiled=True)
    projected = jnp.dot(
        regrouped,
        lax.all_gather(w_out, "seq", axis=0, tiled=True),
        preferred_element_type=jnp.float32,
    )
    return projected.astype(jnp.bfloat16)


def solution(mesh):
    placed = (P("seq", "head"), P("seq", "head"), P("seq", "head"), P("seq", None))
    return jax.shard_map(
        on_device, mesh=mesh, in_specs=placed, out_specs=P(("seq", "head"), None), check_vma=False
    )
```

profile of v0, /device:TPU:1, one launch (start us, length us, event | category | flops | bytes accessed | tf_op | source)
XLA Modules:
  0.0 214.6 jit_solution(4155699273040618494)
XLA Ops:
  6.5 2.3 %fusion.41 = (f32[128,128]{1,0:T(8,128)}, f32[4,128,128]{2,1,0:T(8,128)S(1)}) fusion(bf16[4,512,128]{2,1,0:T(8,128)(2,1)} %bitcast.109, bf16[4,512,128]{2,1,0:T(8,128)(2,1)} %bitcast.105), kind=kOutput, calls=%fused_computation.63 | convolution fusion | flops 67158016 | bytes 1376256 | tf_op jit(solution)/shard_map/bkhd,bkhe->bhde/dot_general | solution.py:93
  8.9 0.7 all-gather.4.cloned.1.call-update
  9.6 1.1 slice_bitcast_fusion.2
  10.6 0.8 pad_maximum_fusion.2
  11.5 4.7 %collective-permute-start = (bf16[2,1024,1,128]{3,1,2,0:T(8,128)(2,1)}, bf16[2,1024,1,128]{3,1,2,0:T(8,128)(2,1)}, u32[]{:S(2)}, u32[]{:S(2)}) collective-permute-start(bf16[2,1024,1,128]{3,1,2,0:T(8,128)(2,1)} %pad_maximum_fusion.2), channel_id=1, source_target_pairs={{0,16},{16,32},{32,48},{48,64},{64,80},{80,96},{96,112},{112,128},... | collective-permute-start | bytes 1572872 | tf_op jit(solution)/shard_map/ppermute | solution.py:18
  16.3 0.7 fusion.42
  17.1 0.6 fusion.14
  17.7 0.4 copy-done
  18.1 1.8 fusion.16
  19.9 0.7 fusion.30
  20.6 0.9 slice.24
  21.6 2.9 %fusion.26 = f32[4,128,512]{1,2,0:T(8,128)} fusion(f32[4,512,128]{2,1,0:T(8,128)} %fusion.16, bf16[4,512,128]{2,1,0:T(8,128)(2,1)S(1)} %bitcast.107, bf16[4,1,512,512]{3,2,0,1:T(8,128)(2,1)S(1)} %fusion.14), kind=kOutput, calls=%fused_computation.35 | convolution fusion | flops 268697600 | bytes 4718592 | tf_op jit(solution)/shard_map/bhqk,bkhd->bqhd/dot_general | solution.py:111
  24.5 1.1 slice_bitcast_fusion
  25.8 36.6 %while.22 = (s32[]{:T(128)}, f32[4,512,1,128]{1,3,2,0:T(8,128)}, s32[4]{0:T(128)S(1)}, bf16[3072,1,128]{2,0,1:T(8,128)(2,1)S(1)}, s32[]{:T(128)}, /*index=5*/bf1...) while((s32[]{:T(128)}, f32[4,512,1,128]{1,3,2,0:T(8,128)}, ...), condition=%wide.region_2.3_spmd, body=%wide.region_0.2_spmd.sunk | while | flops 413671424 | bytes 7516368 | solution.py:71
  25.8 0.6 dynamic_slice.54
  29.6 0.6 iota_add_fusion.4
  30.2 0.7 add_compare_fusion.2
  30.9 0.7 iota_add_fusion.5
  31.6 1.2 fusion.57
  32.8 2.1 fusion.58
  34.9 0.6 dynamic_slice.54
  38.7 0.6 iota_add_fusion.4
  39.4 0.7 add_compare_fusion.2
  40.1 0.7 iota_add_fusion.5
  40.7 1.2 fusion.57
  41.9 2.1 fusion.58
  44.1 0.6 dynamic_slice.54
  47.9 0.6 iota_add_fusion.4
  48.5 0.7 add_compare_fusion.2
  49.2 0.7 iota_add_fusion.5
  49.9 1.2 fusion.57
  51.1 2.2 %fusion.58 = f32[4,512,1,128]{1,3,2,0:T(8,128)} fusion(f32[4,512,1,128]{1,3,2,0:T(8,128)} %get-tuple-element.263, s32[]{:T(128)} %get-tuple-element.262, f32[512,1536]{1,0:T(8,128)S(1)} %get-tuple-element.224, f32[512]{0:T(512)S(1)} %get-tuple-element.225, s32[1536]{0:T(1024)S(1)} %iota_add_fusion.5, s32[512]{0:T(512)S(1)} %get-tuple-element.222, ...), kind=kOutput, calls=%fused_computation.6.clone.1 | convolution fusion | flops 206831616 | bytes 3817988 | tf_op jit(solution)/shard_map/while/body/eval_jaxpr/hqk,khd->qhd/dot_general | solution.py:68
  53.2 0.6 dynamic_slice.54
  57.0 0.6 iota_add_fusion.4
  57.7 0.7 add_compare_fusion.2
  58.4 0.7 iota_add_fusion.5
  59.0 1.2 fusion.57
  60.2 2.2 %fusion.58 = f32[4,512,1,128]{1,3,2,0:T(8,128)} fusion(f32[4,512,1,128]{1,3,2,0:T(8,128)} %get-tuple-element.263, s32[]{:T(128)} %get-tuple-element.262, f32[512,1536]{1,0:T(8,128)S(1)} %get-tuple-element.224, f32[512]{0:T(512)S(1)} %get-tuple-element.225, s32[1536]{0:T(1024)S(1)} %iota_add_fusion.5, s32[512]{0:T(512)S(1)} %get-tuple-element.222, ...), kind=kOutput, calls=%fused_computation.6.clone.1 | convolution fusion | flops 206831616 | bytes 3817988 | tf_op jit(solution)/shard_map/while/body/eval_jaxpr/hqk,khd->qhd/dot_general | solution.py:68
  62.4 1.5 copy.11
  63.9 1.4 multiply_reduce_fusion
  65.3 29.2 %all-gather.6.cloned.1.call-done = f32[4096,128]{1,0:T(8,128)} async-done(((f32[128,128]{1,0:T(8,128)}), f32[4096,128]{1,0:T(8,128)}) %all-gather.6.cloned.1.call-update) | async-done | bytes 2097168 | tf_op jit(solution)/shard_map/all_gather | solution.py:23
  94.5 0.3 fusion.35
  94.8 1.7 fusion.29
  96.6 0.7 multiply_convert_fusion
  97.3 29.8 %all_to_all.16 = bf16[16,128,128]{2,1,0:T(8,128)(2,1)S(1)} all-to-all(bf16[16,128,128]{2,1,0:T(8,128)(2,1)S(1)} %multiply_convert_fusion), channel_id=1, replica_groups=mesh['seq'=32,'head'=16] {'head'}, dimensions={0} | all-to-all | bytes 1048576 | tf_op jit(solution)/shard_map/all_to_all | solution.py:127
  127.2 0.3 copy.17
  127.4 74.9 %all-gather.4.cloned.1.call-done = bf16[2048,2048]{1,0:T(8,128)(2,1)} async-done(((bf16[64,2048]{1,0:T(8,128)(2,1)}), bf16[2048,2048]{1,0:T(8,128)(2,1)}) %all-gather.4.cloned.1.call-update) | async-done | bytes 8388624 | tf_op jit(solution)/shard_map/all_gather | solution.py:130
  202.3 5.5 %convolution_convert_fusion = bf16[128,2048]{1,0:T(8,128)(2,1)} fusion(bf16[128,2048]{0,1:T(8,128)(2,1)S(1)} %bitcast.116, bf16[2048,2048]{1,0:T(8,128)(2,1)} %all-gather.4.cloned.1.call-done), kind=kOutput, calls=%fused_computation.24 | convolution fusion | flops 1074003968 | bytes 9437184 | tf_op jit(solution)/shard_map/dot_general | solution.py:128
  (23 shorter events, 0.3 us)
Async XLA Ops:
  6.5 9.8 %copy-start.1 = (bf16[2048,128]{1,0:T(8,128)(2,1)S(1)}, bf16[2048,128]{1,0:T(8,128)(2,1)}, u32[]{:S(2)}) copy-start(bf16[2048,128]{1,0:T(8,128)(2,1)} %param.9) | copy-start | bytes 1572868
  6.5 9.8 %copy-start.2 = (bf16[2048,128]{1,0:T(8,128)(2,1)S(1)}, bf16[2048,128]{1,0:T(8,128)(2,1)}, u32[]{:S(2)}) copy-start(bf16[2048,128]{1,0:T(8,128)(2,1)} %param.8) | copy-start | bytes 1572868
  6.5 88.0 %all-gather.6.cloned.1.call-start = ((), (), s32[]{:S(2)}) async-start(), calls=%async_computation.2 | async-start | bytes 2162688 | tf_op jit(solution)/shard_map/all_gather | solution.py:23
  8.8 193.5 %all-gather.4.cloned.1.call-start = ((), (), s32[]{:S(2)}) async-start(), calls=%async_computation.1 | async-start | bytes 8650752 | tf_op jit(solution)/shard_map/all_gather | solution.py:130
  11.5 13.0 %collective-permute-start = (bf16[2,1024,1,128]{3,1,2,0:T(8,128)(2,1)}, bf16[2,1024,1,128]{3,1,2,0:T(8,128)(2,1)}, u32[]{:S(2)}, u32[]{:S(2)}) collective-permute-start(bf16[2,1024,1,128]{3,1,2,0:T(8,128)(2,1)} %pad_maximum_fusion.2), channel_id=1, source_target_pairs={{0,16},{16,32},{32,48},{48,64},{64,80},{80,96},{96,112},{112,128},... | collective-permute-start | bytes 1572872 | tf_op jit(solution)/shard_map/ppermute | solution.py:18
  17.0 1.0 copy-start
  24.5 1.3 copy-start.3
Sparse Core Ops, SparseCore 0:
  10.5 83.9 all-gather.5
  97.7 104.5 all-gather.3
where the time goes:
time: 217 us; the launch traced here: 215 us
  waiting for transfers between devices  105 us (48%)
  blocking collectives  29.8 us (14%)
  matrix products  28.6 us (13%)
  between operations  13.5 us (6%)
  loops' own time  13 us (6%)
  other arithmetic  12.3 us (6%)
  local copies, waits for them, and re-layouts  7.72 us (4%)
  starting transfers between devices  4.79 us (2%)
    all_gather x1, waiting for transfers between devices, on_device(): lax.all_gather(w_out, 'seq', axis=0, tiled=True)  74.9 us
    all_to_all x1, blocking collectives, on_device(): lax.all_to_all(mixed_heads, 'head', split_axis=0, concat_axis=1, tiled=True)  29.8 us
    all_gather x1, waiting for transfers between devices, carried_in(): gathered = lax.all_gather(part, axis)  29.2 us
    another operation x1, loops' own time, window_branch(): return lax.map(one_block, starts).reshape(tok_rows, heads_here, head_width)  13 us
    dot_general x4, matrix products, one_block(): jnp.einsum('hqk,khd->qhd', weights, value_block, preferred_element_type=j...  8.59 us
    dot_general x1, matrix products, on_device(): jnp.dot(regrouped, lax.all_gather(w_out, 'seq', axis=0, tiled=True), pref...  5.45 us
    dot_general x4, matrix products, one_block(): jnp.einsum('qhd,khd->hqk', query_block, key_block, preferred_element_type...  4.85 us
    ppermute x1, starting transfers between devices, passed_along(): return lax.ppermute(shard, axis, pairs)  4.74 us
  transfers between devices with their start and end apart: 3, of which 2 were waited for; matrix products, arithmetic and copies ran while one was open for 19% of the time, Pallas kernels for 0%

commit v1 on v0

v1 whole, which is shorter than its diff:
```python
import functools
import math

import jax
import jax.numpy as jnp
from jax import lax
from jax.experimental import pallas as pl
from jax.experimental.pallas import tpu as pltpu
from jax.sharding import Mesh
from jax.sharding import PartitionSpec as P

HD = 128
W = 1024
BLOCK = 256
NY, NX, NZ, NC = 8, 4, 8, 2
AXES = ("y", "x", "z", "c")

norm_eps = 1e-06
log2e_scale = math.log2(math.e) / math.sqrt(HD)
far_below = -1e30

f32, bf16 = jnp.float32, jnp.bfloat16


def dot(a, b):
    return lax.dot_general(a, b, (((1,), (0,)), ((), ())), preferred_element_type=f32)


def dot_nt(a, b):
    return lax.dot_general(a, b, (((1,), (1,)), ((), ())), preferred_element_type=f32)


def dot_tn(a, b):
    return lax.dot_general(a, b, (((0,), (0,)), ((), ())), preferred_element_type=f32)


def normalize(branch):
    return branch * lax.rsqrt(jnp.mean(branch * branch, axis=-1, keepdims=True) + norm_eps)


def split_pair(values):
    upper = values.astype(bf16)
    return upper, (values - upper.astype(f32)).astype(bf16)


VMEM = pl.BlockSpec(memory_space=pltpu.VMEM)
SMEM = pl.BlockSpec(memory_space=pltpu.SMEM)


def call(kernel, name, outs, in_specs, flops, trans=0, nbytes=1 << 20, scratch=()):
    return pl.pallas_call(
        kernel,
        name=name,
        out_shape=outs,
        in_specs=in_specs,
        out_specs=jax.tree.map(lambda _: VMEM, outs),
        scratch_shapes=scratch,
        cost_estimate=pl.CostEstimate(flops=flops, transcendentals=trans, bytes_accessed=nbytes),
    )


def state_kernel(k_ref, v_ref, out_ref):
    total = dot_tn(k_ref[...], v_ref[...])
    for i in range(NX):
        out_ref[i] = total


def row_kernel(place_ref, states_ref, before_ref, total_ref):
    x = place_ref[1]
    before = jnp.zeros((HD, HD), f32)
    total = jnp.zeros((HD, HD), f32)
    for i in range(NX):
        state = states_ref[i]
        total = total + state
        before = before + jnp.where(i < x, state, 0.0)
    before_ref[...] = before
    sent = total.astype(bf16)
    for i in range(NY):
        total_ref[i] = sent


def window_rows(q, keys, values, bias, upper):
    key_blocks = [dot_nt(q, key) for key in keys]
    if bias is not None:
        key_blocks = [s + b if b is not None else s for s, b in zip(key_blocks, bias)]
    ends = jnp.where(upper, key_blocks[0], key_blocks[-1])
    scores = [ends] + key_blocks[1:-1]
    top = scores[0]
    for s in scores[1:]:
        top = jnp.maximum(top, s)
    top = jnp.max(top, axis=-1, keepdims=True)
    weights = [jnp.exp2((s - top) * log2e_scale) for s in scores]
    ends = weights[0]
    parts = [jnp.where(upper, ends, 0.0)] + weights[1:] + [jnp.where(upper, 0.0, ends)]
    soft = None
    for part, value in zip(parts, values):
        term = dot(part.astype(bf16), value)
        soft = term if soft is None else soft + term
    return normalize(soft) * 0.5


def upper_mask():
    rows = lax.broadcasted_iota(jnp.int32, (BLOCK, BLOCK), 0)
    cols = lax.broadcasted_iota(jnp.int32, (BLOCK, BLOCK), 1)
    return cols > rows


def rows_of(ref, index):
    return ref[index * BLOCK : (index + 1) * BLOCK, :]


def inner_kernel(q_ref, k_ref, v_ref, out_ref):
    upper = upper_mask()
    near = W // BLOCK
    for b in range(near):
        keys = [rows_of(k_ref, b + j) for j in range(near + 1)]
        values = [rows_of(v_ref, b + j) for j in range(near + 1)]
        out_ref[b * BLOCK : (b + 1) * BLOCK, :] = window_rows(
            rows_of(q_ref, near + b), keys, values, None, upper
        )


def outer_kernel(place_ref, q_ref, k_ref, v_ref, rim_ref, out_ref):
    upper = upper_mask()
    near = W // BLOCK
    first = jnp.logical_and(place_ref[0] == 0, place_ref[1] == 0)
    hidden = jnp.where(first, far_below, 0.0).astype(f32)
    for b in range(near):
        keys, values, bias = [], [], []
        for j in range(near + 1):
            at = b + j
            if at < near:
                keys.append(rim_ref[0, at * BLOCK : (at + 1) * BLOCK, :])
                values.append(rim_ref[1, at * BLOCK : (at + 1) * BLOCK, :])
                bias.append(hidden)
            else:
                keys.append(rows_of(k_ref, at - near))
                values.append(rows_of(v_ref, at - near))
                bias.append(None)
        out_ref[b * BLOCK : (b + 1) * BLOCK, :] = window_rows(
            rows_of(q_ref, b), keys, values, bias, upper
        )


def local_kernel(q_ref, k_ref, v_ref, out_ref):
    causal = jnp.logical_not(upper_mask())
    state = None
    for b in range(q_ref.shape[0] // BLOCK):
        q, k, v = rows_of(q_ref, b), rows_of(k_ref, b), rows_of(v_ref, b)
        upper, lower = split_pair(jnp.where(causal, dot_nt(q, k), 0.0))
        linear = dot(upper, v) + dot(lower, v)
        if state is not None:
            upper, lower = split_pair(state)
            both = dot(q, jnp.concatenate([upper, lower], axis=1))
            linear = linear + (both[:, :HD] + both[:, HD:])
        out_ref[b * BLOCK : (b + 1) * BLOCK, :] = linear
        own = dot_tn(k, v)
        state = own if state is None else state + own


def mix_kernel(place_ref, q_ref, linear_ref, outer_ref, inner_ref, before_ref, totals_ref, out_ref):
    y = place_ref[0]
    state = before_ref[...]
    for i in range(NY):
        state = state + jnp.where(i < y, totals_ref[i].astype(f32), 0.0)
    upper, lower = split_pair(state)
    state = jnp.concatenate([upper, lower], axis=1)
    half = W // BLOCK
    for b in range(q_ref.shape[0] // BLOCK):
        both = dot(rows_of(q_ref, b), state)
        linear = rows_of(linear_ref, b) + (both[:, :HD] + both[:, HD:])
        soft = rows_of(outer_ref, b) if b < half else rows_of(inner_ref, b - half)
        out_ref[b] = (soft + normalize(linear) * 0.5).astype(bf16)


def project_kernel(take_ref, mixed_ref, *refs):
    units, out_ref = refs[:-1], refs[-1]
    start = pl.multiple_of(take_ref[0] * HD, HD)
    parts = [mixed_ref[take_ref[1 + i], pl.ds(start, HD), :] for i in range(NY)]
    width = 512
    for n in range(out_ref.shape[1] // width):
        cols = slice(n * width, (n + 1) * width)
        total = None
        for i in range(0, NY, 2):
            pair = jnp.concatenate([parts[i], parts[i + 1]], axis=1)
            rows = jnp.concatenate([units[i][:, cols], units[i + 1][:, cols]], axis=0)
            term = dot(pair, rows)
            total = term if total is None else total + term
        out_ref[:, cols] = total.astype(out_ref.dtype)


def linear_index(y, x, z, c):
    return ((y % NY * NX + x % NX) * NZ + z % NZ) * NC + c


def moved(shard, source):
    pairs = []
    for y in range(NY):
        for x in range(NX):
            for z in range(NZ):
                for c in range(NC):
                    at = source(y, x, z, c)
                    if at is not None:
                        pairs.append((linear_index(*at), linear_index(y, x, z, c)))
    return lax.ppermute(shard, AXES, pairs)


def first_chunk(y, x, z, c):
    if x // 2 == c:
        return (y, x ^ 1, z, 1 - c)
    return (y, 3 - x, z, c)


def second_chunk(y, x, z, c):
    return None if x // 2 == c else (y, x ^ 2, z, c)


def way(z, c):
    return 1 - 2 * ((z + c) % 2)


def along(y, x, z, c):
    return (y + way(z, c), x, z, c)


def across(y, x, z, c):
    return (y, x, (z ^ 1) if c == 0 else ((z + 1) ^ 1) - 1, c)


def on_device(queries, key_vectors, value_vectors, w_out):
    y, x, z, c = (lax.axis_index(a) for a in AXES)
    place = jnp.stack([y, x, z, c]).astype(jnp.int32)
    rows = queries.shape[0]
    wide = w_out.shape[1]

    chunk_a = moved(w_out, first_chunk)
    chunk_b = moved(w_out, second_chunk)

    states = call(
        state_kernel, "state", jax.ShapeDtypeStruct((NX, HD, HD), f32), [VMEM, VMEM],
        2 * rows * HD * HD,
    )(key_vectors, value_vectors)
    row_states = lax.all_to_all(states, "x", 0, 0, tiled=True)

    rim = jnp.stack([key_vectors[rows - W :], value_vectors[rows - W :]])
    rim = lax.ppermute(rim, ("y", "x"), [(i, i + 1) for i in range(NY * NX - 1)])

    own = jnp.where(x // 2 == c, w_out, chunk_b)
    even = x % 2 == 0
    unit = jnp.concatenate([jnp.where(even, own, chunk_a), jnp.where(even, chunk_a, own)], axis=0)
    y1 = moved(unit, along)
    z1 = moved(y1, across)
    y2 = moved(y1, along)
    z2 = moved(y2, across)
    y3 = moved(y2, along)
    z3 = moved(y3, across)
    y4 = moved(y3, along)

    before, totals = call(
        row_kernel, "row",
        (jax.ShapeDtypeStruct((HD, HD), f32), jax.ShapeDtypeStruct((NY, HD, HD), bf16)),
        [SMEM, VMEM], 8 * HD * HD,
    )(place, row_states)
    totals = lax.all_to_all(totals, "y", 0, 0, tiled=True)

    half = jax.ShapeDtypeStruct((W, HD), f32)
    work = 2 * W * (W + BLOCK) * HD * 2
    inner = call(inner_kernel, "inner", half, [VMEM] * 3, work, W * W)(
        queries, key_vectors, value_vectors
    )
    linear = call(
        local_kernel, "local", jax.ShapeDtypeStruct((rows, HD), f32), [VMEM] * 3,
        2 * rows * BLOCK * HD * 4,
    )(queries, key_vectors, value_vectors)
    outer = call(outer_kernel, "outer", half, [SMEM] + [VMEM] * 4, work, W * W)(
        place, queries, key_vectors, value_vectors, rim
    )
    mixed = call(
        mix_kernel, "mix", jax.ShapeDtypeStruct((NZ, rows // NZ, HD), bf16), [SMEM] + [VMEM] * 6,
        4 * rows * HD * HD,
    )(place, queries, linear, outer, inner, before, totals)
    mixed = lax.all_to_all(mixed, "z", 0, 0, tiled=True)

    turn = way(z, c)
    units = (unit, y1, y2, y3, y4, z1, z2, z3)
    steps = (0, 1, 2, 3, 4, -1, -2, -3)
    at = [(y + turn * s) % NY for s in steps]

    def project(share, dtype):
        take = jnp.stack([share] + at).astype(jnp.int32)
        return call(
            project_kernel, "project", jax.ShapeDtypeStruct((HD, wide), dtype),
            [SMEM] + [VMEM] * (1 + NY), 2 * HD * wide * NY * HD, 0, NY * HD * wide * 2,
        )(take, mixed, *units)

    given = project(1 - c, bf16)
    taken = lax.ppermute(given, "c", [(0, 1), (1, 0)])
    kept = project(c, f32)
    return (kept + taken.astype(f32)).astype(bf16)


def solution(mesh):
    fine = Mesh(mesh.devices.reshape(NY, NX, NZ, NC), AXES)
    split = P(("y", "x"), ("z", "c"))
    return jax.shard_map(
        on_device,
        mesh=fine,
        in_specs=(split, split, split, P(("y", "x"), None)),
        out_specs=P(AXES, None),
        check_vma=False,
    )
```

time: 217 us -> 118 us (0.54)
  waiting for transfers between devices: 105 us -> 25.6 us
  starting transfers between devices: 4.79 us -> 55.3 us
  blocking collectives: 29.8 us -> 0 us
  Pallas kernels: 0 us -> 29 us
  matrix products: 28.6 us -> 0 us
  between operations: 13.5 us -> 0.36 us
  loops' own time: 13 us -> 0 us
  other arithmetic: 12.3 us -> 3.68 us
  local copies, waits for them, and re-layouts: 7.72 us -> 3.55 us
    all_gather x2 -> x0, waiting for transfers between devices: 104 us -> none  [the longest x1 74.9 us: on_device(): lax.all_gather(w_out, 'seq', axis=0, tiled=True)]
    ppermute x1 -> x11, starting transfers between devices: 4.74 us -> 36.9 us  [the longest x9 28.4 us: moved(): return lax.ppermute(shard, AXES, pairs)]
    all_to_all x1 -> x0, blocking collectives: 29.8 us -> none  [on_device(): lax.all_to_all(mixed_heads, 'head', split_axis=0, concat_axis=1, tiled=True)]
    pallas_call x0 -> x8, Pallas kernels: none -> 29 us  [the longest x2 7.88 us: project(): call(project_kernel, 'project', jax.ShapeDtypeStruct((HD, wide), dtype),...]
    dot_general x15 -> x0, matrix products: 28.6 us -> none  [the longest x4 8.59 us: one_block(): jnp.einsum('hqk,khd->qhd', weights, value_block, preferred_element_type=j...]
    ppermute x1 -> x11, waiting for transfers between devices: 0.01 us -> 25.6 us  [the longest x9 25.6 us: moved(): return lax.ppermute(shard, AXES, pairs)]
    all_to_all x0 -> x3, starting transfers between devices: none -> 18.4 us  [the longest x1 9.08 us: on_device(): mixed = lax.all_to_all(mixed, 'z', 0, 0, tiled=True)]
    another operation x2 -> x0, loops' own time: 13 us -> none  [the longest x1 13 us: window_branch(): return lax.map(one_block, starts).reshape(tok_rows, heads_here, head_width)]
  transfers between devices with their start and end apart: 3 -> 14, of which waited for: 2 -> 6; matrix products, arithmetic and copies ran while one was open for 19% -> 2% of each run, Pallas kernels for 0% -> 21%
where the time goes in v1:
time: 118 us
  starting transfers between devices  55.3 us (47%)
  Pallas kernels  29 us (25%)
  waiting for transfers between devices  25.6 us (22%)
  other arithmetic  3.68 us (3%)
  local copies, waits for them, and re-layouts  3.55 us (3%)
    ppermute x9, starting transfers between devices, moved(): return lax.ppermute(shard, AXES, pairs)  28.4 us
    ppermute x9, waiting for transfers between devices, moved(): return lax.ppermute(shard, AXES, pairs)  25.6 us
    all_to_all x1, starting transfers between devices, on_device(): mixed = lax.all_to_all(mixed, 'z', 0, 0, tiled=True)  9.08 us
    pallas_call x2, Pallas kernels, project(): call(project_kernel, 'project', jax.ShapeDtypeStruct((HD, wide), dtype),...  7.88 us
    ppermute x1, starting transfers between devices, on_device(): lax.ppermute(rim, ('y', 'x'), [(i, i + 1) for i in range(NY * NX - 1)])  6.61 us
    all_to_all x1, starting transfers between devices, on_device(): row_states = lax.all_to_all(states, 'x', 0, 0, tiled=True)  5.37 us
    pallas_call x1, Pallas kernels, on_device(): call(outer_kernel, 'outer', half, [SMEM] + [VMEM] * 4, work, W * W)  4.76 us
    pallas_call x1, Pallas kernels, on_device(): call(inner_kernel, 'inner', half, [VMEM] * 3, work, W * W)  4.63 us
  transfers between devices with their start and end apart: 14, of which 6 were waited for; matrix products, arithmetic and copies ran while one was open for 2% of the time, Pallas kernels for 21%

profile of v1, /device:TPU:1, one launch (start us, length us, event | category | flops | bytes accessed | tf_op | source)
XLA Modules:
  0.0 117.5 jit_solution(16369778307307576061)
XLA Ops:
  0.0 4.5 %collective-permute-start.2 = (bf16[64,2048]{1,0:T(8,128)(2,1)}, bf16[64,2048]{1,0:T(8,128)(2,1)S(1)}, u32[]{:S(2)}, u32[]{:S(2)}) collective-permute-start(bf16[64,2048]{1,0:T(8,128)(2,1)} %param.7), channel_id=1, source_target_pairs={{17,0},{49,1},{19,2},{51,3},{21,4},{53,5},{23,6},{55,7},{25,8},{57... | collective-permute-start | bytes 786440 | tf_op jit(solution)/shard_map/ppermute | solution.py:205
  4.5 1.3 %collective-permute-start.1 = (bf16[64,2048]{1,0:T(8,128)(2,1)}, bf16[64,2048]{1,0:T(8,128)(2,1)S(1)}, u32[]{:S(2)}, u32[]{:S(2)}) collective-permute-start(bf16[64,2048]{1,0:T(8,128)(2,1)} %param.7), channel_id=1, source_target_pairs={{33,1},{35,3},{37,5},{39,7},{41,9},{43,11},{45,13},{47,15},{49,17}... | collective-permute-start | bytes 786440 | tf_op jit(solution)/shard_map/ppermute | solution.py:205
  5.8 3.3 %collective-permute-done.2 = bf16[64,2048]{1,0:T(8,128)(2,1)S(1)} collective-permute-done((bf16[64,2048]{1,0:T(8,128)(2,1)}, bf16[64,2048]{1,0:T(8,128)(2,1)S(1)}, u32[]{:S(2)}, u32[]{:S(2)}) %collective-permute-start.2) | collective-permute-done | bytes 262176 | tf_op jit(solution)/shard_map/ppermute | solution.py:205
  9.2 4.6 %collective-permute-done.1 = bf16[64,2048]{1,0:T(8,128)(2,1)S(1)} collective-permute-done((bf16[64,2048]{1,0:T(8,128)(2,1)}, bf16[64,2048]{1,0:T(8,128)(2,1)S(1)}, u32[]{:S(2)}, u32[]{:S(2)}) %collective-permute-start.1) | collective-permute-done | bytes 262176 | tf_op jit(solution)/shard_map/ppermute | solution.py:205
  13.7 0.1 broadcast_select_fusion.2
  13.8 3.2 %collective-permute-start.3 = (bf16[128,2048]{1,0:T(8,128)(2,1)S(1)}, bf16[128,2048]{1,0:T(8,128)(2,1)S(1)}, u32[]{:S(2)}, u32[]{:S(2)}) collective-permute-start(bf16[128,2048]{1,0:T(8,128)(2,1)S(1)} %pad_maximum_fusion.1.refs_0_), channel_id=1, source_target_pairs={{64,0},{449,1},{450,2},{67,3},{68,4},{453,5},{454,6},{71,7},{72,8}... | collective-permute-start | bytes 1572872 | tf_op jit(solution)/shard_map/ppermute | solution.py:205
  17.0 0.0 copy-start.1
  17.1 2.3 %state.1 = f32[4,128,128]{2,1,0:T(8,128)} custom-call(bf16[2048,128]{1,0:T(8,128)(2,1)} %k_ref.7, bf16[2048,128]{1,0:T(8,128)(2,1)} %v_ref.7), custom_call_target="tpu_custom_call" | custom-call | flops 67108864 | bytes 1048576 | tf_op jit(solution)/shard_map/state/pallas_call | solution.py:239
  19.4 5.4 %all-to-all-start = ((f32[4,128,128]{2,1,0:T(8,128)}), f32[4,128,128]{2,1,0:T(8,128)S(1)}, u32[]{:S(2)}, u32[]{:S(2)}) async-start(f32[4,128,128]{2,1,0:T(8,128)} %state.1), calls=%async_computation | async-start | bytes 524288 | tf_op jit(solution)/shard_map/all_to_all | solution.py:243
  24.7 0.0 copy-done
  24.8 0.7 collective-permute-done.3.refs_1_
  25.5 1.9 %collective-permute-start.4 = (bf16[128,2048]{1,0:T(8,128)(2,1)S(1)}, bf16[128,2048]{1,0:T(8,128)(2,1)S(1)}, u32[]{:S(2)}, u32[]{:S(2)}) collective-permute-start(bf16[128,2048]{1,0:T(8,128)(2,1)S(1)} %collective-permute-done.3.refs_1_), channel_id=1, source_target_pairs={{64,0},{449,1},{450,2},{67,3},{68,4},{453,5},{454,6},{71,7},{72,8}... | collective-permute-start | bytes 1572872 | tf_op jit(solution)/shard_map/ppermute | solution.py:205
  27.4 0.8 pad_maximum_fusion
  28.2 6.6 %collective-permute-start = (bf16[2,1024,128]{2,1,0:T(8,128)(2,1)}, bf16[2,1024,128]{2,1,0:T(8,128)(2,1)S(1)}, u32[]{:S(2)}, u32[]{:S(2)}) collective-permute-start(bf16[2,1024,128]{2,1,0:T(8,128)(2,1)} %pad_maximum_fusion), channel_id=1, source_target_pairs={{0,16},{16,32},{32,48},{48,64},{64,80},{80,96},{96,112},{112,128},... | collective-permute-start | bytes 1572872 | tf_op jit(solution)/shard_map/ppermute | solution.py:246
  34.9 0.6 pad_add_fusion.place_ref
  35.5 0.0 all-to-all-done.states_ref
  35.5 0.7 copy-done.10
  36.2 1.7 %row.1 = (f32[128,128]{1,0:T(8,128)}, bf16[8,128,128]{2,1,0:T(8,128)(2,1)}) custom-call(s32[4]{0:T(128)} %pad_add_fusion.place_ref, f32[4,128,128]{2,1,0:T(8,128)} %copy-done.10), custom_call_target="tpu_custom_call" | custom-call | flops 131072 | bytes 1048576 | tf_op jit(solution)/shard_map/row/pallas_call | solution.py:259
  37.9 3.9 %all-to-all-start.1 = ((bf16[8,128,128]{2,1,0:T(8,128)(2,1)}), bf16[8,128,128]{2,1,0:T(8,128)(2,1)S(1)}, u32[]{:S(2)}, u32[]{:S(2)}) async-start(bf16[8,128,128]{2,1,0:T(8,128)(2,1)} %get-tuple-element.8), calls=%async_computation.1 | async-start | bytes 524288 | tf_op jit(solution)/shard_map/all_to_all | solution.py:264
  41.8 0.0 collective-permute-done.4.refs_2_
  41.8 3.4 %collective-permute-start.5 = (bf16[128,2048]{1,0:T(8,128)(2,1)S(1)}, bf16[128,2048]{1,0:T(8,128)(2,1)S(1)}, u32[]{:S(2)}, u32[]{:S(2)}) collective-permute-start(bf16[128,2048]{1,0:T(8,128)(2,1)S(1)} %collective-permute-done.4.refs_2_), channel_id=1, source_target_pairs={{64,0},{449,1},{450,2},{67,3},{68,4},{453,5},{454,6},{71,7},{72,8}... | collective-permute-start | bytes 1572872 | tf_op jit(solution)/shard_map/ppermute | solution.py:205
  45.2 4.6 %inner.1.inner_ref = f32[1024,128]{1,0:T(8,128)} custom-call(bf16[2048,128]{1,0:T(8,128)(2,1)} %q_ref.7, bf16[2048,128]{1,0:T(8,128)(2,1)} %k_ref.7, bf16[2048,128]{1,0:T(8,128)(2,1)} %v_ref.7), custom_call_target="tpu_custom_call" | custom-call | flops 671088640 | bytes 1048576 | tf_op jit(solution)/shard_map/inner/pallas_call | solution.py:268
  49.8 4.6 %local.1.linear_ref = f32[2048,128]{1,0:T(8,128)} custom-call(bf16[2048,128]{1,0:T(8,128)(2,1)} %q_ref.7, bf16[2048,128]{1,0:T(8,128)(2,1)} %k_ref.7, bf16[2048,128]{1,0:T(8,128)(2,1)} %v_ref.7), custom_call_target="tpu_custom_call" | custom-call | flops 536870912 | bytes 1048576 | tf_op jit(solution)/shard_map/local/pallas_call | solution.py:271
  54.4 0.0 collective-permute-done.rim_ref
  54.4 0.8 copy-done.11
  55.2 4.8 %outer.1.outer_ref = f32[1024,128]{1,0:T(8,128)} custom-call(s32[4]{0:T(128)} %pad_add_fusion.place_ref, bf16[2048,128]{1,0:T(8,128)(2,1)} %q_ref.7, bf16[2048,128]{1,0:T(8,128)(2,1)} %k_ref.7, bf16[2048,128]{1,0:T(8,128)(2,1)} %v_ref.7, bf16[2,1024,128]{2,1,0:T(8,128)(2,1)} %copy-done.11), custom_call_target="tpu_custom_call" | custom-call | flops 671088640 | bytes 1048576 | tf_op jit(solution)/shard_map/outer/pallas_call | solution.py:275
  60.0 0.0 all-to-all-done.1.totals_ref
  60.0 0.7 copy-done.9
  60.7 3.2 %mix.1 = bf16[8,256,128]{2,1,0:T(8,128)(2,1)} custom-call(s32[4]{0:T(128)} %pad_add_fusion.place_ref, bf16[2048,128]{1,0:T(8,128)(2,1)} %q_ref.7, f32[2048,128]{1,0:T(8,128)} %local.1.linear_ref, f32[1024,128]{1,0:T(8,128)} %outer.1.outer_ref, f32[1024,128]{1,0:T(8,128)} %inner.1.inner_ref, f32[128,128]{1,0:T(8,128)} %get-tuple-element.7.before_ref, ...), custom_call_target="tpu_custom_call" | custom-call | flops 134217728 | bytes 1048576 | tf_op jit(solution)/shard_map/mix/pallas_call | solution.py:278
  63.8 9.1 %all-to-all-start.2 = ((bf16[8,256,128]{2,1,0:T(8,128)(2,1)}), bf16[8,256,128]{2,1,0:T(8,128)(2,1)S(1)}, u32[]{:S(2)}, u32[]{:S(2)}) async-start(bf16[8,256,128]{2,1,0:T(8,128)(2,1)} %mix.1), calls=%async_computation.2 | async-start | bytes 1048576 | tf_op jit(solution)/shard_map/all_to_all | solution.py:282
  72.9 4.6 %collective-permute-start.7 = (bf16[128,2048]{1,0:T(8,128)(2,1)S(1)}, bf16[128,2048]{1,0:T(8,128)(2,1)S(1)}, u32[]{:S(2)}, u32[]{:S(2)}) collective-permute-start(bf16[128,2048]{1,0:T(8,128)(2,1)S(1)} %collective-permute-done.3.refs_1_), channel_id=1, source_target_pairs={{2,0},{15,1},{0,2},{5,3},{6,4},{3,5},{4,6},{9,7},{10,8},{7,9},{8,1... | collective-permute-start | bytes 1572872 | tf_op jit(solution)/shard_map/ppermute | solution.py:205
  77.5 0.0 copy-done.5
  77.5 1.9 %collective-permute-start.8 = (bf16[128,2048]{1,0:T(8,128)(2,1)S(1)}, bf16[128,2048]{1,0:T(8,128)(2,1)S(1)}, u32[]{:S(2)}, u32[]{:S(2)}) collective-permute-start(bf16[128,2048]{1,0:T(8,128)(2,1)S(1)} %collective-permute-done.4.refs_2_), channel_id=1, source_target_pairs={{2,0},{15,1},{0,2},{5,3},{6,4},{3,5},{4,6},{9,7},{10,8},{7,9},{8,1... | collective-permute-start | bytes 1572872 | tf_op jit(solution)/shard_map/ppermute | solution.py:205
  79.4 0.0 collective-permute-done.5.refs_3_
  79.5 2.0 %collective-permute-start.6 = (bf16[128,2048]{1,0:T(8,128)(2,1)S(1)}, bf16[128,2048]{1,0:T(8,128)(2,1)}, u32[]{:S(2)}, u32[]{:S(2)}) collective-permute-start(bf16[128,2048]{1,0:T(8,128)(2,1)S(1)} %collective-permute-done.5.refs_3_), channel_id=1, source_target_pairs={{64,0},{449,1},{450,2},{67,3},{68,4},{453,5},{454,6},{71,7},{72,8}... | collective-permute-start | bytes 1572872 | tf_op jit(solution)/shard_map/ppermute | solution.py:205
  81.5 5.7 %collective-permute-start.9 = (bf16[128,2048]{1,0:T(8,128)(2,1)S(1)}, bf16[128,2048]{1,0:T(8,128)(2,1)}, u32[]{:S(2)}, u32[]{:S(2)}) collective-permute-start(bf16[128,2048]{1,0:T(8,128)(2,1)S(1)} %collective-permute-done.5.refs_3_), channel_id=1, source_target_pairs={{2,0},{15,1},{0,2},{5,3},{6,4},{3,5},{4,6},{9,7},{10,8},{7,9},{8,1... | collective-permute-start | bytes 1572872 | tf_op jit(solution)/shard_map/ppermute | solution.py:205
  87.3 0.7 stack.84.take_ref
  88.0 5.6 %collective-permute-done.7.refs_5_ = bf16[128,2048]{1,0:T(8,128)(2,1)S(1)} collective-permute-done((bf16[128,2048]{1,0:T(8,128)(2,1)S(1)}, bf16[128,2048]{1,0:T(8,128)(2,1)S(1)}, u32[]{:S(2)}, u32[]{:S(2)}) %collective-permute-start.7) | collective-permute-done | bytes 524320 | tf_op jit(solution)/shard_map/ppermute | solution.py:205
  93.6 0.0 all-to-all-done.2.mixed_ref
  93.6 5.6 %collective-permute-done.8.refs_6_ = bf16[128,2048]{1,0:T(8,128)(2,1)S(1)} collective-permute-done((bf16[128,2048]{1,0:T(8,128)(2,1)S(1)}, bf16[128,2048]{1,0:T(8,128)(2,1)S(1)}, u32[]{:S(2)}, u32[]{:S(2)}) %collective-permute-start.8) | collective-permute-done | bytes 524320 | tf_op jit(solution)/shard_map/ppermute | solution.py:205
  99.2 0.0 collective-permute-done.6.refs_4_
  99.2 5.7 %collective-permute-done.9.refs_7_ = bf16[128,2048]{1,0:T(8,128)(2,1)} collective-permute-done((bf16[128,2048]{1,0:T(8,128)(2,1)S(1)}, bf16[128,2048]{1,0:T(8,128)(2,1)}, u32[]{:S(2)}, u32[]{:S(2)}) %collective-permute-start.9) | collective-permute-done | bytes 524320 | tf_op jit(solution)/shard_map/ppermute | solution.py:205
  105.0 3.9 %project.3 = bf16[128,2048]{1,0:T(8,128)(2,1)} custom-call(s32[9]{0:T(128)} %stack.84.take_ref, bf16[8,256,128]{2,1,0:T(8,128)(2,1)} %copy-done.3, bf16[128,2048]{1,0:T(8,128)(2,1)} %copy-done.2, bf16[128,2048]{1,0:T(8,128)(2,1)} %copy-done.4, bf16[128,2048]{1,0:T(8,128)(2,1)} %copy-done.5, bf16[128,2048]{1,0:T(8,128)(2,1)} %copy-done.6, ...), custom_call_target="tpu_custom_call" | custom-call | flops 536870912 | bytes 4194304 | tf_op jit(solution)/shard_map/project/pallas_call | solution.py:291
  108.8 1.9 %collective-permute-start.10 = (bf16[128,2048]{1,0:T(8,128)(2,1)}, bf16[128,2048]{1,0:T(8,128)(2,1)S(1)}, u32[]{:S(2)}, u32[]{:S(2)}) collective-permute-start(bf16[128,2048]{1,0:T(8,128)(2,1)} %project.3), channel_id=1, source_target_pairs={{0,1},{1,0},{2,3},{3,2},{4,5},{5,4},{6,7},{7,6},{8,9},{9,8},{10,11... | collective-permute-start | bytes 1572872 | tf_op jit(solution)/shard_map/ppermute | solution.py:297
  110.7 0.6 stack.75.take_ref
  111.4 4.0 %project.2 = f32[128,2048]{1,0:T(8,128)} custom-call(s32[9]{0:T(128)} %stack.75.take_ref, bf16[8,256,128]{2,1,0:T(8,128)(2,1)} %copy-done.3, bf16[128,2048]{1,0:T(8,128)(2,1)} %copy-done.2, bf16[128,2048]{1,0:T(8,128)(2,1)} %copy-done.4, bf16[128,2048]{1,0:T(8,128)(2,1)} %copy-done.5, bf16[128,2048]{1,0:T(8,128)(2,1)} %copy-done.6, ...), custom_call_target="tpu_custom_call" | custom-call | flops 536870912 | bytes 4194304 | tf_op jit(solution)/shard_map/project/pallas_call | solution.py:291
  115.4 0.0 collective-permute-done.10
  115.4 2.1 %add_convert_fusion = bf16[128,2048]{1,0:T(8,128)(2,1)} fusion(f32[128,2048]{1,0:T(8,128)} %project.2, bf16[128,2048]{1,0:T(8,128)(2,1)S(1)} %collective-permute-done.10), kind=kLoop, calls=%fused_computation | loop fusion | flops 786432 | bytes 2097152 | tf_op jit(solution)/shard_map/convert_element_type | solution.py:299
  (20 shorter events, 0.1 us)
Async XLA Ops:
  0.0 9.2 %collective-permute-start.2 = (bf16[64,2048]{1,0:T(8,128)(2,1)}, bf16[64,2048]{1,0:T(8,128)(2,1)S(1)}, u32[]{:S(2)}, u32[]{:S(2)}) collective-permute-start(bf16[64,2048]{1,0:T(8,128)(2,1)} %param.7), channel_id=1, source_target_pairs={{17,0},{49,1},{19,2},{51,3},{21,4},{53,5},{23,6},{55,7},{25,8},{57... | collective-permute-start | bytes 786440 | tf_op jit(solution)/shard_map/ppermute | solution.py:205
  4.5 9.2 %collective-permute-start.1 = (bf16[64,2048]{1,0:T(8,128)(2,1)}, bf16[64,2048]{1,0:T(8,128)(2,1)S(1)}, u32[]{:S(2)}, u32[]{:S(2)}) collective-permute-start(bf16[64,2048]{1,0:T(8,128)(2,1)} %param.7), channel_id=1, source_target_pairs={{33,1},{35,3},{37,5},{39,7},{41,9},{43,11},{45,13},{47,15},{49,17}... | collective-permute-start | bytes 786440 | tf_op jit(solution)/shard_map/ppermute | solution.py:205
  13.8 5.5 %copy-start.2 = (bf16[128,2048]{1,0:T(8,128)(2,1)}, bf16[128,2048]{1,0:T(8,128)(2,1)S(1)}, u32[]{:S(2)}) copy-start(bf16[128,2048]{1,0:T(8,128)(2,1)S(1)} %pad_maximum_fusion.1.refs_0_) | copy-start | bytes 1572868
  13.8 11.7 %collective-permute-start.3 = (bf16[128,2048]{1,0:T(8,128)(2,1)S(1)}, bf16[128,2048]{1,0:T(8,128)(2,1)S(1)}, u32[]{:S(2)}, u32[]{:S(2)}) collective-permute-start(bf16[128,2048]{1,0:T(8,128)(2,1)S(1)} %pad_maximum_fusion.1.refs_0_), channel_id=1, source_target_pairs={{64,0},{449,1},{450,2},{67,3},{68,4},{453,5},{454,6},{71,7},{72,8}... | collective-permute-start | bytes 1572872 | tf_op jit(solution)/shard_map/ppermute | solution.py:205
  17.0 7.7 %copy-start.1 = (bf16[2048,128]{1,0:T(8,128)(2,1)S(1)}, bf16[2048,128]{1,0:T(8,128)(2,1)}, u32[]{:S(2)}) copy-start(bf16[2048,128]{1,0:T(8,128)(2,1)} %v_ref.7) | copy-start | bytes 1572868
  19.4 5.4 %copy-start = (bf16[2048,128]{1,0:T(8,128)(2,1)S(1)}, bf16[2048,128]{1,0:T(8,128)(2,1)}, u32[]{:S(2)}) copy-start(bf16[2048,128]{1,0:T(8,128)(2,1)} %k_ref.7) | copy-start | bytes 1572868
  19.4 16.1 %all-to-all-start = ((f32[4,128,128]{2,1,0:T(8,128)}), f32[4,128,128]{2,1,0:T(8,128)S(1)}, u32[]{:S(2)}, u32[]{:S(2)}) async-start(f32[4,128,128]{2,1,0:T(8,128)} %state.1), calls=%async_computation | async-start | bytes 524288 | tf_op jit(solution)/shard_map/all_to_all | solution.py:243
  25.5 47.4 %copy-start.4 = (bf16[128,2048]{1,0:T(8,128)(2,1)}, bf16[128,2048]{1,0:T(8,128)(2,1)S(1)}, u32[]{:S(2)}) copy-start(bf16[128,2048]{1,0:T(8,128)(2,1)S(1)} %collective-permute-done.3.refs_1_) | copy-start | bytes 1572868
  25.5 16.3 %collective-permute-start.4 = (bf16[128,2048]{1,0:T(8,128)(2,1)S(1)}, bf16[128,2048]{1,0:T(8,128)(2,1)S(1)}, u32[]{:S(2)}, u32[]{:S(2)}) collective-permute-start(bf16[128,2048]{1,0:T(8,128)(2,1)S(1)} %collective-permute-done.3.refs_1_), channel_id=1, source_target_pairs={{64,0},{449,1},{450,2},{67,3},{68,4},{453,5},{454,6},{71,7},{72,8}... | collective-permute-start | bytes 1572872 | tf_op jit(solution)/shard_map/ppermute | solution.py:205
  28.2 26.2 %collective-permute-start = (bf16[2,1024,128]{2,1,0:T(8,128)(2,1)}, bf16[2,1024,128]{2,1,0:T(8,128)(2,1)S(1)}, u32[]{:S(2)}, u32[]{:S(2)}) collective-permute-start(bf16[2,1024,128]{2,1,0:T(8,128)(2,1)} %pad_maximum_fusion), channel_id=1, source_target_pairs={{0,16},{16,32},{32,48},{48,64},{64,80},{80,96},{96,112},{112,128},... | collective-permute-start | bytes 1572872 | tf_op jit(solution)/shard_map/ppermute | solution.py:246
  35.5 0.7 copy-start.10
  37.9 22.1 %all-to-all-start.1 = ((bf16[8,128,128]{2,1,0:T(8,128)(2,1)}), bf16[8,128,128]{2,1,0:T(8,128)(2,1)S(1)}, u32[]{:S(2)}, u32[]{:S(2)}) async-start(bf16[8,128,128]{2,1,0:T(8,128)(2,1)} %get-tuple-element.8), calls=%async_computation.1 | async-start | bytes 524288 | tf_op jit(solution)/shard_map/all_to_all | solution.py:264
  41.8 35.7 %copy-start.5 = (bf16[128,2048]{1,0:T(8,128)(2,1)}, bf16[128,2048]{1,0:T(8,128)(2,1)S(1)}, u32[]{:S(2)}) copy-start(bf16[128,2048]{1,0:T(8,128)(2,1)S(1)} %collective-permute-done.4.refs_2_) | copy-start | bytes 1572868
  41.8 37.6 %collective-permute-start.5 = (bf16[128,2048]{1,0:T(8,128)(2,1)S(1)}, bf16[128,2048]{1,0:T(8,128)(2,1)S(1)}, u32[]{:S(2)}, u32[]{:S(2)}) collective-permute-start(bf16[128,2048]{1,0:T(8,128)(2,1)S(1)} %collective-permute-done.4.refs_2_), channel_id=1, source_target_pairs={{64,0},{449,1},{450,2},{67,3},{68,4},{453,5},{454,6},{71,7},{72,8}... | collective-permute-start | bytes 1572872 | tf_op jit(solution)/shard_map/ppermute | solution.py:205
  54.4 0.8 copy-start.11
  60.0 0.7 copy-start.9
  63.8 29.8 %all-to-all-start.2 = ((bf16[8,256,128]{2,1,0:T(8,128)(2,1)}), bf16[8,256,128]{2,1,0:T(8,128)(2,1)S(1)}, u32[]{:S(2)}, u32[]{:S(2)}) async-start(bf16[8,256,128]{2,1,0:T(8,128)(2,1)} %mix.1), calls=%async_computation.2 | async-start | bytes 1048576 | tf_op jit(solution)/shard_map/all_to_all | solution.py:282
  72.9 20.7 %collective-permute-start.7 = (bf16[128,2048]{1,0:T(8,128)(2,1)S(1)}, bf16[128,2048]{1,0:T(8,128)(2,1)S(1)}, u32[]{:S(2)}, u32[]{:S(2)}) collective-permute-start(bf16[128,2048]{1,0:T(8,128)(2,1)S(1)} %collective-permute-done.3.refs_1_), channel_id=1, source_target_pairs={{2,0},{15,1},{0,2},{5,3},{6,4},{3,5},{4,6},{9,7},{10,8},{7,9},{8,1... | collective-permute-start | bytes 1572872 | tf_op jit(solution)/shard_map/ppermute | solution.py:205
  77.5 21.7 %collective-permute-start.8 = (bf16[128,2048]{1,0:T(8,128)(2,1)S(1)}, bf16[128,2048]{1,0:T(8,128)(2,1)S(1)}, u32[]{:S(2)}, u32[]{:S(2)}) collective-permute-start(bf16[128,2048]{1,0:T(8,128)(2,1)S(1)} %collective-permute-done.4.refs_2_), channel_id=1, source_target_pairs={{2,0},{15,1},{0,2},{5,3},{6,4},{3,5},{4,6},{9,7},{10,8},{7,9},{8,1... | collective-permute-start | bytes 1572872 | tf_op jit(solution)/shard_map/ppermute | solution.py:205
  79.5 25.5 %copy-start.6 = (bf16[128,2048]{1,0:T(8,128)(2,1)}, bf16[128,2048]{1,0:T(8,128)(2,1)S(1)}, u32[]{:S(2)}) copy-start(bf16[128,2048]{1,0:T(8,128)(2,1)S(1)} %collective-permute-done.5.refs_3_) | copy-start | bytes 1572868
  79.5 19.8 %collective-permute-start.6 = (bf16[128,2048]{1,0:T(8,128)(2,1)S(1)}, bf16[128,2048]{1,0:T(8,128)(2,1)}, u32[]{:S(2)}, u32[]{:S(2)}) collective-permute-start(bf16[128,2048]{1,0:T(8,128)(2,1)S(1)} %collective-permute-done.5.refs_3_), channel_id=1, source_target_pairs={{64,0},{449,1},{450,2},{67,3},{68,4},{453,5},{454,6},{71,7},{72,8}... | collective-permute-start | bytes 1572872 | tf_op jit(solution)/shard_map/ppermute | solution.py:205
  81.5 23.5 %collective-permute-start.9 = (bf16[128,2048]{1,0:T(8,128)(2,1)S(1)}, bf16[128,2048]{1,0:T(8,128)(2,1)}, u32[]{:S(2)}, u32[]{:S(2)}) collective-permute-start(bf16[128,2048]{1,0:T(8,128)(2,1)S(1)} %collective-permute-done.5.refs_3_), channel_id=1, source_target_pairs={{2,0},{15,1},{0,2},{5,3},{6,4},{3,5},{4,6},{9,7},{10,8},{7,9},{8,1... | collective-permute-start | bytes 1572872 | tf_op jit(solution)/shard_map/ppermute | solution.py:205
  93.6 11.3 %copy-start.7 = (bf16[128,2048]{1,0:T(8,128)(2,1)}, bf16[128,2048]{1,0:T(8,128)(2,1)S(1)}, u32[]{:S(2)}) copy-start(bf16[128,2048]{1,0:T(8,128)(2,1)S(1)} %collective-permute-done.7.refs_5_) | copy-start | bytes 1572868
  93.6 11.3 %copy-start.3 = (bf16[8,256,128]{2,1,0:T(8,128)(2,1)}, bf16[8,256,128]{2,1,0:T(8,128)(2,1)S(1)}, u32[]{:S(2)}) copy-start(bf16[8,256,128]{2,1,0:T(8,128)(2,1)S(1)} %all-to-all-done.2.mixed_ref) | copy-start | bytes 1572868
  99.2 5.7 %copy-start.8 = (bf16[128,2048]{1,0:T(8,128)(2,1)}, bf16[128,2048]{1,0:T(8,128)(2,1)S(1)}, u32[]{:S(2)}) copy-start(bf16[128,2048]{1,0:T(8,128)(2,1)S(1)} %collective-permute-done.8.refs_6_) | copy-start | bytes 1572868
  108.8 6.6 %collective-permute-start.10 = (bf16[128,2048]{1,0:T(8,128)(2,1)}, bf16[128,2048]{1,0:T(8,128)(2,1)S(1)}, u32[]{:S(2)}, u32[]{:S(2)}) collective-permute-start(bf16[128,2048]{1,0:T(8,128)(2,1)} %project.3), channel_id=1, source_target_pairs={{0,1},{1,0},{2,3},{3,2},{4,5},{5,4},{6,7},{7,6},{8,9},{9,8},{10,11... | collective-permute-start | bytes 1572872 | tf_op jit(solution)/shard_map/ppermute | solution.py:297

commit v2 on v1

v2 whole, which is shorter than its diff:
```python
import math

import jax
import jax.numpy as jnp
from jax import lax
from jax.experimental import pallas as pl
from jax.experimental.pallas import tpu as pltpu
from jax.sharding import Mesh
from jax.sharding import PartitionSpec as P

HD = 128
W = 1024
BLOCK = 256
NY, NX, NZ, NC = 8, 4, 8, 2
AXES = ("y", "x", "z", "c")

norm_eps = 1e-06
log2e_scale = math.log2(math.e) / math.sqrt(HD)
far_below = -1e30

f32, bf16 = jnp.float32, jnp.bfloat16


def dot(a, b):
    return lax.dot_general(a, b, (((1,), (0,)), ((), ())), preferred_element_type=f32)


def dot_nt(a, b):
    return lax.dot_general(a, b, (((1,), (1,)), ((), ())), preferred_element_type=f32)


def dot_tn(a, b):
    return lax.dot_general(a, b, (((0,), (0,)), ((), ())), preferred_element_type=f32)


def normalize(branch):
    return branch * lax.rsqrt(jnp.mean(branch * branch, axis=-1, keepdims=True) + norm_eps)


def split_pair(values):
    upper = values.astype(bf16)
    return upper, (values - upper.astype(f32)).astype(bf16)


VMEM = pl.BlockSpec(memory_space=pltpu.VMEM)
SMEM = pl.BlockSpec(memory_space=pltpu.SMEM)


def call(kernel, outs, in_specs, flops, trans=0, nbytes=1 << 20):
    return pl.pallas_call(
        kernel,
        out_shape=outs,
        in_specs=in_specs,
        out_specs=jax.tree.map(lambda _: VMEM, outs),
        compiler_params=pltpu.CompilerParams(vmem_limit_bytes=12 << 20),
        cost_estimate=pl.CostEstimate(flops=flops, transcendentals=trans, bytes_accessed=nbytes),
    )


def rows_of(ref, index):
    return ref[index * BLOCK : (index + 1) * BLOCK, :]


def state_kernel(k_ref, v_ref, out_ref, before_ref, rim_ref):
    count = k_ref.shape[0] // BLOCK
    total = jnp.zeros((HD, HD), f32)
    for b in range(count):
        before_ref[b] = total
        total = total + dot_tn(rows_of(k_ref, b), rows_of(v_ref, b))
    for i in range(NX):
        out_ref[i] = total
    rim_ref[0] = k_ref[k_ref.shape[0] - W :, :]
    rim_ref[1] = v_ref[v_ref.shape[0] - W :, :]


def row_kernel(states_ref, before_ref, total_ref):
    x = lax.axis_index("x")
    before = jnp.zeros((HD, HD), f32)
    total = jnp.zeros((HD, HD), f32)
    for i in range(NX):
        state = states_ref[i]
        total = total + state
        before = before + jnp.where(i < x, state, 0.0)
    before_ref[...] = before
    sent = total.astype(bf16)
    for i in range(NY):
        total_ref[i] = sent


def block_rows(q, keys, values, bias, upper):
    key_blocks = [dot_nt(q, key) for key in keys]
    near = key_blocks[-1]
    high, low = split_pair(jnp.where(upper, 0.0, near))
    linear = dot(high, values[-1]) + dot(low, values[-1])
    if bias is not None:
        key_blocks = [s if b is None else s + b for s, b in zip(key_blocks, bias)]
    scores = [jnp.where(upper, key_blocks[0], near)] + key_blocks[1:-1]
    top = scores[0]
    for s in scores[1:]:
        top = jnp.maximum(top, s)
    top = jnp.max(top, axis=-1, keepdims=True)
    weights = [jnp.exp2((s - top) * log2e_scale) for s in scores]
    ends = weights[0]
    parts = [jnp.where(upper, ends, 0.0)] + weights[1:] + [jnp.where(upper, 0.0, ends)]
    soft = None
    for part, value in zip(parts, values):
        term = dot(part.astype(bf16), value)
        soft = term if soft is None else soft + term
    return normalize(soft) * 0.5, linear


def upper_mask():
    rows = lax.broadcasted_iota(jnp.int32, (BLOCK, BLOCK), 0)
    cols = lax.broadcasted_iota(jnp.int32, (BLOCK, BLOCK), 1)
    return cols > rows


def inner_kernel(q_ref, k_ref, v_ref, soft_ref, linear_ref):
    upper = upper_mask()
    near = W // BLOCK
    for b in range(near):
        keys = [rows_of(k_ref, b + j) for j in range(near + 1)]
        values = [rows_of(v_ref, b + j) for j in range(near + 1)]
        soft, linear = block_rows(rows_of(q_ref, near + b), keys, values, None, upper)
        soft_ref[b * BLOCK : (b + 1) * BLOCK, :] = soft
        linear_ref[b * BLOCK : (b + 1) * BLOCK, :] = linear


def outer_kernel(q_ref, k_ref, v_ref, rim_ref, soft_ref, linear_ref):
    upper = upper_mask()
    near = W // BLOCK
    first = jnp.logical_and(lax.axis_index("y") == 0, lax.axis_index("x") == 0)
    hidden = jnp.where(first, far_below, 0.0).astype(f32)
    for b in range(near):
        keys, values, bias = [], [], []
        for j in range(near + 1):
            at = b + j
            if at < near:
                keys.append(rim_ref[0, at * BLOCK : (at + 1) * BLOCK, :])
                values.append(rim_ref[1, at * BLOCK : (at + 1) * BLOCK, :])
                bias.append(hidden)
            else:
                keys.append(rows_of(k_ref, at - near))
                values.append(rows_of(v_ref, at - near))
                bias.append(None)
        soft, linear = block_rows(rows_of(q_ref, b), keys, values, bias, upper)
        soft_ref[b * BLOCK : (b + 1) * BLOCK, :] = soft
        linear_ref[b * BLOCK : (b + 1) * BLOCK, :] = linear


def mix_kernel(
    q_ref, outer_ref, outer_linear_ref, inner_ref, inner_linear_ref, within_ref, before_ref, totals_ref, out_ref
):
    y = lax.axis_index("y")
    odd = lax.axis_index("x") % 2 == 1
    shift = jnp.where(odd, HD // 2, 0)
    prior = before_ref[...]
    for i in range(NY):
        prior = prior + jnp.where(i < y, totals_ref[i].astype(f32), 0.0)
    half = W // BLOCK
    for b in range(q_ref.shape[0] // BLOCK):
        upper, lower = split_pair(prior + within_ref[b])
        both = dot(rows_of(q_ref, b), jnp.concatenate([upper, lower], axis=1))
        near = rows_of(outer_linear_ref, b) if b < half else rows_of(inner_linear_ref, b - half)
        soft = rows_of(outer_ref, b) if b < half else rows_of(inner_ref, b - half)
        linear = near + (both[:, :HD] + both[:, HD:])
        mixed = soft + normalize(linear) * 0.5
        out_ref[b] = pltpu.roll(mixed, shift, 1).astype(bf16)


def project_kernel(mixed_ref, *refs):
    units, given_ref, kept_ref = refs[:-2], refs[-2], refs[-1]
    y, z, c = lax.axis_index("y"), lax.axis_index("z"), lax.axis_index("c")
    turn = way(z, c)
    given, kept = [], []
    for step in unit_steps:
        head = lax.rem(y + turn * step + NY, NY)
        given.append(mixed_ref[head, pl.ds(pl.multiple_of((1 - c) * HD, HD), HD), :])
        kept.append(mixed_ref[head, pl.ds(pl.multiple_of(c * HD, HD), HD), :])
    left = [
        jnp.concatenate(
            [jnp.concatenate(given[i : i + 2], axis=1), jnp.concatenate(kept[i : i + 2], axis=1)], axis=0
        )
        for i in range(0, NY, 2)
    ]
    width = 512
    for n in range(kept_ref.shape[1] // width):
        cols = slice(n * width, (n + 1) * width)
        total = None
        for i in range(0, NY, 2):
            rows = jnp.concatenate([units[i][:, cols], units[i + 1][:, cols]], axis=0)
            term = dot(left[i // 2], rows)
            total = term if total is None else total + term
        given_ref[:, cols] = total[:HD].astype(bf16)
        kept_ref[:, cols] = total[HD:]


def add_kernel(kept_ref, taken_ref, out_ref):
    out_ref[...] = (kept_ref[...] + taken_ref[...].astype(f32)).astype(bf16)


def linear_index(y, x, z, c):
    return ((y % NY * NX + x % NX) * NZ + z % NZ) * NC + c


def moved(shard, source):
    pairs = []
    for y in range(NY):
        for x in range(NX):
            for z in range(NZ):
                for c in range(NC):
                    at = source(y, x, z, c)
                    if at is not None:
                        pairs.append((linear_index(*at), linear_index(y, x, z, c)))
    return lax.ppermute(shard, AXES, pairs)


def first_chunk(y, x, z, c):
    if x // 2 == c:
        return (y, x ^ 1, z, 1 - c)
    return (y, 3 - x, z, c)


def second_chunk(y, x, z, c):
    return (y, x, z, 1 - c) if x // 2 == c else (y, x ^ 2, z, c)


unit_steps = (0, 1, 2, 3, 4, -1, -2, -3)


def way(z, c):
    return 1 - 2 * ((z + c) % 2)


def along(y, x, z, c):
    return (y + way(z, c), x, z, c)


def across(y, x, z, c):
    return (y, x, (z ^ 1) if c == 0 else ((z + 1) ^ 1) - 1, c)


def layer(queries, key_vectors, value_vectors, w_out):
    rows = queries.shape[0]
    wide = w_out.shape[1]

    def shape(dims, kind):
        return jax.ShapeDtypeStruct(dims, kind)

    chunk_a = moved(w_out, first_chunk)
    chunk_b = moved(w_out, second_chunk)
    states, within, rim = call(
        state_kernel,
        (shape((NX, HD, HD), f32), shape((rows // BLOCK, HD, HD), f32), shape((2, W, HD), bf16)),
        [VMEM] * 2, 2 * rows * HD * HD,
    )(key_vectors, value_vectors)
    row_states = lax.all_to_all(states, "x", 0, 0, tiled=True)
    unit = jnp.concatenate([chunk_b, chunk_a], axis=0)
    y1 = moved(unit, along)
    rim = lax.ppermute(rim, ("y", "x"), [(i, i + 1) for i in range(NY * NX - 1)])
    before, totals = call(
        row_kernel, (shape((HD, HD), f32), shape((NY, HD, HD), bf16)), [VMEM], 8 * HD * HD
    )(row_states)
    totals = lax.all_to_all(totals, "y", 0, 0, tiled=True)
    y2 = moved(y1, along)
    z1 = moved(y1, across)
    half = shape((W, HD), f32)
    work = 2 * W * (W + BLOCK) * HD * 2
    inner, inner_linear = call(inner_kernel, (half, half), [VMEM] * 3, work, W * W)(
        queries, key_vectors, value_vectors
    )
    y3 = moved(y2, along)
    z2 = moved(y2, across)
    outer, outer_linear = call(outer_kernel, (half, half), [VMEM] * 4, work, W * W)(
        queries, key_vectors, value_vectors, rim
    )
    y4 = moved(y3, along)
    z3 = moved(y3, across)
    mixed = call(
        mix_kernel, shape((NZ, rows // NZ, HD), bf16), [VMEM] * 8, 4 * rows * HD * HD
    )(queries, outer, outer_linear, inner, inner_linear, within, before, totals)
    mixed = lax.all_to_all(mixed, "z", 0, 0, tiled=True)
    given, kept = call(
        project_kernel, (shape((HD, wide), bf16), shape((HD, wide), f32)),
        [VMEM] * (1 + NY), 4 * HD * wide * NY * HD, 0, NY * HD * wide * 2,
    )(mixed, unit, y1, y2, y3, y4, z1, z2, z3)
    taken = lax.ppermute(given, "c", [(0, 1), (1, 0)])
    return call(add_kernel, shape((HD, wide), bf16), [VMEM] * 2, HD * wide)(kept, taken)


def solution(mesh):
    fine = Mesh(mesh.devices.reshape(NY, NX, NZ, NC), AXES)
    split = P(("y", "x"), ("z", "c"))
    return jax.shard_map(
        layer,
        mesh=fine,
        in_specs=(split, split, split, P(("y", "x"), None)),
        out_specs=P(AXES, None),
        check_vma=False,
    )
```

time: 118 us -> 114 us (0.966)
  the two profiles are of different devices: /device:TPU:1 before, /device:TPU:31 now
where the time goes in v2:
time: 114 us; the launch traced here: 113 us
  starting transfers between devices  60.2 us (53%)
  waiting for transfers between devices  26.8 us (24%)
  Pallas kernels  14.3 us (13%)
  local copies, waits for them, and re-layouts  11.3 us (10%)
    ppermute x9, starting transfers between devices, moved(): return lax.ppermute(shard, AXES, pairs)  31.3 us
    ppermute x9, waiting for transfers between devices, moved(): return lax.ppermute(shard, AXES, pairs)  25.2 us
    unnamed x31, local copies, waits for them, and re-layouts  11.3 us
    all_to_all x1, starting transfers between devices, layer(): mixed = lax.all_to_all(mixed, 'z', 0, 0, tiled=True)  8.02 us
    all_to_all x1, starting transfers between devices, layer(): totals = lax.all_to_all(totals, 'y', 0, 0, tiled=True)  6.81 us
    ppermute x1, starting transfers between devices, layer(): taken = lax.ppermute(given, 'c', [(0, 1), (1, 0)])  6.64 us
    all_to_all x1, starting transfers between devices, layer(): row_states = lax.all_to_all(states, 'x', 0, 0, tiled=True)  4.55 us
    pallas_call x1, Pallas kernels, layer(): call(outer_kernel, (half, half), [VMEM] * 4, work, W * W)  4.24 us
  transfers between devices with their start and end apart: 14, of which 6 were waited for; matrix products, arithmetic and copies ran while one was open for 0% of the time, Pallas kernels for 10%

profile of v2, /device:TPU:31, one launch (start us, length us, event | category | flops | bytes accessed | tf_op | source)
XLA Modules:
  0.0 112.8 jit_solution(8395500999751808614)
XLA Ops:
  0.0 3.2 %collective-permute-start.1 = (bf16[64,2048]{1,0:T(8,128)(2,1)}, bf16[64,2048]{1,0:T(8,128)(2,1)S(1)}, u32[]{:S(2)}, u32[]{:S(2)}) collective-permute-start(bf16[64,2048]{1,0:T(8,128)(2,1)} %param.7), channel_id=1, source_target_pairs={{1,0},{33,1},{3,2},{35,3},{5,4},{37,5},{7,6},{39,7},{9,8},{41,9},{... | collective-permute-start | bytes 786440 | tf_op jit(solution)/shard_map/ppermute | solution.py:215
  3.2 1.9 %collective-permute-start.2 = (bf16[64,2048]{1,0:T(8,128)(2,1)}, bf16[64,2048]{1,0:T(8,128)(2,1)S(1)}, u32[]{:S(2)}, u32[]{:S(2)}) collective-permute-start(bf16[64,2048]{1,0:T(8,128)(2,1)} %param.7), channel_id=1, source_target_pairs={{17,0},{49,1},{19,2},{51,3},{21,4},{53,5},{23,6},{55,7},{25,8},{57... | collective-permute-start | bytes 786440 | tf_op jit(solution)/shard_map/ppermute | solution.py:215
  5.1 2.3 %collective-permute-done.1 = bf16[64,2048]{1,0:T(8,128)(2,1)S(1)} collective-permute-done((bf16[64,2048]{1,0:T(8,128)(2,1)}, bf16[64,2048]{1,0:T(8,128)(2,1)S(1)}, u32[]{:S(2)}, u32[]{:S(2)}) %collective-permute-start.1) | collective-permute-done | bytes 262176 | tf_op jit(solution)/shard_map/ppermute | solution.py:215
  7.5 3.9 %collective-permute-done.2 = bf16[64,2048]{1,0:T(8,128)(2,1)S(1)} collective-permute-done((bf16[64,2048]{1,0:T(8,128)(2,1)}, bf16[64,2048]{1,0:T(8,128)(2,1)S(1)}, u32[]{:S(2)}, u32[]{:S(2)}) %collective-permute-start.2) | collective-permute-done | bytes 262176 | tf_op jit(solution)/shard_map/ppermute | solution.py:215
  11.4 4.4 %collective-permute-start.3 = (bf16[128,2048]{1,0:T(8,128)(2,1)S(1)}, bf16[128,2048]{1,0:T(8,128)(2,1)S(1)}, u32[]{:S(2)}, u32[]{:S(2)}) collective-permute-start(bf16[128,2048]{1,0:T(8,128)(2,1)S(1)} %constant_dynamic-update-slice_fusion.refs_0_), channel_id=1, source_target_pairs={{64,0},{449,1},{450,2},{67,3},{68,4},{453,5},{454,6},{71,7},{72,8}... | collective-permute-start | bytes 1572872 | tf_op jit(solution)/shard_map/ppermute | solution.py:215
  15.8 1.2 %shard_map.46 = (f32[4,128,128]{2,1,0:T(8,128)}, f32[8,128,128]{2,1,0:T(8,128)S(1)}, bf16[2,1024,128]{2,1,0:T(8,128)(2,1)}) custom-call(bf16[2048,128]{1,0:T(8,128)(2,1)S(1)} %copy-done.11, bf16[2048,128]{1,0:T(8,128)(2,1)S(1)} %copy-done.13), custom_call_target="tpu_custom_call" | custom-call | flops 67108864 | bytes 1048576 | tf_op jit(solution)/shard_map/pallas_call | solution.py:252
  17.0 0.8 copy-done.1
  17.8 4.6 %all-to-all-start = ((f32[4,128,128]{2,1,0:T(8,128)}), f32[4,128,128]{2,1,0:T(8,128)S(1)}, u32[]{:S(2)}, u32[]{:S(2)}) async-start(f32[4,128,128]{2,1,0:T(8,128)} %get-tuple-element.22), calls=%async_computation | async-start | bytes 524288 | tf_op jit(solution)/shard_map/all_to_all | solution.py:257
  22.4 0.0 collective-permute-done.3.refs_1_
  22.4 4.6 %collective-permute-start.4 = (bf16[128,2048]{1,0:T(8,128)(2,1)S(1)}, bf16[128,2048]{1,0:T(8,128)(2,1)S(1)}, u32[]{:S(2)}, u32[]{:S(2)}) collective-permute-start(bf16[128,2048]{1,0:T(8,128)(2,1)S(1)} %collective-permute-done.3.refs_1_), channel_id=1, source_target_pairs={{64,0},{449,1},{450,2},{67,3},{68,4},{453,5},{454,6},{71,7},{72,8}... | collective-permute-start | bytes 1572872 | tf_op jit(solution)/shard_map/ppermute | solution.py:215
  26.9 2.8 %collective-permute-start = (bf16[2,1024,128]{2,1,0:T(8,128)(2,1)}, bf16[2,1024,128]{2,1,0:T(8,128)(2,1)}, u32[]{:S(2)}, u32[]{:S(2)}) collective-permute-start(bf16[2,1024,128]{2,1,0:T(8,128)(2,1)} %get-tuple-element.16), channel_id=1, source_target_pairs={{0,16},{16,32},{32,48},{48,64},{64,80},{80,96},{96,112},{112,128},... | collective-permute-start | bytes 1572872 | tf_op jit(solution)/shard_map/ppermute | solution.py:260
  29.8 0.0 all-to-all-done.states_ref
  29.8 0.7 shard_map.49
  30.5 6.8 %all-to-all-start.1 = ((bf16[8,128,128]{2,1,0:T(8,128)(2,1)}), bf16[8,128,128]{2,1,0:T(8,128)(2,1)S(1)}, u32[]{:S(2)}, u32[]{:S(2)}) async-start(bf16[8,128,128]{2,1,0:T(8,128)(2,1)} %get-tuple-element.24), calls=%async_computation.1 | async-start | bytes 524288 | tf_op jit(solution)/shard_map/all_to_all | solution.py:264
  37.3 0.0 collective-permute-done.4.refs_2_
  37.3 4.3 %collective-permute-start.5 = (bf16[128,2048]{1,0:T(8,128)(2,1)S(1)}, bf16[128,2048]{1,0:T(8,128)(2,1)S(1)}, u32[]{:S(2)}, u32[]{:S(2)}) collective-permute-start(bf16[128,2048]{1,0:T(8,128)(2,1)S(1)} %collective-permute-done.4.refs_2_), channel_id=1, source_target_pairs={{64,0},{449,1},{450,2},{67,3},{68,4},{453,5},{454,6},{71,7},{72,8}... | collective-permute-start | bytes 1572872 | tf_op jit(solution)/shard_map/ppermute | solution.py:215
  41.6 0.0 copy-start.12
  41.6 1.0 copy-done.12
  42.7 1.0 copy-done.14
  43.7 2.6 %shard_map.48 = (f32[1024,128]{1,0:T(8,128)S(1)}, f32[1024,128]{1,0:T(8,128)S(1)}) custom-call(bf16[2048,128]{1,0:T(8,128)(2,1)S(1)} %copy-done, bf16[2048,128]{1,0:T(8,128)(2,1)S(1)} %copy-done.12, bf16[2048,128]{1,0:T(8,128)(2,1)S(1)} %copy-done.14), custom_call_target="tpu_custom_call" | custom-call | flops 671088640 | bytes 1048576 | tf_op jit(solution)/shard_map/pallas_call | solution.py:269
  46.3 0.8 copy-done.3
  47.1 0.8 copy-done.5
  47.9 4.2 %shard_map.47 = (f32[1024,128]{1,0:T(8,128)S(1)}, f32[1024,128]{1,0:T(8,128)S(1)}) custom-call(bf16[2048,128]{1,0:T(8,128)(2,1)S(1)} %copy-done, bf16[2048,128]{1,0:T(8,128)(2,1)S(1)} %copy-done.12, bf16[2048,128]{1,0:T(8,128)(2,1)S(1)} %copy-done.14, bf16[2,1024,128]{2,1,0:T(8,128)(2,1)} %collective-permute-done.rim_ref), custom_call_target="tpu_custom_call" | custom-call | flops 671088640 | bytes 1048576 | tf_op jit(solution)/shard_map/pallas_call | solution.py:274
  52.1 0.0 copy-start.7
  52.1 0.8 copy-done.7
  52.9 0.8 copy-done.9
  53.7 0.0 all-to-all-done.1.totals_ref
  53.7 1.0 copy-done.2
  54.7 1.0 copy-done.4
  55.8 1.0 copy-done.6
  56.8 1.0 copy-done.8
  57.9 1.0 copy-done.10
  58.9 2.2 %shard_map.50 = bf16[8,256,128]{2,1,0:T(8,128)(2,1)} custom-call(bf16[2048,128]{1,0:T(8,128)(2,1)S(1)} %copy-done, f32[1024,128]{1,0:T(8,128)S(1)} %copy-done.8, f32[1024,128]{1,0:T(8,128)S(1)} %copy-done.10, f32[1024,128]{1,0:T(8,128)S(1)} %copy-done.4, f32[1024,128]{1,0:T(8,128)S(1)} %copy-done.6, f32[8,128,128]{2,1,0:T(8,128)S(1)} %copy-done.2, ...), custom_call_target="tpu_custom_call" | custom-call | flops 134217728 | bytes 1048576 | tf_op jit(solution)/shard_map/pallas_call | solution.py:279
  61.1 8.0 %all-to-all-start.2 = ((bf16[8,256,128]{2,1,0:T(8,128)(2,1)}), bf16[8,256,128]{2,1,0:T(8,128)(2,1)S(1)}, u32[]{:S(2)}, u32[]{:S(2)}) async-start(bf16[8,256,128]{2,1,0:T(8,128)(2,1)} %shard_map.50), calls=%async_computation.2 | async-start | bytes 1048576 | tf_op jit(solution)/shard_map/all_to_all | solution.py:282
  69.1 4.6 %collective-permute-start.7 = (bf16[128,2048]{1,0:T(8,128)(2,1)S(1)}, bf16[128,2048]{1,0:T(8,128)(2,1)S(1)}, u32[]{:S(2)}, u32[]{:S(2)}) collective-permute-start(bf16[128,2048]{1,0:T(8,128)(2,1)S(1)} %collective-permute-done.3.refs_1_), channel_id=1, source_target_pairs={{2,0},{15,1},{0,2},{5,3},{6,4},{3,5},{4,6},{9,7},{10,8},{7,9},{8,1... | collective-permute-start | bytes 1572872 | tf_op jit(solution)/shard_map/ppermute | solution.py:215
  73.7 1.9 %collective-permute-start.8 = (bf16[128,2048]{1,0:T(8,128)(2,1)S(1)}, bf16[128,2048]{1,0:T(8,128)(2,1)}, u32[]{:S(2)}, u32[]{:S(2)}) collective-permute-start(bf16[128,2048]{1,0:T(8,128)(2,1)S(1)} %collective-permute-done.4.refs_2_), channel_id=1, source_target_pairs={{2,0},{15,1},{0,2},{5,3},{6,4},{3,5},{4,6},{9,7},{10,8},{7,9},{8,1... | collective-permute-start | bytes 1572872 | tf_op jit(solution)/shard_map/ppermute | solution.py:215
  75.6 0.0 collective-permute-done.5.refs_3_
  75.6 2.2 %collective-permute-start.6 = (bf16[128,2048]{1,0:T(8,128)(2,1)S(1)}, bf16[128,2048]{1,0:T(8,128)(2,1)}, u32[]{:S(2)}, u32[]{:S(2)}) collective-permute-start(bf16[128,2048]{1,0:T(8,128)(2,1)S(1)} %collective-permute-done.5.refs_3_), channel_id=1, source_target_pairs={{64,0},{449,1},{450,2},{67,3},{68,4},{453,5},{454,6},{71,7},{72,8}... | collective-permute-start | bytes 1572872 | tf_op jit(solution)/shard_map/ppermute | solution.py:215
  77.8 4.3 %collective-permute-start.9 = (bf16[128,2048]{1,0:T(8,128)(2,1)S(1)}, bf16[128,2048]{1,0:T(8,128)(2,1)}, u32[]{:S(2)}, u32[]{:S(2)}) collective-permute-start(bf16[128,2048]{1,0:T(8,128)(2,1)S(1)} %collective-permute-done.5.refs_3_), channel_id=1, source_target_pairs={{2,0},{15,1},{0,2},{5,3},{6,4},{3,5},{4,6},{9,7},{10,8},{7,9},{8,1... | collective-permute-start | bytes 1572872 | tf_op jit(solution)/shard_map/ppermute | solution.py:215
  82.1 2.4 %collective-permute-done.7.refs_5_ = bf16[128,2048]{1,0:T(8,128)(2,1)S(1)} collective-permute-done((bf16[128,2048]{1,0:T(8,128)(2,1)S(1)}, bf16[128,2048]{1,0:T(8,128)(2,1)S(1)}, u32[]{:S(2)}, u32[]{:S(2)}) %collective-permute-start.7) | collective-permute-done | bytes 524320 | tf_op jit(solution)/shard_map/ppermute | solution.py:215
  84.6 0.0 all-to-all-done.2.mixed_ref
  84.6 11.2 %collective-permute-done.8.refs_6_ = bf16[128,2048]{1,0:T(8,128)(2,1)} collective-permute-done((bf16[128,2048]{1,0:T(8,128)(2,1)S(1)}, bf16[128,2048]{1,0:T(8,128)(2,1)}, u32[]{:S(2)}, u32[]{:S(2)}) %collective-permute-start.8) | collective-permute-done | bytes 524320 | tf_op jit(solution)/shard_map/ppermute | solution.py:215
  95.8 0.0 collective-permute-done.6.refs_4_
  95.8 5.3 %collective-permute-done.9.refs_7_ = bf16[128,2048]{1,0:T(8,128)(2,1)} collective-permute-done((bf16[128,2048]{1,0:T(8,128)(2,1)S(1)}, bf16[128,2048]{1,0:T(8,128)(2,1)}, u32[]{:S(2)}, u32[]{:S(2)}) %collective-permute-start.9) | collective-permute-done | bytes 524320 | tf_op jit(solution)/shard_map/ppermute | solution.py:215
  101.1 2.6 %shard_map.51 = (bf16[128,2048]{1,0:T(8,128)(2,1)S(1)}, f32[128,2048]{1,0:T(8,128)S(1)}) custom-call(bf16[8,256,128]{2,1,0:T(8,128)(2,1)S(1)} %all-to-all-done.2.mixed_ref, bf16[128,2048]{1,0:T(8,128)(2,1)S(1)} %constant_dynamic-update-slice_fusion.refs_0_, bf16[128,2048]{1,0:T(8,128)(2,1)S(1)} %collective-permute-done.3.refs_1_, ...), custom_call_target="tpu_custom_call" | custom-call | flops 1073741824 | bytes 4194304 | tf_op jit(solution)/shard_map/pallas_call | solution.py:283
  103.7 6.6 %collective-permute-start.10 = (bf16[128,2048]{1,0:T(8,128)(2,1)S(1)}, bf16[128,2048]{1,0:T(8,128)(2,1)S(1)}, u32[]{:S(2)}, u32[]{:S(2)}) collective-permute-start(bf16[128,2048]{1,0:T(8,128)(2,1)S(1)} %get-tuple-element.26), channel_id=1, source_target_pairs={{0,1},{1,0},{2,3},{3,2},{4,5},{5,4},{6,7},{7,6},{8,9},{9,8},{10,11... | collective-permute-start | bytes 1572872 | tf_op jit(solution)/shard_map/ppermute | solution.py:287
  110.4 1.5 %collective-permute-done.10.taken_ref = bf16[128,2048]{1,0:T(8,128)(2,1)S(1)} collective-permute-done((bf16[128,2048]{1,0:T(8,128)(2,1)S(1)}, bf16[128,2048]{1,0:T(8,128)(2,1)S(1)}, u32[]{:S(2)}, u32[]{:S(2)}) %collective-permute-start.10) | collective-permute-done | bytes 524320 | tf_op jit(solution)/shard_map/ppermute | solution.py:287
  111.9 0.9 shard_map.52
  (19 shorter events, 0.1 us)
Async XLA Ops:
  0.0 15.8 %copy-start.11 = (bf16[2048,128]{1,0:T(8,128)(2,1)S(1)}, bf16[2048,128]{1,0:T(8,128)(2,1)}, u32[]{:S(2)}) copy-start(bf16[2048,128]{1,0:T(8,128)(2,1)} %k_ref.5) | copy-start | bytes 1572868
  0.0 15.8 %copy-start.13 = (bf16[2048,128]{1,0:T(8,128)(2,1)S(1)}, bf16[2048,128]{1,0:T(8,128)(2,1)}, u32[]{:S(2)}) copy-start(bf16[2048,128]{1,0:T(8,128)(2,1)} %v_ref.5) | copy-start | bytes 1572868
  0.0 7.4 %collective-permute-start.1 = (bf16[64,2048]{1,0:T(8,128)(2,1)}, bf16[64,2048]{1,0:T(8,128)(2,1)S(1)}, u32[]{:S(2)}, u32[]{:S(2)}) collective-permute-start(bf16[64,2048]{1,0:T(8,128)(2,1)} %param.7), channel_id=1, source_target_pairs={{1,0},{33,1},{3,2},{35,3},{5,4},{37,5},{7,6},{39,7},{9,8},{41,9},{... | collective-permute-start | bytes 786440 | tf_op jit(solution)/shard_map/ppermute | solution.py:215
  3.2 8.2 %collective-permute-start.2 = (bf16[64,2048]{1,0:T(8,128)(2,1)}, bf16[64,2048]{1,0:T(8,128)(2,1)S(1)}, u32[]{:S(2)}, u32[]{:S(2)}) collective-permute-start(bf16[64,2048]{1,0:T(8,128)(2,1)} %param.7), channel_id=1, source_target_pairs={{17,0},{49,1},{19,2},{51,3},{21,4},{53,5},{23,6},{55,7},{25,8},{57... | collective-permute-start | bytes 786440 | tf_op jit(solution)/shard_map/ppermute | solution.py:215
  11.4 11.0 %collective-permute-start.3 = (bf16[128,2048]{1,0:T(8,128)(2,1)S(1)}, bf16[128,2048]{1,0:T(8,128)(2,1)S(1)}, u32[]{:S(2)}, u32[]{:S(2)}) collective-permute-start(bf16[128,2048]{1,0:T(8,128)(2,1)S(1)} %constant_dynamic-update-slice_fusion.refs_0_), channel_id=1, source_target_pairs={{64,0},{449,1},{450,2},{67,3},{68,4},{453,5},{454,6},{71,7},{72,8}... | collective-permute-start | bytes 1572872 | tf_op jit(solution)/shard_map/ppermute | solution.py:215
  17.0 0.8 copy-start.1
  17.8 12.0 %all-to-all-start = ((f32[4,128,128]{2,1,0:T(8,128)}), f32[4,128,128]{2,1,0:T(8,128)S(1)}, u32[]{:S(2)}, u32[]{:S(2)}) async-start(f32[4,128,128]{2,1,0:T(8,128)} %get-tuple-element.22), calls=%async_computation | async-start | bytes 524288 | tf_op jit(solution)/shard_map/all_to_all | solution.py:257
  22.4 19.3 %copy-start = (bf16[2048,128]{1,0:T(8,128)(2,1)S(1)}, bf16[2048,128]{1,0:T(8,128)(2,1)}, u32[]{:S(2)}) copy-start(bf16[2048,128]{1,0:T(8,128)(2,1)} %q_ref.5) | copy-start | bytes 1572868
  22.4 14.9 %collective-permute-start.4 = (bf16[128,2048]{1,0:T(8,128)(2,1)S(1)}, bf16[128,2048]{1,0:T(8,128)(2,1)S(1)}, u32[]{:S(2)}, u32[]{:S(2)}) collective-permute-start(bf16[128,2048]{1,0:T(8,128)(2,1)S(1)} %collective-permute-done.3.refs_1_), channel_id=1, source_target_pairs={{64,0},{449,1},{450,2},{67,3},{68,4},{453,5},{454,6},{71,7},{72,8}... | collective-permute-start | bytes 1572872 | tf_op jit(solution)/shard_map/ppermute | solution.py:215
  26.9 20.9 %collective-permute-start = (bf16[2,1024,128]{2,1,0:T(8,128)(2,1)}, bf16[2,1024,128]{2,1,0:T(8,128)(2,1)}, u32[]{:S(2)}, u32[]{:S(2)}) collective-permute-start(bf16[2,1024,128]{2,1,0:T(8,128)(2,1)} %get-tuple-element.16), channel_id=1, source_target_pairs={{0,16},{16,32},{32,48},{48,64},{64,80},{80,96},{96,112},{112,128},... | collective-permute-start | bytes 1572872 | tf_op jit(solution)/shard_map/ppermute | solution.py:260
  30.5 23.2 %all-to-all-start.1 = ((bf16[8,128,128]{2,1,0:T(8,128)(2,1)}), bf16[8,128,128]{2,1,0:T(8,128)(2,1)S(1)}, u32[]{:S(2)}, u32[]{:S(2)}) async-start(bf16[8,128,128]{2,1,0:T(8,128)(2,1)} %get-tuple-element.24), calls=%async_computation.1 | async-start | bytes 524288 | tf_op jit(solution)/shard_map/all_to_all | solution.py:264
  37.3 38.3 %collective-permute-start.5 = (bf16[128,2048]{1,0:T(8,128)(2,1)S(1)}, bf16[128,2048]{1,0:T(8,128)(2,1)S(1)}, u32[]{:S(2)}, u32[]{:S(2)}) collective-permute-start(bf16[128,2048]{1,0:T(8,128)(2,1)S(1)} %collective-permute-done.4.refs_2_), channel_id=1, source_target_pairs={{64,0},{449,1},{450,2},{67,3},{68,4},{453,5},{454,6},{71,7},{72,8}... | collective-permute-start | bytes 1572872 | tf_op jit(solution)/shard_map/ppermute | solution.py:215
  41.6 1.0 copy-start.12
  42.7 1.0 copy-start.14
  46.3 0.8 copy-start.3
  47.1 0.8 copy-start.5
  52.1 0.8 copy-start.7
  52.9 0.8 copy-start.9
  53.7 1.0 copy-start.2
  54.7 1.0 copy-start.4
  55.8 1.0 copy-start.6
  56.8 1.0 copy-start.8
  57.9 1.0 copy-start.10
  61.1 23.5 %all-to-all-start.2 = ((bf16[8,256,128]{2,1,0:T(8,128)(2,1)}), bf16[8,256,128]{2,1,0:T(8,128)(2,1)S(1)}, u32[]{:S(2)}, u32[]{:S(2)}) async-start(bf16[8,256,128]{2,1,0:T(8,128)(2,1)} %shard_map.50), calls=%async_computation.2 | async-start | bytes 1048576 | tf_op jit(solution)/shard_map/all_to_all | solution.py:282
  69.1 15.5 %collective-permute-start.7 = (bf16[128,2048]{1,0:T(8,128)(2,1)S(1)}, bf16[128,2048]{1,0:T(8,128)(2,1)S(1)}, u32[]{:S(2)}, u32[]{:S(2)}) collective-permute-start(bf16[128,2048]{1,0:T(8,128)(2,1)S(1)} %collective-permute-done.3.refs_1_), channel_id=1, source_target_pairs={{2,0},{15,1},{0,2},{5,3},{6,4},{3,5},{4,6},{9,7},{10,8},{7,9},{8,1... | collective-permute-start | bytes 1572872 | tf_op jit(solution)/shard_map/ppermute | solution.py:215
  73.7 22.1 %collective-permute-start.8 = (bf16[128,2048]{1,0:T(8,128)(2,1)S(1)}, bf16[128,2048]{1,0:T(8,128)(2,1)}, u32[]{:S(2)}, u32[]{:S(2)}) collective-permute-start(bf16[128,2048]{1,0:T(8,128)(2,1)S(1)} %collective-permute-done.4.refs_2_), channel_id=1, source_target_pairs={{2,0},{15,1},{0,2},{5,3},{6,4},{3,5},{4,6},{9,7},{10,8},{7,9},{8,1... | collective-permute-start | bytes 1572872 | tf_op jit(solution)/shard_map/ppermute | solution.py:215
  75.6 20.2 %collective-permute-start.6 = (bf16[128,2048]{1,0:T(8,128)(2,1)S(1)}, bf16[128,2048]{1,0:T(8,128)(2,1)}, u32[]{:S(2)}, u32[]{:S(2)}) collective-permute-start(bf16[128,2048]{1,0:T(8,128)(2,1)S(1)} %collective-permute-done.5.refs_3_), channel_id=1, source_target_pairs={{64,0},{449,1},{450,2},{67,3},{68,4},{453,5},{454,6},{71,7},{72,8}... | collective-permute-start | bytes 1572872 | tf_op jit(solution)/shard_map/ppermute | solution.py:215
  77.8 23.3 %collective-permute-start.9 = (bf16[128,2048]{1,0:T(8,128)(2,1)S(1)}, bf16[128,2048]{1,0:T(8,128)(2,1)}, u32[]{:S(2)}, u32[]{:S(2)}) collective-permute-start(bf16[128,2048]{1,0:T(8,128)(2,1)S(1)} %collective-permute-done.5.refs_3_), channel_id=1, source_target_pairs={{2,0},{15,1},{0,2},{5,3},{6,4},{3,5},{4,6},{9,7},{10,8},{7,9},{8,1... | collective-permute-start | bytes 1572872 | tf_op jit(solution)/shard_map/ppermute | solution.py:215
  103.7 8.2 %collective-permute-start.10 = (bf16[128,2048]{1,0:T(8,128)(2,1)S(1)}, bf16[128,2048]{1,0:T(8,128)(2,1)S(1)}, u32[]{:S(2)}, u32[]{:S(2)}) collective-permute-start(bf16[128,2048]{1,0:T(8,128)(2,1)S(1)} %get-tuple-element.26), channel_id=1, source_target_pairs={{0,1},{1,0},{2,3},{3,2},{4,5},{5,4},{6,7},{7,6},{8,9},{9,8},{10,11... | collective-permute-start | bytes 1572872 | tf_op jit(solution)/shard_map/ppermute | solution.py:287

commit v3 on v2

--- a/solution.py
+++ b/solution.py
@@ -11,6 +11,7 @@
 HD = 128
 W = 1024
 BLOCK = 256
+FETCHES = 4
 NY, NX, NZ, NC = 8, 4, 8, 2
 AXES = ("y", "x", "z", "c")
 
@@ -43,17 +44,18 @@
 
 
 VMEM = pl.BlockSpec(memory_space=pltpu.VMEM)
-SMEM = pl.BlockSpec(memory_space=pltpu.SMEM)
-
-
-def call(kernel, outs, in_specs, flops, trans=0, nbytes=1 << 20):
+ANY = pl.BlockSpec(memory_space=pl.ANY)
+
+
+def call(kernel, outs, in_specs, scratch=(), grant=12 << 20, out_specs=None):
     return pl.pallas_call(
         kernel,
         out_shape=outs,
         in_specs=in_specs,
-        out_specs=jax.tree.map(lambda _: VMEM, outs),
-        compiler_params=pltpu.CompilerParams(vmem_limit_bytes=12 << 20),
-        cost_estimate=pl.CostEstimate(flops=flops, transcendentals=trans, bytes_accessed=nbytes),
+        scratch_shapes=scratch,
+        out_specs=out_specs or jax.tree.map(lambda _: VMEM, outs),
+        compiler_params=pltpu.CompilerParams(vmem_limit_bytes=grant),
+        cost_estimate=pl.CostEstimate(flops=1, transcendentals=0, bytes_accessed=64 << 20),
     )
 
 
@@ -61,16 +63,40 @@
     return ref[index * BLOCK : (index + 1) * BLOCK, :]
 
 
-def state_kernel(k_ref, v_ref, out_ref, before_ref, rim_ref):
-    count = k_ref.shape[0] // BLOCK
+def state_kernel(k_hbm, v_hbm, out_hbm, before_hbm, rim_hbm, k_ref, v_ref, before_ref, total_ref, sems, out_sems):
+    chunk = k_hbm.shape[0] // FETCHES
+    copies = []
+    for i in range(FETCHES):
+        part = pl.ds(i * chunk, chunk)
+        pair = (
+            pltpu.make_async_copy(k_hbm.at[part], k_ref.at[part], sems.at[0, i]),
+            pltpu.make_async_copy(v_hbm.at[part], v_ref.at[part], sems.at[1, i]),
+        )
+        for copy in pair:
+            copy.start()
+        copies.append(pair)
+    tail = pl.ds(k_hbm.shape[0] - W, W)
+    sent = [
+        pltpu.make_async_copy(k_ref.at[tail], rim_hbm.at[0], out_sems.at[0]),
+        pltpu.make_async_copy(v_ref.at[tail], rim_hbm.at[1], out_sems.at[1]),
+    ]
     total = jnp.zeros((HD, HD), f32)
-    for b in range(count):
-        before_ref[b] = total
-        total = total + dot_tn(rows_of(k_ref, b), rows_of(v_ref, b))
-    for i in range(NX):
-        out_ref[i] = total
-    rim_ref[0] = k_ref[k_ref.shape[0] - W :, :]
-    rim_ref[1] = v_ref[v_ref.shape[0] - W :, :]
+    for i in range(FETCHES):
+        for copy in copies[i]:
+            copy.wait()
+        if i == FETCHES - 1:
+            for copy in sent:
+                copy.start()
+        for b in range(i * chunk // BLOCK, (i + 1) * chunk // BLOCK):
+            before_ref[b] = total
+            total = total + dot_tn(rows_of(k_ref, b), rows_of(v_ref, b))
+    total_ref[...] = total
+    last = [pltpu.make_async_copy(before_ref, before_hbm, out_sems.at[2])]
+    last += [pltpu.make_async_copy(total_ref, out_hbm.at[i], out_sems.at[3 + i]) for i in range(NX)]
+    for copy in last:
+        copy.start()
+    for copy in sent + last:
+        copy.wait()
 
 
 def row_kernel(states_ref, before_ref, total_ref):
@@ -115,23 +141,50 @@
     return cols > rows
 
 
-def inner_kernel(q_ref, k_ref, v_ref, soft_ref, linear_ref):
+def prior_state(before_ref, totals_ref):
+    y = lax.axis_index("y")
+    prior = before_ref[...]
+    for i in range(NY):
+        prior = prior + jnp.where(i < y, totals_ref[i].astype(f32), 0.0)
+    return prior
+
+
+def mix(q, soft, linear, state):
+    upper, lower = split_pair(state)
+    both = dot(q, jnp.concatenate([upper, lower], axis=1))
+    linear = linear + (both[:, :HD] + both[:, HD:])
+    return (soft + normalize(linear) * 0.5).astype(bf16)
+
+
+def inner_kernel(q_ref, k_ref, v_ref, within_ref, before_ref, totals_ref, out_ref):
     upper = upper_mask()
+    prior = prior_state(before_ref, totals_ref)
     near = W // BLOCK
-    for b in range(near):
-        keys = [rows_of(k_ref, b + j) for j in range(near + 1)]
-        values = [rows_of(v_ref, b + j) for j in range(near + 1)]
-        soft, linear = block_rows(rows_of(q_ref, near + b), keys, values, None, upper)
-        soft_ref[b * BLOCK : (b + 1) * BLOCK, :] = soft
-        linear_ref[b * BLOCK : (b + 1) * BLOCK, :] = linear
-
-
-def outer_kernel(q_ref, k_ref, v_ref, rim_ref, soft_ref, linear_ref):
+    for b in range(near, q_ref.shape[0] // BLOCK):
+        q = rows_of(q_ref, b)
+        keys = [rows_of(k_ref, b - near + j) for j in range(near + 1)]
+        values = [rows_of(v_ref, b - near + j) for j in range(near + 1)]
+        soft, linear = block_rows(q, keys, values, None, upper)
+        out_ref[b - near] = mix(q, soft, linear, prior + within_ref[b])
+
+
+def outer_kernel(
+    q_ref, k_ref, v_ref, rim_hbm, within_ref, before_ref, totals_ref, inner_ref, out_hbm, rim_ref, out_ref, sems, out_sems
+):
+    near = W // BLOCK
+    copies = []
+    for j in reversed(range(near)):
+        part = pl.ds(j * BLOCK, BLOCK)
+        copies.append(pltpu.make_async_copy(rim_hbm.at[:, part], rim_ref.at[:, part], sems.at[j]))
+        copies[-1].start()
+    sent = [pltpu.make_async_copy(inner_ref, out_hbm.at[pl.ds(near, near)], out_sems.at[near])]
+    sent[0].start()
     upper = upper_mask()
-    near = W // BLOCK
+    prior = prior_state(before_ref, totals_ref)
     first = jnp.logical_and(lax.axis_index("y") == 0, lax.axis_index("x") == 0)
     hidden = jnp.where(first, far_below, 0.0).astype(f32)
-    for b in range(near):
+    for b in reversed(range(near)):
+        copies[near - 1 - b].wait()
         keys, values, bias = [], [], []
         for j in range(near + 1):
             at = b + j
@@ -143,35 +196,27 @@
                 keys.append(rows_of(k_ref, at - near))
                 values.append(rows_of(v_ref, at - near))
                 bias.append(None)
-        soft, linear = block_rows(rows_of(q_ref, b), keys, values, bias, upper)
-        soft_ref[b * BLOCK : (b + 1) * BLOCK, :] = soft
-        linear_ref[b * BLOCK : (b + 1) * BLOCK, :] = linear
-
-
-def mix_kernel(
-    q_ref, outer_ref, outer_linear_ref, inner_ref, inner_linear_ref, within_ref, before_ref, totals_ref, out_ref
-):
-    y = lax.axis_index("y")
+        q = rows_of(q_ref, b)
+        soft, linear = block_rows(q, keys, values, bias, upper)
+        out_ref[b] = mix(q, soft, linear, prior + within_ref[b])
+        sent.append(pltpu.make_async_copy(out_ref.at[b], out_hbm.at[b], out_sems.at[b]))
+        sent[-1].start()
+    for copy in sent:
+        copy.wait()
+
+
+def unit_kernel(first_ref, second_ref, out_ref):
+    half = first_ref.shape[0]
     odd = lax.axis_index("x") % 2 == 1
-    shift = jnp.where(odd, HD // 2, 0)
-    prior = before_ref[...]
-    for i in range(NY):
-        prior = prior + jnp.where(i < y, totals_ref[i].astype(f32), 0.0)
-    half = W // BLOCK
-    for b in range(q_ref.shape[0] // BLOCK):
-        upper, lower = split_pair(prior + within_ref[b])
-        both = dot(rows_of(q_ref, b), jnp.concatenate([upper, lower], axis=1))
-        near = rows_of(outer_linear_ref, b) if b < half else rows_of(inner_linear_ref, b - half)
-        soft = rows_of(outer_ref, b) if b < half else rows_of(inner_ref, b - half)
-        linear = near + (both[:, :HD] + both[:, HD:])
-        mixed = soft + normalize(linear) * 0.5
-        out_ref[b] = pltpu.roll(mixed, shift, 1).astype(bf16)
+    first, second = first_ref[...], second_ref[...]
+    out_ref[:half, :] = jnp.where(odd, second, first)
+    out_ref[half:, :] = jnp.where(odd, first, second)
 
 
 def project_kernel(mixed_ref, *refs):
     units, given_ref, kept_ref = refs[:-2], refs[-2], refs[-1]
-    y, z, c = lax.axis_index("y"), lax.axis_index("z"), lax.axis_index("c")
-    turn = way(z, c)
+    y, x, c = lax.axis_index("y"), lax.axis_index("x"), lax.axis_index("c")
+    turn = way(x, c)
     given, kept = [], []
     for step in unit_steps:
         head = lax.rem(y + turn * step + NY, NY)
@@ -228,16 +273,16 @@
 unit_steps = (0, 1, 2, 3, 4, -1, -2, -3)
 
 
-def way(z, c):
-    return 1 - 2 * ((z + c) % 2)
+def way(x, c):
+    return 1 - 2 * ((x + c) % 2)
 
 
 def along(y, x, z, c):
-    return (y + way(z, c), x, z, c)
+    return (y + way(x, c), x, z, c)
 
 
 def across(y, x, z, c):
-    return (y, x, (z ^ 1) if c == 0 else ((z + 1) ^ 1) - 1, c)
+    return (y, (x ^ 1) if c == 0 else ((x + 1) ^ 1) - 1, z, c)
 
 
 def layer(queries, key_vectors, value_vectors, w_out):
@@ -252,40 +297,45 @@
     states, within, rim = call(
         state_kernel,
         (shape((NX, HD, HD), f32), shape((rows // BLOCK, HD, HD), f32), shape((2, W, HD), bf16)),
-        [VMEM] * 2, 2 * rows * HD * HD,
+        [ANY] * 2,
+        grant=60 << 20, out_specs=[ANY] * 3,
+        scratch=[pltpu.VMEM((rows, HD), bf16)] * 2
+        + [pltpu.VMEM((rows // BLOCK, HD, HD), f32), pltpu.VMEM((HD, HD), f32)]
+        + [pltpu.SemaphoreType.DMA((2, FETCHES)), pltpu.SemaphoreType.DMA((3 + NX,))],
     )(key_vectors, value_vectors)
     row_states = lax.all_to_all(states, "x", 0, 0, tiled=True)
-    unit = jnp.concatenate([chunk_b, chunk_a], axis=0)
+    unit = call(unit_kernel, shape((2 * w_out.shape[0], wide), bf16), [VMEM] * 2)(chunk_b, chunk_a)
     y1 = moved(unit, along)
     rim = lax.ppermute(rim, ("y", "x"), [(i, i + 1) for i in range(NY * NX - 1)])
     before, totals = call(
-        row_kernel, (shape((HD, HD), f32), shape((NY, HD, HD), bf16)), [VMEM], 8 * HD * HD
+        row_kernel, (shape((HD, HD), f32), shape((NY, HD, HD), bf16)), [VMEM]
     )(row_states)
     totals = lax.all_to_all(totals, "y", 0, 0, tiled=True)
     y2 = moved(y1, along)
-    z1 = moved(y1, across)
-    half = shape((W, HD), f32)
-    work = 2 * W * (W + BLOCK) * HD * 2
-    inner, inner_linear = call(inner_kernel, (half, half), [VMEM] * 3, work, W * W)(
-        queries, key_vectors, value_vectors
+    e1 = moved(y1, across)
+    shared = (within, before, totals)
+    inner = call(inner_kernel, shape((NZ // 2, rows // NZ, HD), bf16), [VMEM] * 6)(
+        queries, key_vectors, value_vectors, *shared
     )
     y3 = moved(y2, along)
-    z2 = moved(y2, across)
-    outer, outer_linear = call(outer_kernel, (half, half), [VMEM] * 4, work, W * W)(
-        queries, key_vectors, value_vectors, rim
+    e2 = moved(y2, across)
+    mixed = call(
+        outer_kernel, shape((NZ, rows // NZ, HD), bf16), [VMEM] * 3 + [ANY] + [VMEM] * 4,
+        out_specs=ANY,
+        scratch=[pltpu.VMEM((2, W, HD), bf16), pltpu.VMEM((W // BLOCK, BLOCK, HD), bf16)]
+        + [pltpu.SemaphoreType.DMA((W // BLOCK,)), pltpu.SemaphoreType.DMA((1 + W // BLOCK,))],
+    )(
+        queries, key_vectors, value_vectors, rim, *shared, inner
     )
+    mixed = lax.all_to_all(mixed, "z", 0, 0, tiled=True)
     y4 = moved(y3, along)
-    z3 = moved(y3, across)
-    mixed = call(
-        mix_kernel, shape((NZ, rows // NZ, HD), bf16), [VMEM] * 8, 4 * rows * HD * HD
-    )(queries, outer, outer_linear, inner, inner_linear, within, before, totals)
-    mixed = lax.all_to_all(mixed, "z", 0, 0, tiled=True)
+    e3 = moved(y3, across)
     given, kept = call(
         project_kernel, (shape((HD, wide), bf16), shape((HD, wide), f32)),
-        [VMEM] * (1 + NY), 4 * HD * wide * NY * HD, 0, NY * HD * wide * 2,
-    )(mixed, unit, y1, y2, y3, y4, z1, z2, z3)
+        [VMEM] * (1 + NY),
+    )(mixed, unit, y1, y2, y3, y4, e1, e2, e3)
     taken = lax.ppermute(given, "c", [(0, 1), (1, 0)])
-    return call(add_kernel, shape((HD, wide), bf16), [VMEM] * 2, HD * wide)(kept, taken)
+    return call(add_kernel, shape((HD, wide), bf16), [VMEM] * 2)(kept, taken)
 
 
 def solution(mesh):

time: 114 us -> 106 us (0.930)
  the two profiles are of different devices: /device:TPU:31 before, /device:TPU:7 now
where the time goes in v3:
time: 106 us; the launch traced here: 105 us
  starting transfers between devices  62.2 us (59%)
  waiting for transfers between devices  26.1 us (25%)
  Pallas kernels  15 us (14%)
  local copies, waits for them, and re-layouts  1.76 us (2%)
    ppermute x9, starting transfers between devices, moved(): return lax.ppermute(shard, AXES, pairs)  32.3 us
    ppermute x9, waiting for transfers between devices, moved(): return lax.ppermute(shard, AXES, pairs)  14.9 us
    ppermute x1, starting transfers between devices, layer(): taken = lax.ppermute(given, 'c', [(0, 1), (1, 0)])  9.14 us
    all_to_all x1, waiting for transfers between devices, layer(): totals = lax.all_to_all(totals, 'y', 0, 0, tiled=True)  8.56 us
    all_to_all x1, starting transfers between devices, layer(): mixed = lax.all_to_all(mixed, 'z', 0, 0, tiled=True)  8.33 us
    all_to_all x1, starting transfers between devices, layer(): row_states = lax.all_to_all(states, 'x', 0, 0, tiled=True)  5.78 us
    pallas_call x1, Pallas kernels, layer(): call(outer_kernel, shape((NZ, rows // NZ, HD), bf16), [VMEM] * 3 + [ANY]...  5.7 us
    all_to_all x1, starting transfers between devices, layer(): totals = lax.all_to_all(totals, 'y', 0, 0, tiled=True)  4.79 us
  transfers between devices with their start and end apart: 14, of which 8 were waited for; matrix products, arithmetic and copies ran while one was open for 0% of the time, Pallas kernels for 11%

profile of v3, /device:TPU:7, one launch (start us, length us, event | category | flops | bytes accessed | tf_op | source)
XLA Modules:
  0.0 105.3 jit_solution(464637937049440790)
XLA Ops:
  0.0 3.0 %collective-permute-start.1 = (bf16[64,2048]{1,0:T(8,128)(2,1)}, bf16[64,2048]{1,0:T(8,128)(2,1)S(1)}, u32[]{:S(2)}, u32[]{:S(2)}) collective-permute-start(bf16[64,2048]{1,0:T(8,128)(2,1)} %param.7), channel_id=1, source_target_pairs={{1,0},{33,1},{3,2},{35,3},{5,4},{37,5},{7,6},{39,7},{9,8},{41,9},{... | collective-permute-start | bytes 786440 | tf_op jit(solution)/shard_map/ppermute | solution.py:260
  3.0 7.0 %collective-permute-start.2 = (bf16[64,2048]{1,0:T(8,128)(2,1)}, bf16[64,2048]{1,0:T(8,128)(2,1)S(1)}, u32[]{:S(2)}, u32[]{:S(2)}) collective-permute-start(bf16[64,2048]{1,0:T(8,128)(2,1)} %param.7), channel_id=1, source_target_pairs={{17,0},{49,1},{19,2},{51,3},{21,4},{53,5},{23,6},{55,7},{25,8},{57... | collective-permute-start | bytes 786440 | tf_op jit(solution)/shard_map/ppermute | solution.py:260
  10.0 0.0 collective-permute-done.1.first_ref
  10.0 3.6 %collective-permute-done.2.second_ref = bf16[64,2048]{1,0:T(8,128)(2,1)S(1)} collective-permute-done((bf16[64,2048]{1,0:T(8,128)(2,1)}, bf16[64,2048]{1,0:T(8,128)(2,1)S(1)}, u32[]{:S(2)}, u32[]{:S(2)}) %collective-permute-start.2) | collective-permute-done | bytes 262176 | tf_op jit(solution)/shard_map/ppermute | solution.py:260
  13.6 0.1 shard_map.50.refs_0_
  13.7 2.7 %collective-permute-start.3 = (bf16[128,2048]{1,0:T(8,128)(2,1)S(1)}, bf16[128,2048]{1,0:T(8,128)(2,1)S(1)}, u32[]{:S(2)}, u32[]{:S(2)}) collective-permute-start(bf16[128,2048]{1,0:T(8,128)(2,1)S(1)} %shard_map.50.refs_0_), channel_id=1, source_target_pairs={{64,0},{449,1},{66,2},{451,3},{68,4},{453,5},{70,6},{455,7},{72,8}... | collective-permute-start | bytes 1572872 | tf_op jit(solution)/shard_map/ppermute | solution.py:260
  16.4 0.0 copy-start.2
  16.4 2.9 %shard_map.46 = (f32[4,128,128]{2,1,0:T(8,128)}, f32[8,128,128]{2,1,0:T(8,128)}, bf16[2,1024,128]{2,1,0:T(8,128)(2,1)}) custom-call(bf16[2048,128]{1,0:T(8,128)(2,1)} %k_ref.3, bf16[2048,128]{1,0:T(8,128)(2,1)} %v_ref.3), custom_call_target="tpu_custom_call" | custom-call | flops 1 | bytes 67108864 | tf_op jit(solution)/shard_map/pallas_call | solution.py:297
  19.3 0.0 copy-start.1
  19.3 5.8 %all-to-all-start = ((f32[4,128,128]{2,1,0:T(8,128)}), f32[4,128,128]{2,1,0:T(8,128)S(1)}, u32[]{:S(2)}, u32[]{:S(2)}) async-start(f32[4,128,128]{2,1,0:T(8,128)} %get-tuple-element.14), calls=%async_computation | async-start | bytes 524288 | tf_op jit(solution)/shard_map/all_to_all | solution.py:306
  25.1 0.0 copy-start
  25.1 0.0 collective-permute-done.3.refs_1_
  25.1 4.7 %collective-permute-start.4 = (bf16[128,2048]{1,0:T(8,128)(2,1)S(1)}, bf16[128,2048]{1,0:T(8,128)(2,1)S(1)}, u32[]{:S(2)}, u32[]{:S(2)}) collective-permute-start(bf16[128,2048]{1,0:T(8,128)(2,1)S(1)} %collective-permute-done.3.refs_1_), channel_id=1, source_target_pairs={{64,0},{449,1},{66,2},{451,3},{68,4},{453,5},{70,6},{455,7},{72,8}... | collective-permute-start | bytes 1572872 | tf_op jit(solution)/shard_map/ppermute | solution.py:260
  29.8 1.9 %collective-permute-start = (bf16[2,1024,128]{2,1,0:T(8,128)(2,1)}, bf16[2,1024,128]{2,1,0:T(8,128)(2,1)}, u32[]{:S(2)}, u32[]{:S(2)}) collective-permute-start(bf16[2,1024,128]{2,1,0:T(8,128)(2,1)} %get-tuple-element.12), channel_id=1, source_target_pairs={{0,16},{16,32},{32,48},{48,64},{64,80},{80,96},{96,112},{112,128},... | collective-permute-start | bytes 1572872 | tf_op jit(solution)/shard_map/ppermute | solution.py:309
  31.8 0.0 all-to-all-done.states_ref
  31.8 0.0 copy-start.4
  31.8 0.7 copy-done.4
  32.5 4.8 %all-to-all-start.1 = ((bf16[8,128,128]{2,1,0:T(8,128)(2,1)}), bf16[8,128,128]{2,1,0:T(8,128)(2,1)S(1)}, u32[]{:S(2)}, u32[]{:S(2)}) async-start(bf16[8,128,128]{2,1,0:T(8,128)(2,1)} %copy-done.4), calls=%async_computation.1 | async-start | bytes 524288 | tf_op jit(solution)/shard_map/all_to_all | solution.py:313
  37.3 0.0 collective-permute-done.4.refs_2_
  37.3 4.6 %collective-permute-start.5 = (bf16[128,2048]{1,0:T(8,128)(2,1)S(1)}, bf16[128,2048]{1,0:T(8,128)(2,1)}, u32[]{:S(2)}, u32[]{:S(2)}) collective-permute-start(bf16[128,2048]{1,0:T(8,128)(2,1)S(1)} %collective-permute-done.4.refs_2_), channel_id=1, source_target_pairs={{64,0},{449,1},{66,2},{451,3},{68,4},{453,5},{70,6},{455,7},{72,8}... | collective-permute-start | bytes 1572872 | tf_op jit(solution)/shard_map/ppermute | solution.py:260
  41.9 8.6 %all-to-all-done.1.totals_ref = bf16[8,128,128]{2,1,0:T(8,128)(2,1)S(1)} async-done(((bf16[8,128,128]{2,1,0:T(8,128)(2,1)}), bf16[8,128,128]{2,1,0:T(8,128)(2,1)S(1)}, u32[]{:S(2)}, u32[]{:S(2)}) %all-to-all-start.1) | async-done | bytes 262176 | tf_op jit(solution)/shard_map/all_to_all | solution.py:313
  50.4 0.0 copy-done.2
  50.4 0.0 copy-done.1
  50.4 0.0 copy-done
  50.5 0.0 copy-start.3
  50.5 1.0 copy-done.3
  51.5 2.8 %shard_map.48.inner_ref = bf16[4,256,128]{2,1,0:T(8,128)(2,1)S(1)} custom-call(bf16[2048,128]{1,0:T(8,128)(2,1)S(1)} %copy-done.2, bf16[2048,128]{1,0:T(8,128)(2,1)S(1)} %copy-done, bf16[2048,128]{1,0:T(8,128)(2,1)S(1)} %copy-done.1, f32[8,128,128]{2,1,0:T(8,128)S(1)} %copy-done.3, f32[128,128]{1,0:T(8,128)S(1)} %get-tuple-element.15.before_ref, ...), custom_call_target="tpu_custom_call" | custom-call | flops 1 | bytes 67108864 | tf_op jit(solution)/shard_map/pallas_call | solution.py:317
  54.3 0.0 collective-permute-done.rim_hbm
  54.4 5.7 %shard_map.49 = bf16[8,256,128]{2,1,0:T(8,128)(2,1)} custom-call(bf16[2048,128]{1,0:T(8,128)(2,1)S(1)} %copy-done.2, bf16[2048,128]{1,0:T(8,128)(2,1)S(1)} %copy-done, bf16[2048,128]{1,0:T(8,128)(2,1)S(1)} %copy-done.1, bf16[2,1024,128]{2,1,0:T(8,128)(2,1)} %collective-permute-done.rim_hbm, f32[8,128,128]{2,1,0:T(8,128)S(1)} %copy-done.3, ...), custom_call_target="tpu_custom_call" | custom-call | flops 1 | bytes 67108864 | tf_op jit(solution)/shard_map/pallas_call | solution.py:322
  60.1 8.3 %all-to-all-start.2 = ((bf16[8,256,128]{2,1,0:T(8,128)(2,1)}), bf16[8,256,128]{2,1,0:T(8,128)(2,1)S(1)}, u32[]{:S(2)}, u32[]{:S(2)}) async-start(bf16[8,256,128]{2,1,0:T(8,128)(2,1)} %shard_map.49), calls=%async_computation.2 | async-start | bytes 1048576 | tf_op jit(solution)/shard_map/all_to_all | solution.py:330
  68.4 1.9 %collective-permute-start.7 = (bf16[128,2048]{1,0:T(8,128)(2,1)S(1)}, bf16[128,2048]{1,0:T(8,128)(2,1)S(1)}, u32[]{:S(2)}, u32[]{:S(2)}) collective-permute-start(bf16[128,2048]{1,0:T(8,128)(2,1)S(1)} %collective-permute-done.3.refs_1_), channel_id=1, source_target_pairs={{16,0},{49,1},{18,2},{51,3},{20,4},{53,5},{22,6},{55,7},{24,8},{57... | collective-permute-start | bytes 1572872 | tf_op jit(solution)/shard_map/ppermute | solution.py:260
  70.3 4.6 %collective-permute-start.8 = (bf16[128,2048]{1,0:T(8,128)(2,1)S(1)}, bf16[128,2048]{1,0:T(8,128)(2,1)S(1)}, u32[]{:S(2)}, u32[]{:S(2)}) collective-permute-start(bf16[128,2048]{1,0:T(8,128)(2,1)S(1)} %collective-permute-done.4.refs_2_), channel_id=1, source_target_pairs={{16,0},{49,1},{18,2},{51,3},{20,4},{53,5},{22,6},{55,7},{24,8},{57... | collective-permute-start | bytes 1572872 | tf_op jit(solution)/shard_map/ppermute | solution.py:260
  74.9 0.0 collective-permute-done.5.refs_3_
  74.9 1.9 %collective-permute-start.6 = (bf16[128,2048]{1,0:T(8,128)(2,1)}, bf16[128,2048]{1,0:T(8,128)(2,1)}, u32[]{:S(2)}, u32[]{:S(2)}) collective-permute-start(bf16[128,2048]{1,0:T(8,128)(2,1)} %collective-permute-done.5.refs_3_), channel_id=1, source_target_pairs={{64,0},{449,1},{66,2},{451,3},{68,4},{453,5},{70,6},{455,7},{72,8}... | collective-permute-start | bytes 1572872 | tf_op jit(solution)/shard_map/ppermute | solution.py:260
  76.8 1.9 %collective-permute-start.9 = (bf16[128,2048]{1,0:T(8,128)(2,1)}, bf16[128,2048]{1,0:T(8,128)(2,1)}, u32[]{:S(2)}, u32[]{:S(2)}) collective-permute-start(bf16[128,2048]{1,0:T(8,128)(2,1)} %collective-permute-done.5.refs_3_), channel_id=1, source_target_pairs={{16,0},{49,1},{18,2},{51,3},{20,4},{53,5},{22,6},{55,7},{24,8},{57... | collective-permute-start | bytes 1572872 | tf_op jit(solution)/shard_map/ppermute | solution.py:260
  78.8 0.8 collective-permute-done.7.refs_5_
  79.5 1.1 %all-to-all-done.2.mixed_ref = bf16[8,256,128]{2,1,0:T(8,128)(2,1)S(1)} async-done(((bf16[8,256,128]{2,1,0:T(8,128)(2,1)}), bf16[8,256,128]{2,1,0:T(8,128)(2,1)S(1)}, u32[]{:S(2)}, u32[]{:S(2)}) %all-to-all-start.2) | async-done | bytes 524320 | tf_op jit(solution)/shard_map/all_to_all | solution.py:330
  80.6 4.5 %collective-permute-done.8.refs_6_ = bf16[128,2048]{1,0:T(8,128)(2,1)S(1)} collective-permute-done((bf16[128,2048]{1,0:T(8,128)(2,1)S(1)}, bf16[128,2048]{1,0:T(8,128)(2,1)S(1)}, u32[]{:S(2)}, u32[]{:S(2)}) %collective-permute-start.8) | collective-permute-done | bytes 524320 | tf_op jit(solution)/shard_map/ppermute | solution.py:260
  85.1 0.2 collective-permute-done.6.refs_4_
  85.3 5.8 %collective-permute-done.9.refs_7_ = bf16[128,2048]{1,0:T(8,128)(2,1)} collective-permute-done((bf16[128,2048]{1,0:T(8,128)(2,1)}, bf16[128,2048]{1,0:T(8,128)(2,1)}, u32[]{:S(2)}, u32[]{:S(2)}) %collective-permute-start.9) | collective-permute-done | bytes 524320 | tf_op jit(solution)/shard_map/ppermute | solution.py:260
  91.2 2.6 %shard_map.51 = (bf16[128,2048]{1,0:T(8,128)(2,1)S(1)}, f32[128,2048]{1,0:T(8,128)S(1)}) custom-call(bf16[8,256,128]{2,1,0:T(8,128)(2,1)S(1)} %all-to-all-done.2.mixed_ref, bf16[128,2048]{1,0:T(8,128)(2,1)S(1)} %shard_map.50.refs_0_, bf16[128,2048]{1,0:T(8,128)(2,1)S(1)} %collective-permute-done.3.refs_1_, ...), custom_call_target="tpu_custom_call" | custom-call | flops 1 | bytes 67108864 | tf_op jit(solution)/shard_map/pallas_call | solution.py:333
  93.8 9.1 %collective-permute-start.10 = (bf16[128,2048]{1,0:T(8,128)(2,1)S(1)}, bf16[128,2048]{1,0:T(8,128)(2,1)S(1)}, u32[]{:S(2)}, u32[]{:S(2)}) collective-permute-start(bf16[128,2048]{1,0:T(8,128)(2,1)S(1)} %get-tuple-element.18), channel_id=1, source_target_pairs={{0,1},{1,0},{2,3},{3,2},{4,5},{5,4},{6,7},{7,6},{8,9},{9,8},{10,11... | collective-permute-start | bytes 1572872 | tf_op jit(solution)/shard_map/ppermute | solution.py:337
  102.9 1.5 %collective-permute-done.10.taken_ref = bf16[128,2048]{1,0:T(8,128)(2,1)S(1)} collective-permute-done((bf16[128,2048]{1,0:T(8,128)(2,1)S(1)}, bf16[128,2048]{1,0:T(8,128)(2,1)S(1)}, u32[]{:S(2)}, u32[]{:S(2)}) %collective-permute-start.10) | collective-permute-done | bytes 524320 | tf_op jit(solution)/shard_map/ppermute | solution.py:337
  104.4 0.9 shard_map.52
  (1 shorter events, 0.0 us)
Async XLA Ops:
  0.0 10.0 %collective-permute-start.1 = (bf16[64,2048]{1,0:T(8,128)(2,1)}, bf16[64,2048]{1,0:T(8,128)(2,1)S(1)}, u32[]{:S(2)}, u32[]{:S(2)}) collective-permute-start(bf16[64,2048]{1,0:T(8,128)(2,1)} %param.7), channel_id=1, source_target_pairs={{1,0},{33,1},{3,2},{35,3},{5,4},{37,5},{7,6},{39,7},{9,8},{41,9},{... | collective-permute-start | bytes 786440 | tf_op jit(solution)/shard_map/ppermute | solution.py:260
  3.0 10.6 %collective-permute-start.2 = (bf16[64,2048]{1,0:T(8,128)(2,1)}, bf16[64,2048]{1,0:T(8,128)(2,1)S(1)}, u32[]{:S(2)}, u32[]{:S(2)}) collective-permute-start(bf16[64,2048]{1,0:T(8,128)(2,1)} %param.7), channel_id=1, source_target_pairs={{17,0},{49,1},{19,2},{51,3},{21,4},{53,5},{23,6},{55,7},{25,8},{57... | collective-permute-start | bytes 786440 | tf_op jit(solution)/shard_map/ppermute | solution.py:260
  13.7 11.4 %collective-permute-start.3 = (bf16[128,2048]{1,0:T(8,128)(2,1)S(1)}, bf16[128,2048]{1,0:T(8,128)(2,1)S(1)}, u32[]{:S(2)}, u32[]{:S(2)}) collective-permute-start(bf16[128,2048]{1,0:T(8,128)(2,1)S(1)} %shard_map.50.refs_0_), channel_id=1, source_target_pairs={{64,0},{449,1},{66,2},{451,3},{68,4},{453,5},{70,6},{455,7},{72,8}... | collective-permute-start | bytes 1572872 | tf_op jit(solution)/shard_map/ppermute | solution.py:260
  16.4 34.0 %copy-start.2 = (bf16[2048,128]{1,0:T(8,128)(2,1)S(1)}, bf16[2048,128]{1,0:T(8,128)(2,1)}, u32[]{:S(2)}) copy-start(bf16[2048,128]{1,0:T(8,128)(2,1)} %q_ref.3) | copy-start | bytes 1572868
  19.3 31.1 %copy-start.1 = (bf16[2048,128]{1,0:T(8,128)(2,1)S(1)}, bf16[2048,128]{1,0:T(8,128)(2,1)}, u32[]{:S(2)}) copy-start(bf16[2048,128]{1,0:T(8,128)(2,1)} %v_ref.3) | copy-start | bytes 1572868
  19.3 12.4 %all-to-all-start = ((f32[4,128,128]{2,1,0:T(8,128)}), f32[4,128,128]{2,1,0:T(8,128)S(1)}, u32[]{:S(2)}, u32[]{:S(2)}) async-start(f32[4,128,128]{2,1,0:T(8,128)} %get-tuple-element.14), calls=%async_computation | async-start | bytes 524288 | tf_op jit(solution)/shard_map/all_to_all | solution.py:306
  25.1 25.3 %copy-start = (bf16[2048,128]{1,0:T(8,128)(2,1)S(1)}, bf16[2048,128]{1,0:T(8,128)(2,1)}, u32[]{:S(2)}) copy-start(bf16[2048,128]{1,0:T(8,128)(2,1)} %k_ref.3) | copy-start | bytes 1572868
  25.1 12.2 %collective-permute-start.4 = (bf16[128,2048]{1,0:T(8,128)(2,1)S(1)}, bf16[128,2048]{1,0:T(8,128)(2,1)S(1)}, u32[]{:S(2)}, u32[]{:S(2)}) collective-permute-start(bf16[128,2048]{1,0:T(8,128)(2,1)S(1)} %collective-permute-done.3.refs_1_), channel_id=1, source_target_pairs={{64,0},{449,1},{66,2},{451,3},{68,4},{453,5},{70,6},{455,7},{72,8}... | collective-permute-start | bytes 1572872 | tf_op jit(solution)/shard_map/ppermute | solution.py:260
  29.8 24.5 %collective-permute-start = (bf16[2,1024,128]{2,1,0:T(8,128)(2,1)}, bf16[2,1024,128]{2,1,0:T(8,128)(2,1)}, u32[]{:S(2)}, u32[]{:S(2)}) collective-permute-start(bf16[2,1024,128]{2,1,0:T(8,128)(2,1)} %get-tuple-element.12), channel_id=1, source_target_pairs={{0,16},{16,32},{32,48},{48,64},{64,80},{80,96},{96,112},{112,128},... | collective-permute-start | bytes 1572872 | tf_op jit(solution)/shard_map/ppermute | solution.py:309
  31.8 0.7 copy-start.4
  32.5 17.9 %all-to-all-start.1 = ((bf16[8,128,128]{2,1,0:T(8,128)(2,1)}), bf16[8,128,128]{2,1,0:T(8,128)(2,1)S(1)}, u32[]{:S(2)}, u32[]{:S(2)}) async-start(bf16[8,128,128]{2,1,0:T(8,128)(2,1)} %copy-done.4), calls=%async_computation.1 | async-start | bytes 524288 | tf_op jit(solution)/shard_map/all_to_all | solution.py:313
  37.3 37.6 %collective-permute-start.5 = (bf16[128,2048]{1,0:T(8,128)(2,1)S(1)}, bf16[128,2048]{1,0:T(8,128)(2,1)}, u32[]{:S(2)}, u32[]{:S(2)}) collective-permute-start(bf16[128,2048]{1,0:T(8,128)(2,1)S(1)} %collective-permute-done.4.refs_2_), channel_id=1, source_target_pairs={{64,0},{449,1},{66,2},{451,3},{68,4},{453,5},{70,6},{455,7},{72,8}... | collective-permute-start | bytes 1572872 | tf_op jit(solution)/shard_map/ppermute | solution.py:260
  50.5 1.0 copy-start.3
  60.1 20.6 %all-to-all-start.2 = ((bf16[8,256,128]{2,1,0:T(8,128)(2,1)}), bf16[8,256,128]{2,1,0:T(8,128)(2,1)S(1)}, u32[]{:S(2)}, u32[]{:S(2)}) async-start(bf16[8,256,128]{2,1,0:T(8,128)(2,1)} %shard_map.49), calls=%async_computation.2 | async-start | bytes 1048576 | tf_op jit(solution)/shard_map/all_to_all | solution.py:330
  68.4 11.1 %collective-permute-start.7 = (bf16[128,2048]{1,0:T(8,128)(2,1)S(1)}, bf16[128,2048]{1,0:T(8,128)(2,1)S(1)}, u32[]{:S(2)}, u32[]{:S(2)}) collective-permute-start(bf16[128,2048]{1,0:T(8,128)(2,1)S(1)} %collective-permute-done.3.refs_1_), channel_id=1, source_target_pairs={{16,0},{49,1},{18,2},{51,3},{20,4},{53,5},{22,6},{55,7},{24,8},{57... | collective-permute-start | bytes 1572872 | tf_op jit(solution)/shard_map/ppermute | solution.py:260
  70.3 14.8 %collective-permute-start.8 = (bf16[128,2048]{1,0:T(8,128)(2,1)S(1)}, bf16[128,2048]{1,0:T(8,128)(2,1)S(1)}, u32[]{:S(2)}, u32[]{:S(2)}) collective-permute-start(bf16[128,2048]{1,0:T(8,128)(2,1)S(1)} %collective-permute-done.4.refs_2_), channel_id=1, source_target_pairs={{16,0},{49,1},{18,2},{51,3},{20,4},{53,5},{22,6},{55,7},{24,8},{57... | collective-permute-start | bytes 1572872 | tf_op jit(solution)/shard_map/ppermute | solution.py:260
  74.9 10.4 %collective-permute-start.6 = (bf16[128,2048]{1,0:T(8,128)(2,1)}, bf16[128,2048]{1,0:T(8,128)(2,1)}, u32[]{:S(2)}, u32[]{:S(2)}) collective-permute-start(bf16[128,2048]{1,0:T(8,128)(2,1)} %collective-permute-done.5.refs_3_), channel_id=1, source_target_pairs={{64,0},{449,1},{66,2},{451,3},{68,4},{453,5},{70,6},{455,7},{72,8}... | collective-permute-start | bytes 1572872 | tf_op jit(solution)/shard_map/ppermute | solution.py:260
  76.8 14.3 %collective-permute-start.9 = (bf16[128,2048]{1,0:T(8,128)(2,1)}, bf16[128,2048]{1,0:T(8,128)(2,1)}, u32[]{:S(2)}, u32[]{:S(2)}) collective-permute-start(bf16[128,2048]{1,0:T(8,128)(2,1)} %collective-permute-done.5.refs_3_), channel_id=1, source_target_pairs={{16,0},{49,1},{18,2},{51,3},{20,4},{53,5},{22,6},{55,7},{24,8},{57... | collective-permute-start | bytes 1572872 | tf_op jit(solution)/shard_map/ppermute | solution.py:260
  93.8 10.7 %collective-permute-start.10 = (bf16[128,2048]{1,0:T(8,128)(2,1)S(1)}, bf16[128,2048]{1,0:T(8,128)(2,1)S(1)}, u32[]{:S(2)}, u32[]{:S(2)}) collective-permute-start(bf16[128,2048]{1,0:T(8,128)(2,1)S(1)} %get-tuple-element.18), channel_id=1, source_target_pairs={{0,1},{1,0},{2,3},{3,2},{4,5},{5,4},{6,7},{7,6},{8,9},{9,8},{10,11... | collective-permute-start | bytes 1572872 | tf_op jit(solution)/shard_map/ppermute | solution.py:337

commit v4 on v3

--- a/solution.py
+++ b/solution.py
@@ -156,7 +156,9 @@
     return (soft + normalize(linear) * 0.5).astype(bf16)
 
 
-def inner_kernel(q_ref, k_ref, v_ref, within_ref, before_ref, totals_ref, out_ref):
+def inner_kernel(q_ref, k_ref, v_ref, rim_hbm, within_ref, before_ref, totals_ref, out_ref, rim_ref, sem):
+    fetch = pltpu.make_async_copy(rim_hbm, rim_ref, sem)
+    fetch.start()
     upper = upper_mask()
     prior = prior_state(before_ref, totals_ref)
     near = W // BLOCK
@@ -166,17 +168,13 @@
         values = [rows_of(v_ref, b - near + j) for j in range(near + 1)]
         soft, linear = block_rows(q, keys, values, None, upper)
         out_ref[b - near] = mix(q, soft, linear, prior + within_ref[b])
+    fetch.wait()
 
 
 def outer_kernel(
-    q_ref, k_ref, v_ref, rim_hbm, within_ref, before_ref, totals_ref, inner_ref, out_hbm, rim_ref, out_ref, sems, out_sems
+    q_ref, k_ref, v_ref, rim_ref, within_ref, before_ref, totals_ref, inner_ref, out_hbm, out_ref, out_sems
 ):
     near = W // BLOCK
-    copies = []
-    for j in reversed(range(near)):
-        part = pl.ds(j * BLOCK, BLOCK)
-        copies.append(pltpu.make_async_copy(rim_hbm.at[:, part], rim_ref.at[:, part], sems.at[j]))
-        copies[-1].start()
     sent = [pltpu.make_async_copy(inner_ref, out_hbm.at[pl.ds(near, near)], out_sems.at[near])]
     sent[0].start()
     upper = upper_mask()
@@ -184,7 +182,6 @@
     first = jnp.logical_and(lax.axis_index("y") == 0, lax.axis_index("x") == 0)
     hidden = jnp.where(first, far_below, 0.0).astype(f32)
     for b in reversed(range(near)):
-        copies[near - 1 - b].wait()
         keys, values, bias = [], [], []
         for j in range(near + 1):
             at = b + j
@@ -307,23 +304,22 @@
     unit = call(unit_kernel, shape((2 * w_out.shape[0], wide), bf16), [VMEM] * 2)(chunk_b, chunk_a)
     y1 = moved(unit, along)
     rim = lax.ppermute(rim, ("y", "x"), [(i, i + 1) for i in range(NY * NX - 1)])
-    before, totals = call(
-        row_kernel, (shape((HD, HD), f32), shape((NY, HD, HD), bf16)), [VMEM]
-    )(row_states)
+    before, totals = call(row_kernel, (shape((HD, HD), f32), shape((NY, HD, HD), bf16)), [VMEM])(row_states)
     totals = lax.all_to_all(totals, "y", 0, 0, tiled=True)
     y2 = moved(y1, along)
     e1 = moved(y1, across)
     shared = (within, before, totals)
-    inner = call(inner_kernel, shape((NZ // 2, rows // NZ, HD), bf16), [VMEM] * 6)(
-        queries, key_vectors, value_vectors, *shared
+    inner, rim = call(
+        inner_kernel, (shape((NZ // 2, rows // NZ, HD), bf16), shape(rim.shape, bf16)),
+        [VMEM] * 3 + [ANY] + [VMEM] * 3, scratch=[pltpu.SemaphoreType.DMA],
+    )(
+        queries, key_vectors, value_vectors, rim, *shared
     )
     y3 = moved(y2, along)
     e2 = moved(y2, across)
     mixed = call(
-        outer_kernel, shape((NZ, rows // NZ, HD), bf16), [VMEM] * 3 + [ANY] + [VMEM] * 4,
-        out_specs=ANY,
-        scratch=[pltpu.VMEM((2, W, HD), bf16), pltpu.VMEM((W // BLOCK, BLOCK, HD), bf16)]
-        + [pltpu.SemaphoreType.DMA((W // BLOCK,)), pltpu.SemaphoreType.DMA((1 + W // BLOCK,))],
+        outer_kernel, shape((NZ, rows // NZ, HD), bf16), [VMEM] * 8, out_specs=ANY,
+        scratch=[pltpu.VMEM((W // BLOCK, BLOCK, HD), bf16), pltpu.SemaphoreType.DMA((1 + W // BLOCK,))],
     )(
         queries, key_vectors, value_vectors, rim, *shared, inner
     )

time: 106 us -> 104 us (0.981)
  Pallas kernels: 15 us -> 13.4 us
    ppermute x1, waiting for transfers between devices: 0.01 us -> 3.47 us  [layer(): lax.ppermute(rim, ('y', 'x'), [(i, i + 1) for i in range(NY * NX - 1)])]
    all_to_all x1, waiting for transfers between devices: 8.56 us -> 5.09 us  [layer(): totals = lax.all_to_all(totals, 'y', 0, 0, tiled=True)]
    pallas_call x2, Pallas kernels: 8.55 us -> 6.87 us  [the longest x1 4.01 us: layer(): call(outer_kernel, shape((NZ, rows // NZ, HD), bf16), [VMEM] * 8, out_spe...]
  transfers between devices with their start and end apart: 14 -> 14, of which waited for: 8 -> 9; matrix products, arithmetic and copies ran while one was open for 0% -> 0% of each run, Pallas kernels for 11% -> 9%
where the time goes in v4:
time: 104 us
  starting transfers between devices  62.2 us (60%)
  waiting for transfers between devices  26.1 us (25%)
  Pallas kernels  13.4 us (13%)
  local copies, waits for them, and re-layouts  1.75 us (2%)
    ppermute x9, starting transfers between devices, moved(): return lax.ppermute(shard, AXES, pairs)  32.3 us
    ppermute x9, waiting for transfers between devices, moved(): return lax.ppermute(shard, AXES, pairs)  14.9 us
    ppermute x1, starting transfers between devices, layer(): taken = lax.ppermute(given, 'c', [(0, 1), (1, 0)])  9.14 us
    all_to_all x1, starting transfers between devices, layer(): mixed = lax.all_to_all(mixed, 'z', 0, 0, tiled=True)  8.33 us
    all_to_all x1, starting transfers between devices, layer(): row_states = lax.all_to_all(states, 'x', 0, 0, tiled=True)  5.78 us
    all_to_all x1, waiting for transfers between devices, layer(): totals = lax.all_to_all(totals, 'y', 0, 0, tiled=True)  5.09 us
    all_to_all x1, starting transfers between devices, layer(): totals = lax.all_to_all(totals, 'y', 0, 0, tiled=True)  4.78 us
    pallas_call x1, Pallas kernels, layer(): call(outer_kernel, shape((NZ, rows // NZ, HD), bf16), [VMEM] * 8, out_spe...  4.01 us
  transfers between devices with their start and end apart: 14, of which 9 were waited for; matrix products, arithmetic and copies ran while one was open for 0% of the time, Pallas kernels for 9%

profile of v4, /device:TPU:7, one launch (start us, length us, event | category | flops | bytes accessed | tf_op | source)
XLA Modules:
  0.0 103.6 jit_solution(10218206744417336257)
XLA Ops:
  0.0 3.0 %collective-permute-start.1 = (bf16[64,2048]{1,0:T(8,128)(2,1)}, bf16[64,2048]{1,0:T(8,128)(2,1)S(1)}, u32[]{:S(2)}, u32[]{:S(2)}) collective-permute-start(bf16[64,2048]{1,0:T(8,128)(2,1)} %param.7), channel_id=1, source_target_pairs={{1,0},{33,1},{3,2},{35,3},{5,4},{37,5},{7,6},{39,7},{9,8},{41,9},{... | collective-permute-start | bytes 786440 | tf_op jit(solution)/shard_map/ppermute | solution.py:257
  3.0 7.0 %collective-permute-start.2 = (bf16[64,2048]{1,0:T(8,128)(2,1)}, bf16[64,2048]{1,0:T(8,128)(2,1)S(1)}, u32[]{:S(2)}, u32[]{:S(2)}) collective-permute-start(bf16[64,2048]{1,0:T(8,128)(2,1)} %param.7), channel_id=1, source_target_pairs={{17,0},{49,1},{19,2},{51,3},{21,4},{53,5},{23,6},{55,7},{25,8},{57... | collective-permute-start | bytes 786440 | tf_op jit(solution)/shard_map/ppermute | solution.py:257
  10.0 0.0 collective-permute-done.1.first_ref
  10.0 3.6 %collective-permute-done.2.second_ref = bf16[64,2048]{1,0:T(8,128)(2,1)S(1)} collective-permute-done((bf16[64,2048]{1,0:T(8,128)(2,1)}, bf16[64,2048]{1,0:T(8,128)(2,1)S(1)}, u32[]{:S(2)}, u32[]{:S(2)}) %collective-permute-start.2) | collective-permute-done | bytes 262176 | tf_op jit(solution)/shard_map/ppermute | solution.py:257
  13.6 0.1 shard_map.50.refs_0_
  13.7 2.7 %collective-permute-start.3 = (bf16[128,2048]{1,0:T(8,128)(2,1)S(1)}, bf16[128,2048]{1,0:T(8,128)(2,1)S(1)}, u32[]{:S(2)}, u32[]{:S(2)}) collective-permute-start(bf16[128,2048]{1,0:T(8,128)(2,1)S(1)} %shard_map.50.refs_0_), channel_id=1, source_target_pairs={{64,0},{449,1},{66,2},{451,3},{68,4},{453,5},{70,6},{455,7},{72,8}... | collective-permute-start | bytes 1572872 | tf_op jit(solution)/shard_map/ppermute | solution.py:257
  16.4 0.0 copy-start.2
  16.4 2.9 %shard_map.46 = (f32[4,128,128]{2,1,0:T(8,128)}, f32[8,128,128]{2,1,0:T(8,128)}, bf16[2,1024,128]{2,1,0:T(8,128)(2,1)}) custom-call(bf16[2048,128]{1,0:T(8,128)(2,1)} %k_ref.3, bf16[2048,128]{1,0:T(8,128)(2,1)} %v_ref.3), custom_call_target="tpu_custom_call" | custom-call | flops 1 | bytes 67108864 | tf_op jit(solution)/shard_map/pallas_call | solution.py:294
  19.3 0.0 copy-start.1
  19.3 5.8 %all-to-all-start = ((f32[4,128,128]{2,1,0:T(8,128)}), f32[4,128,128]{2,1,0:T(8,128)S(1)}, u32[]{:S(2)}, u32[]{:S(2)}) async-start(f32[4,128,128]{2,1,0:T(8,128)} %get-tuple-element.16), calls=%async_computation | async-start | bytes 524288 | tf_op jit(solution)/shard_map/all_to_all | solution.py:303
  25.1 0.0 copy-start
  25.1 0.0 collective-permute-done.3.refs_1_
  25.1 4.7 %collective-permute-start.4 = (bf16[128,2048]{1,0:T(8,128)(2,1)S(1)}, bf16[128,2048]{1,0:T(8,128)(2,1)S(1)}, u32[]{:S(2)}, u32[]{:S(2)}) collective-permute-start(bf16[128,2048]{1,0:T(8,128)(2,1)S(1)} %collective-permute-done.3.refs_1_), channel_id=1, source_target_pairs={{64,0},{449,1},{66,2},{451,3},{68,4},{453,5},{70,6},{455,7},{72,8}... | collective-permute-start | bytes 1572872 | tf_op jit(solution)/shard_map/ppermute | solution.py:257
  29.8 1.9 %collective-permute-start = (bf16[2,1024,128]{2,1,0:T(8,128)(2,1)}, bf16[2,1024,128]{2,1,0:T(8,128)(2,1)}, u32[]{:S(2)}, u32[]{:S(2)}) collective-permute-start(bf16[2,1024,128]{2,1,0:T(8,128)(2,1)} %get-tuple-element.14), channel_id=1, source_target_pairs={{0,16},{16,32},{32,48},{48,64},{64,80},{80,96},{96,112},{112,128},... | collective-permute-start | bytes 1572872 | tf_op jit(solution)/shard_map/ppermute | solution.py:306
  31.8 0.0 all-to-all-done.states_ref
  31.8 0.0 copy-start.4
  31.8 0.7 copy-done.4
  32.5 4.8 %all-to-all-start.1 = ((bf16[8,128,128]{2,1,0:T(8,128)(2,1)}), bf16[8,128,128]{2,1,0:T(8,128)(2,1)S(1)}, u32[]{:S(2)}, u32[]{:S(2)}) async-start(bf16[8,128,128]{2,1,0:T(8,128)(2,1)} %copy-done.4), calls=%async_computation.1 | async-start | bytes 524288 | tf_op jit(solution)/shard_map/all_to_all | solution.py:308
  37.3 0.0 collective-permute-done.4.refs_2_
  37.3 4.6 %collective-permute-start.5 = (bf16[128,2048]{1,0:T(8,128)(2,1)S(1)}, bf16[128,2048]{1,0:T(8,128)(2,1)}, u32[]{:S(2)}, u32[]{:S(2)}) collective-permute-start(bf16[128,2048]{1,0:T(8,128)(2,1)S(1)} %collective-permute-done.4.refs_2_), channel_id=1, source_target_pairs={{64,0},{449,1},{66,2},{451,3},{68,4},{453,5},{70,6},{455,7},{72,8}... | collective-permute-start | bytes 1572872 | tf_op jit(solution)/shard_map/ppermute | solution.py:257
  41.9 3.5 %collective-permute-done.rim_hbm = bf16[2,1024,128]{2,1,0:T(8,128)(2,1)} collective-permute-done((bf16[2,1024,128]{2,1,0:T(8,128)(2,1)}, bf16[2,1024,128]{2,1,0:T(8,128)(2,1)}, u32[]{:S(2)}, u32[]{:S(2)}) %collective-permute-start) | collective-permute-done | bytes 524320 | tf_op jit(solution)/shard_map/ppermute | solution.py:306
  45.3 5.1 %all-to-all-done.1.totals_ref = bf16[8,128,128]{2,1,0:T(8,128)(2,1)S(1)} async-done(((bf16[8,128,128]{2,1,0:T(8,128)(2,1)}), bf16[8,128,128]{2,1,0:T(8,128)(2,1)S(1)}, u32[]{:S(2)}, u32[]{:S(2)}) %all-to-all-start.1) | async-done | bytes 262176 | tf_op jit(solution)/shard_map/all_to_all | solution.py:308
  50.4 0.0 copy-done.2
  50.4 0.0 copy-done.1
  50.4 0.0 copy-done
  50.5 0.0 copy-start.3
  50.5 1.0 copy-done.3
  51.5 2.9 %shard_map.48 = (bf16[4,256,128]{2,1,0:T(8,128)(2,1)S(1)}, bf16[2,1024,128]{2,1,0:T(8,128)(2,1)S(1)}) custom-call(bf16[2048,128]{1,0:T(8,128)(2,1)S(1)} %copy-done.2, bf16[2048,128]{1,0:T(8,128)(2,1)S(1)} %copy-done, bf16[2048,128]{1,0:T(8,128)(2,1)S(1)} %copy-done.1, bf16[2,1024,128]{2,1,0:T(8,128)(2,1)} %collective-permute-done.rim_hbm, ...), custom_call_target="tpu_custom_call" | custom-call | flops 1 | bytes 67108864 | tf_op jit(solution)/shard_map/pallas_call | solution.py:312
  54.4 4.0 %shard_map.49 = bf16[8,256,128]{2,1,0:T(8,128)(2,1)} custom-call(bf16[2048,128]{1,0:T(8,128)(2,1)S(1)} %copy-done.2, bf16[2048,128]{1,0:T(8,128)(2,1)S(1)} %copy-done, bf16[2048,128]{1,0:T(8,128)(2,1)S(1)} %copy-done.1, bf16[2,1024,128]{2,1,0:T(8,128)(2,1)S(1)} %get-tuple-element.19.rim_ref, f32[8,128,128]{2,1,0:T(8,128)S(1)} %copy-done.3, ...), custom_call_target="tpu_custom_call" | custom-call | flops 1 | bytes 67108864 | tf_op jit(solution)/shard_map/pallas_call | solution.py:320
  58.4 8.3 %all-to-all-start.2 = ((bf16[8,256,128]{2,1,0:T(8,128)(2,1)}), bf16[8,256,128]{2,1,0:T(8,128)(2,1)S(1)}, u32[]{:S(2)}, u32[]{:S(2)}) async-start(bf16[8,256,128]{2,1,0:T(8,128)(2,1)} %shard_map.49), calls=%async_computation.2 | async-start | bytes 1048576 | tf_op jit(solution)/shard_map/all_to_all | solution.py:326
  66.7 1.9 %collective-permute-start.7 = (bf16[128,2048]{1,0:T(8,128)(2,1)S(1)}, bf16[128,2048]{1,0:T(8,128)(2,1)S(1)}, u32[]{:S(2)}, u32[]{:S(2)}) collective-permute-start(bf16[128,2048]{1,0:T(8,128)(2,1)S(1)} %collective-permute-done.3.refs_1_), channel_id=1, source_target_pairs={{16,0},{49,1},{18,2},{51,3},{20,4},{53,5},{22,6},{55,7},{24,8},{57... | collective-permute-start | bytes 1572872 | tf_op jit(solution)/shard_map/ppermute | solution.py:257
  68.6 4.6 %collective-permute-start.8 = (bf16[128,2048]{1,0:T(8,128)(2,1)S(1)}, bf16[128,2048]{1,0:T(8,128)(2,1)S(1)}, u32[]{:S(2)}, u32[]{:S(2)}) collective-permute-start(bf16[128,2048]{1,0:T(8,128)(2,1)S(1)} %collective-permute-done.4.refs_2_), channel_id=1, source_target_pairs={{16,0},{49,1},{18,2},{51,3},{20,4},{53,5},{22,6},{55,7},{24,8},{57... | collective-permute-start | bytes 1572872 | tf_op jit(solution)/shard_map/ppermute | solution.py:257
  73.2 0.0 collective-permute-done.5.refs_3_
  73.2 1.9 %collective-permute-start.6 = (bf16[128,2048]{1,0:T(8,128)(2,1)}, bf16[128,2048]{1,0:T(8,128)(2,1)}, u32[]{:S(2)}, u32[]{:S(2)}) collective-permute-start(bf16[128,2048]{1,0:T(8,128)(2,1)} %collective-permute-done.5.refs_3_), channel_id=1, source_target_pairs={{64,0},{449,1},{66,2},{451,3},{68,4},{453,5},{70,6},{455,7},{72,8}... | collective-permute-start | bytes 1572872 | tf_op jit(solution)/shard_map/ppermute | solution.py:257
  75.1 1.9 %collective-permute-start.9 = (bf16[128,2048]{1,0:T(8,128)(2,1)}, bf16[128,2048]{1,0:T(8,128)(2,1)}, u32[]{:S(2)}, u32[]{:S(2)}) collective-permute-start(bf16[128,2048]{1,0:T(8,128)(2,1)} %collective-permute-done.5.refs_3_), channel_id=1, source_target_pairs={{16,0},{49,1},{18,2},{51,3},{20,4},{53,5},{22,6},{55,7},{24,8},{57... | collective-permute-start | bytes 1572872 | tf_op jit(solution)/shard_map/ppermute | solution.py:257
  77.1 0.8 collective-permute-done.7.refs_5_
  77.8 1.1 %all-to-all-done.2.mixed_ref = bf16[8,256,128]{2,1,0:T(8,128)(2,1)S(1)} async-done(((bf16[8,256,128]{2,1,0:T(8,128)(2,1)}), bf16[8,256,128]{2,1,0:T(8,128)(2,1)S(1)}, u32[]{:S(2)}, u32[]{:S(2)}) %all-to-all-start.2) | async-done | bytes 524320 | tf_op jit(solution)/shard_map/all_to_all | solution.py:326
  79.0 4.5 %collective-permute-done.8.refs_6_ = bf16[128,2048]{1,0:T(8,128)(2,1)S(1)} collective-permute-done((bf16[128,2048]{1,0:T(8,128)(2,1)S(1)}, bf16[128,2048]{1,0:T(8,128)(2,1)S(1)}, u32[]{:S(2)}, u32[]{:S(2)}) %collective-permute-start.8) | collective-permute-done | bytes 524320 | tf_op jit(solution)/shard_map/ppermute | solution.py:257
  83.5 0.2 collective-permute-done.6.refs_4_
  83.6 5.8 %collective-permute-done.9.refs_7_ = bf16[128,2048]{1,0:T(8,128)(2,1)} collective-permute-done((bf16[128,2048]{1,0:T(8,128)(2,1)}, bf16[128,2048]{1,0:T(8,128)(2,1)}, u32[]{:S(2)}, u32[]{:S(2)}) %collective-permute-start.9) | collective-permute-done | bytes 524320 | tf_op jit(solution)/shard_map/ppermute | solution.py:257
  89.5 2.6 %shard_map.51 = (bf16[128,2048]{1,0:T(8,128)(2,1)S(1)}, f32[128,2048]{1,0:T(8,128)S(1)}) custom-call(bf16[8,256,128]{2,1,0:T(8,128)(2,1)S(1)} %all-to-all-done.2.mixed_ref, bf16[128,2048]{1,0:T(8,128)(2,1)S(1)} %shard_map.50.refs_0_, bf16[128,2048]{1,0:T(8,128)(2,1)S(1)} %collective-permute-done.3.refs_1_, ...), custom_call_target="tpu_custom_call" | custom-call | flops 1 | bytes 67108864 | tf_op jit(solution)/shard_map/pallas_call | solution.py:329
  92.1 9.1 %collective-permute-start.10 = (bf16[128,2048]{1,0:T(8,128)(2,1)S(1)}, bf16[128,2048]{1,0:T(8,128)(2,1)S(1)}, u32[]{:S(2)}, u32[]{:S(2)}) collective-permute-start(bf16[128,2048]{1,0:T(8,128)(2,1)S(1)} %get-tuple-element.22), channel_id=1, source_target_pairs={{0,1},{1,0},{2,3},{3,2},{4,5},{5,4},{6,7},{7,6},{8,9},{9,8},{10,11... | collective-permute-start | bytes 1572872 | tf_op jit(solution)/shard_map/ppermute | solution.py:333
  101.2 1.5 %collective-permute-done.10.taken_ref = bf16[128,2048]{1,0:T(8,128)(2,1)S(1)} collective-permute-done((bf16[128,2048]{1,0:T(8,128)(2,1)S(1)}, bf16[128,2048]{1,0:T(8,128)(2,1)S(1)}, u32[]{:S(2)}, u32[]{:S(2)}) %collective-permute-start.10) | collective-permute-done | bytes 524320 | tf_op jit(solution)/shard_map/ppermute | solution.py:333
  102.7 0.9 shard_map.52
  (1 shorter events, 0.0 us)
Async XLA Ops:
  0.0 10.0 %collective-permute-start.1 = (bf16[64,2048]{1,0:T(8,128)(2,1)}, bf16[64,2048]{1,0:T(8,128)(2,1)S(1)}, u32[]{:S(2)}, u32[]{:S(2)}) collective-permute-start(bf16[64,2048]{1,0:T(8,128)(2,1)} %param.7), channel_id=1, source_target_pairs={{1,0},{33,1},{3,2},{35,3},{5,4},{37,5},{7,6},{39,7},{9,8},{41,9},{... | collective-permute-start | bytes 786440 | tf_op jit(solution)/shard_map/ppermute | solution.py:257
  3.0 10.6 %collective-permute-start.2 = (bf16[64,2048]{1,0:T(8,128)(2,1)}, bf16[64,2048]{1,0:T(8,128)(2,1)S(1)}, u32[]{:S(2)}, u32[]{:S(2)}) collective-permute-start(bf16[64,2048]{1,0:T(8,128)(2,1)} %param.7), channel_id=1, source_target_pairs={{17,0},{49,1},{19,2},{51,3},{21,4},{53,5},{23,6},{55,7},{25,8},{57... | collective-permute-start | bytes 786440 | tf_op jit(solution)/shard_map/ppermute | solution.py:257
  13.7 11.4 %collective-permute-start.3 = (bf16[128,2048]{1,0:T(8,128)(2,1)S(1)}, bf16[128,2048]{1,0:T(8,128)(2,1)S(1)}, u32[]{:S(2)}, u32[]{:S(2)}) collective-permute-start(bf16[128,2048]{1,0:T(8,128)(2,1)S(1)} %shard_map.50.refs_0_), channel_id=1, source_target_pairs={{64,0},{449,1},{66,2},{451,3},{68,4},{453,5},{70,6},{455,7},{72,8}... | collective-permute-start | bytes 1572872 | tf_op jit(solution)/shard_map/ppermute | solution.py:257
  16.4 34.0 %copy-start.2 = (bf16[2048,128]{1,0:T(8,128)(2,1)S(1)}, bf16[2048,128]{1,0:T(8,128)(2,1)}, u32[]{:S(2)}) copy-start(bf16[2048,128]{1,0:T(8,128)(2,1)} %q_ref.3) | copy-start | bytes 1572868
  19.3 31.1 %copy-start.1 = (bf16[2048,128]{1,0:T(8,128)(2,1)S(1)}, bf16[2048,128]{1,0:T(8,128)(2,1)}, u32[]{:S(2)}) copy-start(bf16[2048,128]{1,0:T(8,128)(2,1)} %v_ref.3) | copy-start | bytes 1572868
  19.3 12.4 %all-to-all-start = ((f32[4,128,128]{2,1,0:T(8,128)}), f32[4,128,128]{2,1,0:T(8,128)S(1)}, u32[]{:S(2)}, u32[]{:S(2)}) async-start(f32[4,128,128]{2,1,0:T(8,128)} %get-tuple-element.16), calls=%async_computation | async-start | bytes 524288 | tf_op jit(solution)/shard_map/all_to_all | solution.py:303
  25.1 25.3 %copy-start = (bf16[2048,128]{1,0:T(8,128)(2,1)S(1)}, bf16[2048,128]{1,0:T(8,128)(2,1)}, u32[]{:S(2)}) copy-start(bf16[2048,128]{1,0:T(8,128)(2,1)} %k_ref.3) | copy-start | bytes 1572868
  25.1 12.2 %collective-permute-start.4 = (bf16[128,2048]{1,0:T(8,128)(2,1)S(1)}, bf16[128,2048]{1,0:T(8,128)(2,1)S(1)}, u32[]{:S(2)}, u32[]{:S(2)}) collective-permute-start(bf16[128,2048]{1,0:T(8,128)(2,1)S(1)} %collective-permute-done.3.refs_1_), channel_id=1, source_target_pairs={{64,0},{449,1},{66,2},{451,3},{68,4},{453,5},{70,6},{455,7},{72,8}... | collective-permute-start | bytes 1572872 | tf_op jit(solution)/shard_map/ppermute | solution.py:257
  29.8 15.5 %collective-permute-start = (bf16[2,1024,128]{2,1,0:T(8,128)(2,1)}, bf16[2,1024,128]{2,1,0:T(8,128)(2,1)}, u32[]{:S(2)}, u32[]{:S(2)}) collective-permute-start(bf16[2,1024,128]{2,1,0:T(8,128)(2,1)} %get-tuple-element.14), channel_id=1, source_target_pairs={{0,16},{16,32},{32,48},{48,64},{64,80},{80,96},{96,112},{112,128},... | collective-permute-start | bytes 1572872 | tf_op jit(solution)/shard_map/ppermute | solution.py:306
  31.8 0.7 copy-start.4
  32.5 17.9 %all-to-all-start.1 = ((bf16[8,128,128]{2,1,0:T(8,128)(2,1)}), bf16[8,128,128]{2,1,0:T(8,128)(2,1)S(1)}, u32[]{:S(2)}, u32[]{:S(2)}) async-start(bf16[8,128,128]{2,1,0:T(8,128)(2,1)} %copy-done.4), calls=%async_computation.1 | async-start | bytes 524288 | tf_op jit(solution)/shard_map/all_to_all | solution.py:308
  37.3 35.9 %collective-permute-start.5 = (bf16[128,2048]{1,0:T(8,128)(2,1)S(1)}, bf16[128,2048]{1,0:T(8,128)(2,1)}, u32[]{:S(2)}, u32[]{:S(2)}) collective-permute-start(bf16[128,2048]{1,0:T(8,128)(2,1)S(1)} %collective-permute-done.4.refs_2_), channel_id=1, source_target_pairs={{64,0},{449,1},{66,2},{451,3},{68,4},{453,5},{70,6},{455,7},{72,8}... | collective-permute-start | bytes 1572872 | tf_op jit(solution)/shard_map/ppermute | solution.py:257
  50.5 1.0 %copy-start.3 = (f32[8,128,128]{2,1,0:T(8,128)S(1)}, f32[8,128,128]{2,1,0:T(8,128)}, u32[]{:S(2)}) copy-start(f32[8,128,128]{2,1,0:T(8,128)} %get-tuple-element.15.within_ref) | copy-start | bytes 1572868
  58.4 20.6 %all-to-all-start.2 = ((bf16[8,256,128]{2,1,0:T(8,128)(2,1)}), bf16[8,256,128]{2,1,0:T(8,128)(2,1)S(1)}, u32[]{:S(2)}, u32[]{:S(2)}) async-start(bf16[8,256,128]{2,1,0:T(8,128)(2,1)} %shard_map.49), calls=%async_computation.2 | async-start | bytes 1048576 | tf_op jit(solution)/shard_map/all_to_all | solution.py:326
  66.7 11.1 %collective-permute-start.7 = (bf16[128,2048]{1,0:T(8,128)(2,1)S(1)}, bf16[128,2048]{1,0:T(8,128)(2,1)S(1)}, u32[]{:S(2)}, u32[]{:S(2)}) collective-permute-start(bf16[128,2048]{1,0:T(8,128)(2,1)S(1)} %collective-permute-done.3.refs_1_), channel_id=1, source_target_pairs={{16,0},{49,1},{18,2},{51,3},{20,4},{53,5},{22,6},{55,7},{24,8},{57... | collective-permute-start | bytes 1572872 | tf_op jit(solution)/shard_map/ppermute | solution.py:257
  68.6 14.8 %collective-permute-start.8 = (bf16[128,2048]{1,0:T(8,128)(2,1)S(1)}, bf16[128,2048]{1,0:T(8,128)(2,1)S(1)}, u32[]{:S(2)}, u32[]{:S(2)}) collective-permute-start(bf16[128,2048]{1,0:T(8,128)(2,1)S(1)} %collective-permute-done.4.refs_2_), channel_id=1, source_target_pairs={{16,0},{49,1},{18,2},{51,3},{20,4},{53,5},{22,6},{55,7},{24,8},{57... | collective-permute-start | bytes 1572872 | tf_op jit(solution)/shard_map/ppermute | solution.py:257
  73.2 10.4 %collective-permute-start.6 = (bf16[128,2048]{1,0:T(8,128)(2,1)}, bf16[128,2048]{1,0:T(8,128)(2,1)}, u32[]{:S(2)}, u32[]{:S(2)}) collective-permute-start(bf16[128,2048]{1,0:T(8,128)(2,1)} %collective-permute-done.5.refs_3_), channel_id=1, source_target_pairs={{64,0},{449,1},{66,2},{451,3},{68,4},{453,5},{70,6},{455,7},{72,8}... | collective-permute-start | bytes 1572872 | tf_op jit(solution)/shard_map/ppermute | solution.py:257
  75.1 14.3 %collective-permute-start.9 = (bf16[128,2048]{1,0:T(8,128)(2,1)}, bf16[128,2048]{1,0:T(8,128)(2,1)}, u32[]{:S(2)}, u32[]{:S(2)}) collective-permute-start(bf16[128,2048]{1,0:T(8,128)(2,1)} %collective-permute-done.5.refs_3_), channel_id=1, source_target_pairs={{16,0},{49,1},{18,2},{51,3},{20,4},{53,5},{22,6},{55,7},{24,8},{57... | collective-permute-start | bytes 1572872 | tf_op jit(solution)/shard_map/ppermute | solution.py:257
  92.1 10.7 %collective-permute-start.10 = (bf16[128,2048]{1,0:T(8,128)(2,1)S(1)}, bf16[128,2048]{1,0:T(8,128)(2,1)S(1)}, u32[]{:S(2)}, u32[]{:S(2)}) collective-permute-start(bf16[128,2048]{1,0:T(8,128)(2,1)S(1)} %get-tuple-element.22), channel_id=1, source_target_pairs={{0,1},{1,0},{2,3},{3,2},{4,5},{5,4},{6,7},{7,6},{8,9},{9,8},{10,11... | collective-permute-start | bytes 1572872 | tf_op jit(solution)/shard_map/ppermute | solution.py:333

commit v5 on v3

--- a/solution.py
+++ b/solution.py
@@ -156,35 +156,54 @@
     return (soft + normalize(linear) * 0.5).astype(bf16)
 
 
-def inner_kernel(q_ref, k_ref, v_ref, within_ref, before_ref, totals_ref, out_ref):
+def inner_kernel(q_ref, k_ref, v_ref, out_hbm, held_ref, sems):
+    sent = []
+    upper = upper_mask()
+    near = W // BLOCK
+    for b in range(q_ref.shape[0] // BLOCK - near):
+        q = rows_of(q_ref, near + b)
+        keys = [rows_of(k_ref, b + j) for j in range(near + 1)]
+        values = [rows_of(v_ref, b + j) for j in range(near + 1)]
+        soft, linear = block_rows(q, keys, values, None, upper)
+        held_ref[b, 0] = soft
+        held_ref[b, 1] = linear
+        sent.append(pltpu.make_async_copy(held_ref.at[b], out_hbm.at[b], sems.at[b]))
+        sent[-1].start()
+    for copy in sent:
+        copy.wait()
+
+
+def outer_kernel(
+    q_ref, k_ref, v_ref, rim_hbm, within_hbm, inner_hbm, before_ref, totals_ref,
+    out_hbm, rim_ref, within_ref, inner_ref, out_ref, sems, out_sems,
+):
+    near = W // BLOCK
+    fetches = [
+        pltpu.make_async_copy(source, target, sems.at[i])
+        for i, (source, target) in enumerate(
+            ((within_hbm, within_ref), (inner_hbm, inner_ref), (rim_hbm, rim_ref))
+        )
+    ]
+    for fetch in fetches:
+        fetch.start()
+    sent = []
+
+    def send(b):
+        sent.append(pltpu.make_async_copy(out_ref.at[b], out_hbm.at[b], out_sems.at[b]))
+        sent[-1].start()
+
     upper = upper_mask()
     prior = prior_state(before_ref, totals_ref)
-    near = W // BLOCK
+    fetches[0].wait()
+    fetches[1].wait()
     for b in range(near, q_ref.shape[0] // BLOCK):
-        q = rows_of(q_ref, b)
-        keys = [rows_of(k_ref, b - near + j) for j in range(near + 1)]
-        values = [rows_of(v_ref, b - near + j) for j in range(near + 1)]
-        soft, linear = block_rows(q, keys, values, None, upper)
-        out_ref[b - near] = mix(q, soft, linear, prior + within_ref[b])
-
-
-def outer_kernel(
-    q_ref, k_ref, v_ref, rim_hbm, within_ref, before_ref, totals_ref, inner_ref, out_hbm, rim_ref, out_ref, sems, out_sems
-):
-    near = W // BLOCK
-    copies = []
-    for j in reversed(range(near)):
-        part = pl.ds(j * BLOCK, BLOCK)
-        copies.append(pltpu.make_async_copy(rim_hbm.at[:, part], rim_ref.at[:, part], sems.at[j]))
-        copies[-1].start()
-    sent = [pltpu.make_async_copy(inner_ref, out_hbm.at[pl.ds(near, near)], out_sems.at[near])]
-    sent[0].start()
-    upper = upper_mask()
-    prior = prior_state(before_ref, totals_ref)
+        soft, linear = inner_ref[b - near, 0], inner_ref[b - near, 1]
+        out_ref[b] = mix(rows_of(q_ref, b), soft, linear, prior + within_ref[b])
+        send(b)
+    fetches[2].wait()
     first = jnp.logical_and(lax.axis_index("y") == 0, lax.axis_index("x") == 0)
     hidden = jnp.where(first, far_below, 0.0).astype(f32)
-    for b in reversed(range(near)):
-        copies[near - 1 - b].wait()
+    for b in range(near):
         keys, values, bias = [], [], []
         for j in range(near + 1):
             at = b + j
@@ -199,8 +218,7 @@
         q = rows_of(q_ref, b)
         soft, linear = block_rows(q, keys, values, bias, upper)
         out_ref[b] = mix(q, soft, linear, prior + within_ref[b])
-        sent.append(pltpu.make_async_copy(out_ref.at[b], out_hbm.at[b], out_sems.at[b]))
-        sent[-1].start()
+        send(b)
     for copy in sent:
         copy.wait()
 
@@ -313,20 +331,21 @@
     totals = lax.all_to_all(totals, "y", 0, 0, tiled=True)
     y2 = moved(y1, along)
     e1 = moved(y1, across)
-    shared = (within, before, totals)
-    inner = call(inner_kernel, shape((NZ // 2, rows // NZ, HD), bf16), [VMEM] * 6)(
-        queries, key_vectors, value_vectors, *shared
-    )
+    half = (W // BLOCK, 2, BLOCK, HD)
+    inner = call(
+        inner_kernel, shape(half, f32), [VMEM] * 3, out_specs=ANY,
+        scratch=[pltpu.VMEM(half, f32), pltpu.SemaphoreType.DMA((W // BLOCK,))],
+    )(queries, key_vectors, value_vectors)
     y3 = moved(y2, along)
     e2 = moved(y2, across)
+    mixed_shape = (NZ, rows // NZ, HD)
     mixed = call(
-        outer_kernel, shape((NZ, rows // NZ, HD), bf16), [VMEM] * 3 + [ANY] + [VMEM] * 4,
+        outer_kernel, shape(mixed_shape, bf16), [VMEM] * 3 + [ANY] * 3 + [VMEM] * 2,
         out_specs=ANY,
-        scratch=[pltpu.VMEM((2, W, HD), bf16), pltpu.VMEM((W // BLOCK, BLOCK, HD), bf16)]
-        + [pltpu.SemaphoreType.DMA((W // BLOCK,)), pltpu.SemaphoreType.DMA((1 + W // BLOCK,))],
-    )(
-        queries, key_vectors, value_vectors, rim, *shared, inner
-    )
+        scratch=[pltpu.VMEM((2, W, HD), bf16), pltpu.VMEM((rows // BLOCK, HD, HD), f32)]
+        + [pltpu.VMEM(half, f32), pltpu.VMEM(mixed_shape, bf16)]
+        + [pltpu.SemaphoreType.DMA((3,)), pltpu.SemaphoreType.DMA((NZ,))],
+    )(queries, key_vectors, value_vectors, rim, within, inner, before, totals)
     mixed = lax.all_to_all(mixed, "z", 0, 0, tiled=True)
     y4 = moved(y3, along)
     e3 = moved(y3, across)

time: 106 us -> 105 us (level)
  waiting for transfers between devices: 26.1 us -> 22.3 us
  Pallas kernels: 15 us -> 16.9 us
    all_to_all x1, waiting for transfers between devices: 8.56 us -> 4.92 us  [layer(): totals = lax.all_to_all(totals, 'y', 0, 0, tiled=True)]
    pallas_call x2, Pallas kernels: 8.55 us -> 9.67 us  [the longest x1 6.08 us: layer(): call(outer_kernel, shape(mixed_shape, bf16), [VMEM] * 3 + [ANY] * 3 + [VM...]
  transfers between devices with their start and end apart: 14 -> 14, of which waited for: 8 -> 8; matrix products, arithmetic and copies ran while one was open for 0% -> 0% of each run, Pallas kernels for 11% -> 13%
where the time goes in v5:
time: 105 us; the launch traced here: 104 us
  starting transfers between devices  62.5 us (60%)
  waiting for transfers between devices  22.3 us (21%)
  Pallas kernels  16.9 us (16%)
  local copies, waits for them, and re-layouts  1.85 us (2%)
    ppermute x9, starting transfers between devices, moved(): return lax.ppermute(shard, AXES, pairs)  32.3 us
    ppermute x9, waiting for transfers between devices, moved(): return lax.ppermute(shard, AXES, pairs)  14.8 us
    ppermute x1, starting transfers between devices, layer(): taken = lax.ppermute(given, 'c', [(0, 1), (1, 0)])  9.23 us
    all_to_all x1, starting transfers between devices, layer(): mixed = lax.all_to_all(mixed, 'z', 0, 0, tiled=True)  8.49 us
    pallas_call x1, Pallas kernels, layer(): call(outer_kernel, shape(mixed_shape, bf16), [VMEM] * 3 + [ANY] * 3 + [VM...  6.08 us
    all_to_all x1, starting transfers between devices, layer(): row_states = lax.all_to_all(states, 'x', 0, 0, tiled=True)  5.78 us
    all_to_all x1, waiting for transfers between devices, layer(): totals = lax.all_to_all(totals, 'y', 0, 0, tiled=True)  4.92 us
    all_to_all x1, starting transfers between devices, layer(): totals = lax.all_to_all(totals, 'y', 0, 0, tiled=True)  4.77 us
  transfers between devices with their start and end apart: 14, of which 8 were waited for; matrix products, arithmetic and copies ran while one was open for 0% of the time, Pallas kernels for 13%

profile of v5, /device:TPU:7, one launch (start us, length us, event | category | flops | bytes accessed | tf_op | source)
XLA Modules:
  0.0 103.8 jit_solution(16577562833437532755)
XLA Ops:
  0.0 3.0 %collective-permute-start.1 = (bf16[64,2048]{1,0:T(8,128)(2,1)}, bf16[64,2048]{1,0:T(8,128)(2,1)S(1)}, u32[]{:S(2)}, u32[]{:S(2)}) collective-permute-start(bf16[64,2048]{1,0:T(8,128)(2,1)} %param.7), channel_id=1, source_target_pairs={{1,0},{33,1},{3,2},{35,3},{5,4},{37,5},{7,6},{39,7},{9,8},{41,9},{... | collective-permute-start | bytes 786440 | tf_op jit(solution)/shard_map/ppermute | solution.py:278
  3.0 7.0 %collective-permute-start.2 = (bf16[64,2048]{1,0:T(8,128)(2,1)}, bf16[64,2048]{1,0:T(8,128)(2,1)S(1)}, u32[]{:S(2)}, u32[]{:S(2)}) collective-permute-start(bf16[64,2048]{1,0:T(8,128)(2,1)} %param.7), channel_id=1, source_target_pairs={{17,0},{49,1},{19,2},{51,3},{21,4},{53,5},{23,6},{55,7},{25,8},{57... | collective-permute-start | bytes 786440 | tf_op jit(solution)/shard_map/ppermute | solution.py:278
  10.0 0.0 collective-permute-done.1.first_ref
  10.0 3.6 %collective-permute-done.2.second_ref = bf16[64,2048]{1,0:T(8,128)(2,1)S(1)} collective-permute-done((bf16[64,2048]{1,0:T(8,128)(2,1)}, bf16[64,2048]{1,0:T(8,128)(2,1)S(1)}, u32[]{:S(2)}, u32[]{:S(2)}) %collective-permute-start.2) | collective-permute-done | bytes 262176 | tf_op jit(solution)/shard_map/ppermute | solution.py:278
  13.6 0.1 shard_map.50.refs_0_
  13.7 2.7 %collective-permute-start.3 = (bf16[128,2048]{1,0:T(8,128)(2,1)S(1)}, bf16[128,2048]{1,0:T(8,128)(2,1)S(1)}, u32[]{:S(2)}, u32[]{:S(2)}) collective-permute-start(bf16[128,2048]{1,0:T(8,128)(2,1)S(1)} %shard_map.50.refs_0_), channel_id=1, source_target_pairs={{64,0},{449,1},{66,2},{451,3},{68,4},{453,5},{70,6},{455,7},{72,8}... | collective-permute-start | bytes 1572872 | tf_op jit(solution)/shard_map/ppermute | solution.py:278
  16.4 0.0 copy-start.2
  16.4 2.9 %shard_map.46 = (f32[4,128,128]{2,1,0:T(8,128)}, f32[8,128,128]{2,1,0:T(8,128)}, bf16[2,1024,128]{2,1,0:T(8,128)(2,1)}) custom-call(bf16[2048,128]{1,0:T(8,128)(2,1)} %k_ref.3, bf16[2048,128]{1,0:T(8,128)(2,1)} %v_ref.3), custom_call_target="tpu_custom_call" | custom-call | flops 1 | bytes 67108864 | tf_op jit(solution)/shard_map/pallas_call | solution.py:315
  19.3 0.0 copy-start.1
  19.3 5.8 %all-to-all-start = ((f32[4,128,128]{2,1,0:T(8,128)}), f32[4,128,128]{2,1,0:T(8,128)S(1)}, u32[]{:S(2)}, u32[]{:S(2)}) async-start(f32[4,128,128]{2,1,0:T(8,128)} %get-tuple-element.14), calls=%async_computation | async-start | bytes 524288 | tf_op jit(solution)/shard_map/all_to_all | solution.py:324
  25.1 0.0 copy-start
  25.1 0.0 collective-permute-done.3.refs_1_
  25.1 0.0 copy-start.4
  25.1 4.7 %collective-permute-start.4 = (bf16[128,2048]{1,0:T(8,128)(2,1)S(1)}, bf16[128,2048]{1,0:T(8,128)(2,1)}, u32[]{:S(2)}, u32[]{:S(2)}) collective-permute-start(bf16[128,2048]{1,0:T(8,128)(2,1)S(1)} %collective-permute-done.3.refs_1_), channel_id=1, source_target_pairs={{64,0},{449,1},{66,2},{451,3},{68,4},{453,5},{70,6},{455,7},{72,8}... | collective-permute-start | bytes 1572872 | tf_op jit(solution)/shard_map/ppermute | solution.py:278
  29.8 1.9 %collective-permute-start = (bf16[2,1024,128]{2,1,0:T(8,128)(2,1)}, bf16[2,1024,128]{2,1,0:T(8,128)(2,1)}, u32[]{:S(2)}, u32[]{:S(2)}) collective-permute-start(bf16[2,1024,128]{2,1,0:T(8,128)(2,1)} %get-tuple-element.12), channel_id=1, source_target_pairs={{0,16},{16,32},{32,48},{48,64},{64,80},{80,96},{96,112},{112,128},... | collective-permute-start | bytes 1572872 | tf_op jit(solution)/shard_map/ppermute | solution.py:327
  31.8 0.0 all-to-all-done.states_ref
  31.8 0.7 shard_map.48
  32.5 4.8 %all-to-all-start.1 = ((bf16[8,128,128]{2,1,0:T(8,128)(2,1)}), bf16[8,128,128]{2,1,0:T(8,128)(2,1)S(1)}, u32[]{:S(2)}, u32[]{:S(2)}) async-start(bf16[8,128,128]{2,1,0:T(8,128)(2,1)} %get-tuple-element.16), calls=%async_computation.1 | async-start | bytes 524288 | tf_op jit(solution)/shard_map/all_to_all | solution.py:331
  37.3 0.0 collective-permute-done.4.refs_2_
  37.3 0.0 copy-done.4
  37.3 4.6 %collective-permute-start.5 = (bf16[128,2048]{1,0:T(8,128)(2,1)}, bf16[128,2048]{1,0:T(8,128)(2,1)}, u32[]{:S(2)}, u32[]{:S(2)}) collective-permute-start(bf16[128,2048]{1,0:T(8,128)(2,1)} %collective-permute-done.4.refs_2_), channel_id=1, source_target_pairs={{64,0},{449,1},{66,2},{451,3},{68,4},{453,5},{70,6},{455,7},{72,8}... | collective-permute-start | bytes 1572872 | tf_op jit(solution)/shard_map/ppermute | solution.py:278
  41.9 0.0 copy-done.2
  41.9 0.0 copy-done.1
  41.9 0.0 copy-done
  41.9 3.6 %shard_map.47.inner_hbm = f32[4,2,256,128]{3,2,1,0:T(8,128)S(1)} custom-call(bf16[2048,128]{1,0:T(8,128)(2,1)S(1)} %copy-done.2, bf16[2048,128]{1,0:T(8,128)(2,1)S(1)} %copy-done, bf16[2048,128]{1,0:T(8,128)(2,1)S(1)} %copy-done.1), custom_call_target="tpu_custom_call" | custom-call | flops 1 | bytes 67108864 | tf_op jit(solution)/shard_map/pallas_call | solution.py:335
  45.5 0.0 collective-permute-done.rim_hbm
  45.5 4.9 %all-to-all-done.1.totals_ref = bf16[8,128,128]{2,1,0:T(8,128)(2,1)S(1)} async-done(((bf16[8,128,128]{2,1,0:T(8,128)(2,1)}), bf16[8,128,128]{2,1,0:T(8,128)(2,1)S(1)}, u32[]{:S(2)}, u32[]{:S(2)}) %all-to-all-start.1) | async-done | bytes 262176 | tf_op jit(solution)/shard_map/all_to_all | solution.py:331
  50.4 0.0 copy-start.6
  50.4 1.0 %copy-done.6 = f32[8,128,128]{2,1,0:T(8,128)S(1)} copy-done((f32[8,128,128]{2,1,0:T(8,128)S(1)}, f32[8,128,128]{2,1,0:T(8,128)}, u32[]{:S(2)}) %copy-start.6) | copy-done | bytes 524312
  51.5 6.1 %shard_map.49 = bf16[8,256,128]{2,1,0:T(8,128)(2,1)S(1)} custom-call(bf16[2048,128]{1,0:T(8,128)(2,1)S(1)} %copy-done.2, bf16[2048,128]{1,0:T(8,128)(2,1)S(1)} %copy-done, bf16[2048,128]{1,0:T(8,128)(2,1)S(1)} %copy-done.1, bf16[2,1024,128]{2,1,0:T(8,128)(2,1)} %collective-permute-done.rim_hbm, f32[8,128,128]{2,1,0:T(8,128)S(1)} %copy-done.6, ...), custom_call_target="tpu_custom_call" | custom-call | flops 1 | bytes 67108864 | tf_op jit(solution)/shard_map/pallas_call | solution.py:342
  57.6 0.0 copy-start.3
  57.6 0.8 copy-done.3
  58.4 8.5 %all-to-all-start.2 = ((bf16[8,256,128]{2,1,0:T(8,128)(2,1)}), bf16[8,256,128]{2,1,0:T(8,128)(2,1)S(1)}, u32[]{:S(2)}, u32[]{:S(2)}) async-start(bf16[8,256,128]{2,1,0:T(8,128)(2,1)} %copy-done.3), calls=%async_computation.2 | async-start | bytes 1048576 | tf_op jit(solution)/shard_map/all_to_all | solution.py:349
  66.9 0.0 copy-done.5
  66.9 1.9 %collective-permute-start.7 = (bf16[128,2048]{1,0:T(8,128)(2,1)S(1)}, bf16[128,2048]{1,0:T(8,128)(2,1)S(1)}, u32[]{:S(2)}, u32[]{:S(2)}) collective-permute-start(bf16[128,2048]{1,0:T(8,128)(2,1)S(1)} %copy-done.5), channel_id=1, source_target_pairs={{16,0},{49,1},{18,2},{51,3},{20,4},{53,5},{22,6},{55,7},{24,8},{57... | collective-permute-start | bytes 1572872 | tf_op jit(solution)/shard_map/ppermute | solution.py:278
  68.8 4.6 %collective-permute-start.8 = (bf16[128,2048]{1,0:T(8,128)(2,1)}, bf16[128,2048]{1,0:T(8,128)(2,1)S(1)}, u32[]{:S(2)}, u32[]{:S(2)}) collective-permute-start(bf16[128,2048]{1,0:T(8,128)(2,1)} %collective-permute-done.4.refs_2_), channel_id=1, source_target_pairs={{16,0},{49,1},{18,2},{51,3},{20,4},{53,5},{22,6},{55,7},{24,8},{57... | collective-permute-start | bytes 1572872 | tf_op jit(solution)/shard_map/ppermute | solution.py:278
  73.4 0.0 collective-permute-done.5.refs_3_
  73.4 1.9 %collective-permute-start.6 = (bf16[128,2048]{1,0:T(8,128)(2,1)}, bf16[128,2048]{1,0:T(8,128)(2,1)S(1)}, u32[]{:S(2)}, u32[]{:S(2)}) collective-permute-start(bf16[128,2048]{1,0:T(8,128)(2,1)} %collective-permute-done.5.refs_3_), channel_id=1, source_target_pairs={{64,0},{449,1},{66,2},{451,3},{68,4},{453,5},{70,6},{455,7},{72,8}... | collective-permute-start | bytes 1572872 | tf_op jit(solution)/shard_map/ppermute | solution.py:278
  75.3 1.9 %collective-permute-start.9 = (bf16[128,2048]{1,0:T(8,128)(2,1)}, bf16[128,2048]{1,0:T(8,128)(2,1)}, u32[]{:S(2)}, u32[]{:S(2)}) collective-permute-start(bf16[128,2048]{1,0:T(8,128)(2,1)} %collective-permute-done.5.refs_3_), channel_id=1, source_target_pairs={{16,0},{49,1},{18,2},{51,3},{20,4},{53,5},{22,6},{55,7},{24,8},{57... | collective-permute-start | bytes 1572872 | tf_op jit(solution)/shard_map/ppermute | solution.py:278
  77.2 0.8 collective-permute-done.7.refs_5_
  78.0 1.1 %all-to-all-done.2.mixed_ref = bf16[8,256,128]{2,1,0:T(8,128)(2,1)S(1)} async-done(((bf16[8,256,128]{2,1,0:T(8,128)(2,1)}), bf16[8,256,128]{2,1,0:T(8,128)(2,1)S(1)}, u32[]{:S(2)}, u32[]{:S(2)}) %all-to-all-start.2) | async-done | bytes 524320 | tf_op jit(solution)/shard_map/all_to_all | solution.py:349
  79.1 4.5 %collective-permute-done.8.refs_6_ = bf16[128,2048]{1,0:T(8,128)(2,1)S(1)} collective-permute-done((bf16[128,2048]{1,0:T(8,128)(2,1)}, bf16[128,2048]{1,0:T(8,128)(2,1)S(1)}, u32[]{:S(2)}, u32[]{:S(2)}) %collective-permute-start.8) | collective-permute-done | bytes 524320 | tf_op jit(solution)/shard_map/ppermute | solution.py:278
  83.6 0.2 collective-permute-done.6.refs_4_
  83.8 5.7 %collective-permute-done.9.refs_7_ = bf16[128,2048]{1,0:T(8,128)(2,1)} collective-permute-done((bf16[128,2048]{1,0:T(8,128)(2,1)}, bf16[128,2048]{1,0:T(8,128)(2,1)}, u32[]{:S(2)}, u32[]{:S(2)}) %collective-permute-start.9) | collective-permute-done | bytes 524320 | tf_op jit(solution)/shard_map/ppermute | solution.py:278
  89.5 2.6 %shard_map.51 = (bf16[128,2048]{1,0:T(8,128)(2,1)S(1)}, f32[128,2048]{1,0:T(8,128)S(1)}) custom-call(bf16[8,256,128]{2,1,0:T(8,128)(2,1)S(1)} %all-to-all-done.2.mixed_ref, bf16[128,2048]{1,0:T(8,128)(2,1)S(1)} %shard_map.50.refs_0_, bf16[128,2048]{1,0:T(8,128)(2,1)S(1)} %copy-done.5, bf16[128,2048]{1,0:T(8,128)(2,1)} %collective-permute-done.4.refs_2_, ...), custom_call_target="tpu_custom_call" | custom-call | flops 1 | bytes 67108864 | tf_op jit(solution)/shard_map/pallas_call | solution.py:352
  92.1 9.2 %collective-permute-start.10 = (bf16[128,2048]{1,0:T(8,128)(2,1)S(1)}, bf16[128,2048]{1,0:T(8,128)(2,1)S(1)}, u32[]{:S(2)}, u32[]{:S(2)}) collective-permute-start(bf16[128,2048]{1,0:T(8,128)(2,1)S(1)} %get-tuple-element.18), channel_id=1, source_target_pairs={{0,1},{1,0},{2,3},{3,2},{4,5},{5,4},{6,7},{7,6},{8,9},{9,8},{10,11... | collective-permute-start | bytes 1572872 | tf_op jit(solution)/shard_map/ppermute | solution.py:356
  101.4 1.5 %collective-permute-done.10.taken_ref = bf16[128,2048]{1,0:T(8,128)(2,1)S(1)} collective-permute-done((bf16[128,2048]{1,0:T(8,128)(2,1)S(1)}, bf16[128,2048]{1,0:T(8,128)(2,1)S(1)}, u32[]{:S(2)}, u32[]{:S(2)}) %collective-permute-start.10) | collective-permute-done | bytes 524320 | tf_op jit(solution)/shard_map/ppermute | solution.py:356
  102.9 0.9 shard_map.52
  (1 shorter events, 0.0 us)
Async XLA Ops:
  0.0 10.0 %collective-permute-start.1 = (bf16[64,2048]{1,0:T(8,128)(2,1)}, bf16[64,2048]{1,0:T(8,128)(2,1)S(1)}, u32[]{:S(2)}, u32[]{:S(2)}) collective-permute-start(bf16[64,2048]{1,0:T(8,128)(2,1)} %param.7), channel_id=1, source_target_pairs={{1,0},{33,1},{3,2},{35,3},{5,4},{37,5},{7,6},{39,7},{9,8},{41,9},{... | collective-permute-start | bytes 786440 | tf_op jit(solution)/shard_map/ppermute | solution.py:278
  3.0 10.6 %collective-permute-start.2 = (bf16[64,2048]{1,0:T(8,128)(2,1)}, bf16[64,2048]{1,0:T(8,128)(2,1)S(1)}, u32[]{:S(2)}, u32[]{:S(2)}) collective-permute-start(bf16[64,2048]{1,0:T(8,128)(2,1)} %param.7), channel_id=1, source_target_pairs={{17,0},{49,1},{19,2},{51,3},{21,4},{53,5},{23,6},{55,7},{25,8},{57... | collective-permute-start | bytes 786440 | tf_op jit(solution)/shard_map/ppermute | solution.py:278
  13.7 11.4 %collective-permute-start.3 = (bf16[128,2048]{1,0:T(8,128)(2,1)S(1)}, bf16[128,2048]{1,0:T(8,128)(2,1)S(1)}, u32[]{:S(2)}, u32[]{:S(2)}) collective-permute-start(bf16[128,2048]{1,0:T(8,128)(2,1)S(1)} %shard_map.50.refs_0_), channel_id=1, source_target_pairs={{64,0},{449,1},{66,2},{451,3},{68,4},{453,5},{70,6},{455,7},{72,8}... | collective-permute-start | bytes 1572872 | tf_op jit(solution)/shard_map/ppermute | solution.py:278
  16.4 25.5 %copy-start.2 = (bf16[2048,128]{1,0:T(8,128)(2,1)S(1)}, bf16[2048,128]{1,0:T(8,128)(2,1)}, u32[]{:S(2)}) copy-start(bf16[2048,128]{1,0:T(8,128)(2,1)} %q_ref.3) | copy-start | bytes 1572868
  19.3 22.6 %copy-start.1 = (bf16[2048,128]{1,0:T(8,128)(2,1)S(1)}, bf16[2048,128]{1,0:T(8,128)(2,1)}, u32[]{:S(2)}) copy-start(bf16[2048,128]{1,0:T(8,128)(2,1)} %v_ref.3) | copy-start | bytes 1572868
  19.3 12.4 %all-to-all-start = ((f32[4,128,128]{2,1,0:T(8,128)}), f32[4,128,128]{2,1,0:T(8,128)S(1)}, u32[]{:S(2)}, u32[]{:S(2)}) async-start(f32[4,128,128]{2,1,0:T(8,128)} %get-tuple-element.14), calls=%async_computation | async-start | bytes 524288 | tf_op jit(solution)/shard_map/all_to_all | solution.py:324
  25.1 16.8 %copy-start = (bf16[2048,128]{1,0:T(8,128)(2,1)S(1)}, bf16[2048,128]{1,0:T(8,128)(2,1)}, u32[]{:S(2)}) copy-start(bf16[2048,128]{1,0:T(8,128)(2,1)} %k_ref.3) | copy-start | bytes 1572868
  25.1 12.2 %copy-start.4 = (bf16[128,2048]{1,0:T(8,128)(2,1)}, bf16[128,2048]{1,0:T(8,128)(2,1)S(1)}, u32[]{:S(2)}) copy-start(bf16[128,2048]{1,0:T(8,128)(2,1)S(1)} %collective-permute-done.3.refs_1_) | copy-start | bytes 1572868
  25.1 12.2 %collective-permute-start.4 = (bf16[128,2048]{1,0:T(8,128)(2,1)S(1)}, bf16[128,2048]{1,0:T(8,128)(2,1)}, u32[]{:S(2)}, u32[]{:S(2)}) collective-permute-start(bf16[128,2048]{1,0:T(8,128)(2,1)S(1)} %collective-permute-done.3.refs_1_), channel_id=1, source_target_pairs={{64,0},{449,1},{66,2},{451,3},{68,4},{453,5},{70,6},{455,7},{72,8}... | collective-permute-start | bytes 1572872 | tf_op jit(solution)/shard_map/ppermute | solution.py:278
  29.8 15.7 %collective-permute-start = (bf16[2,1024,128]{2,1,0:T(8,128)(2,1)}, bf16[2,1024,128]{2,1,0:T(8,128)(2,1)}, u32[]{:S(2)}, u32[]{:S(2)}) collective-permute-start(bf16[2,1024,128]{2,1,0:T(8,128)(2,1)} %get-tuple-element.12), channel_id=1, source_target_pairs={{0,16},{16,32},{32,48},{48,64},{64,80},{80,96},{96,112},{112,128},... | collective-permute-start | bytes 1572872 | tf_op jit(solution)/shard_map/ppermute | solution.py:327
  32.5 17.9 %all-to-all-start.1 = ((bf16[8,128,128]{2,1,0:T(8,128)(2,1)}), bf16[8,128,128]{2,1,0:T(8,128)(2,1)S(1)}, u32[]{:S(2)}, u32[]{:S(2)}) async-start(bf16[8,128,128]{2,1,0:T(8,128)(2,1)} %get-tuple-element.16), calls=%async_computation.1 | async-start | bytes 524288 | tf_op jit(solution)/shard_map/all_to_all | solution.py:331
  37.3 36.1 %collective-permute-start.5 = (bf16[128,2048]{1,0:T(8,128)(2,1)}, bf16[128,2048]{1,0:T(8,128)(2,1)}, u32[]{:S(2)}, u32[]{:S(2)}) collective-permute-start(bf16[128,2048]{1,0:T(8,128)(2,1)} %collective-permute-done.4.refs_2_), channel_id=1, source_target_pairs={{64,0},{449,1},{66,2},{451,3},{68,4},{453,5},{70,6},{455,7},{72,8}... | collective-permute-start | bytes 1572872 | tf_op jit(solution)/shard_map/ppermute | solution.py:278
  50.4 1.0 %copy-start.6 = (f32[8,128,128]{2,1,0:T(8,128)S(1)}, f32[8,128,128]{2,1,0:T(8,128)}, u32[]{:S(2)}) copy-start(f32[8,128,128]{2,1,0:T(8,128)} %get-tuple-element.13.within_hbm) | copy-start | bytes 1572868
  57.6 0.8 copy-start.3
  58.4 8.5 %copy-start.5 = (bf16[128,2048]{1,0:T(8,128)(2,1)S(1)}, bf16[128,2048]{1,0:T(8,128)(2,1)}, u32[]{:S(2)}) copy-start(bf16[128,2048]{1,0:T(8,128)(2,1)} %copy-done.4) | copy-start | bytes 1572868
  58.4 20.7 %all-to-all-start.2 = ((bf16[8,256,128]{2,1,0:T(8,128)(2,1)}), bf16[8,256,128]{2,1,0:T(8,128)(2,1)S(1)}, u32[]{:S(2)}, u32[]{:S(2)}) async-start(bf16[8,256,128]{2,1,0:T(8,128)(2,1)} %copy-done.3), calls=%async_computation.2 | async-start | bytes 1048576 | tf_op jit(solution)/shard_map/all_to_all | solution.py:349
  66.9 11.1 %collective-permute-start.7 = (bf16[128,2048]{1,0:T(8,128)(2,1)S(1)}, bf16[128,2048]{1,0:T(8,128)(2,1)S(1)}, u32[]{:S(2)}, u32[]{:S(2)}) collective-permute-start(bf16[128,2048]{1,0:T(8,128)(2,1)S(1)} %copy-done.5), channel_id=1, source_target_pairs={{16,0},{49,1},{18,2},{51,3},{20,4},{53,5},{22,6},{55,7},{24,8},{57... | collective-permute-start | bytes 1572872 | tf_op jit(solution)/shard_map/ppermute | solution.py:278
  68.8 14.8 %collective-permute-start.8 = (bf16[128,2048]{1,0:T(8,128)(2,1)}, bf16[128,2048]{1,0:T(8,128)(2,1)S(1)}, u32[]{:S(2)}, u32[]{:S(2)}) collective-permute-start(bf16[128,2048]{1,0:T(8,128)(2,1)} %collective-permute-done.4.refs_2_), channel_id=1, source_target_pairs={{16,0},{49,1},{18,2},{51,3},{20,4},{53,5},{22,6},{55,7},{24,8},{57... | collective-permute-start | bytes 1572872 | tf_op jit(solution)/shard_map/ppermute | solution.py:278
  73.4 10.4 %collective-permute-start.6 = (bf16[128,2048]{1,0:T(8,128)(2,1)}, bf16[128,2048]{1,0:T(8,128)(2,1)S(1)}, u32[]{:S(2)}, u32[]{:S(2)}) collective-permute-start(bf16[128,2048]{1,0:T(8,128)(2,1)} %collective-permute-done.5.refs_3_), channel_id=1, source_target_pairs={{64,0},{449,1},{66,2},{451,3},{68,4},{453,5},{70,6},{455,7},{72,8}... | collective-permute-start | bytes 1572872 | tf_op jit(solution)/shard_map/ppermute | solution.py:278
  75.3 14.2 %collective-permute-start.9 = (bf16[128,2048]{1,0:T(8,128)(2,1)}, bf16[128,2048]{1,0:T(8,128)(2,1)}, u32[]{:S(2)}, u32[]{:S(2)}) collective-permute-start(bf16[128,2048]{1,0:T(8,128)(2,1)} %collective-permute-done.5.refs_3_), channel_id=1, source_target_pairs={{16,0},{49,1},{18,2},{51,3},{20,4},{53,5},{22,6},{55,7},{24,8},{57... | collective-permute-start | bytes 1572872 | tf_op jit(solution)/shard_map/ppermute | solution.py:278
  92.1 10.8 %collective-permute-start.10 = (bf16[128,2048]{1,0:T(8,128)(2,1)S(1)}, bf16[128,2048]{1,0:T(8,128)(2,1)S(1)}, u32[]{:S(2)}, u32[]{:S(2)}) collective-permute-start(bf16[128,2048]{1,0:T(8,128)(2,1)S(1)} %get-tuple-element.18), channel_id=1, source_target_pairs={{0,1},{1,0},{2,3},{3,2},{4,5},{5,4},{6,7},{7,6},{8,9},{9,8},{10,11... | collective-permute-start | bytes 1572872 | tf_op jit(solution)/shard_map/ppermute | solution.py:356

commit v6 on v4

--- a/solution.py
+++ b/solution.py
@@ -47,7 +47,7 @@
 ANY = pl.BlockSpec(memory_space=pl.ANY)
 
 
-def call(kernel, outs, in_specs, scratch=(), grant=12 << 20, out_specs=None):
+def call(kernel, outs, in_specs, nbytes=64 << 20, scratch=(), grant=12 << 20, out_specs=None):
     return pl.pallas_call(
         kernel,
         out_shape=outs,
@@ -55,7 +55,7 @@
         scratch_shapes=scratch,
         out_specs=out_specs or jax.tree.map(lambda _: VMEM, outs),
         compiler_params=pltpu.CompilerParams(vmem_limit_bytes=grant),
-        cost_estimate=pl.CostEstimate(flops=1, transcendentals=0, bytes_accessed=64 << 20),
+        cost_estimate=pl.CostEstimate(flops=1, transcendentals=0, bytes_accessed=nbytes),
     )
 
 
@@ -210,29 +210,47 @@
     out_ref[half:, :] = jnp.where(odd, first, second)
 
 
-def project_kernel(mixed_ref, *refs):
-    units, given_ref, kept_ref = refs[:-2], refs[-2], refs[-1]
+def heads_of(mixed_ref, steps):
     y, x, c = lax.axis_index("y"), lax.axis_index("x"), lax.axis_index("c")
     turn = way(x, c)
     given, kept = [], []
-    for step in unit_steps:
+    for step in steps:
         head = lax.rem(y + turn * step + NY, NY)
         given.append(mixed_ref[head, pl.ds(pl.multiple_of((1 - c) * HD, HD), HD), :])
         kept.append(mixed_ref[head, pl.ds(pl.multiple_of(c * HD, HD), HD), :])
-    left = [
+    return [
         jnp.concatenate(
             [jnp.concatenate(given[i : i + 2], axis=1), jnp.concatenate(kept[i : i + 2], axis=1)], axis=0
         )
-        for i in range(0, NY, 2)
+        for i in range(0, len(steps), 2)
     ]
-    width = 512
-    for n in range(kept_ref.shape[1] // width):
-        cols = slice(n * width, (n + 1) * width)
-        total = None
-        for i in range(0, NY, 2):
-            rows = jnp.concatenate([units[i][:, cols], units[i + 1][:, cols]], axis=0)
-            term = dot(left[i // 2], rows)
-            total = term if total is None else total + term
+
+
+def units_sum(left, units, cols):
+    total = None
+    for i in range(0, len(units), 2):
+        rows = jnp.concatenate([units[i][:, cols], units[i + 1][:, cols]], axis=0)
+        term = dot(left[i // 2], rows)
+        total = term if total is None else total + term
+    return total
+
+
+def blocks_of_columns(ref, width=512):
+    return [slice(n, n + width) for n in range(0, ref.shape[1], width)]
+
+
+def early_kernel(mixed_ref, *refs):
+    units, out_ref = refs[:-1], refs[-1]
+    left = heads_of(mixed_ref, early_steps)
+    for cols in blocks_of_columns(out_ref):
+        out_ref[:, cols] = units_sum(left, units, cols)
+
+
+def late_kernel(mixed_ref, early_ref, *refs):
+    units, given_ref, kept_ref = refs[:-2], refs[-2], refs[-1]
+    left = heads_of(mixed_ref, late_steps)
+    for cols in blocks_of_columns(kept_ref):
+        total = early_ref[:, cols] + units_sum(left, units, cols)
         given_ref[:, cols] = total[:HD].astype(bf16)
         kept_ref[:, cols] = total[HD:]
 
@@ -267,7 +285,8 @@
     return (y, x, z, 1 - c) if x // 2 == c else (y, x ^ 2, z, c)
 
 
-unit_steps = (0, 1, 2, 3, 4, -1, -2, -3)
+early_steps = (0, 1, 2, 3, -1, -2)
+late_steps = (4, -3)
 
 
 def way(x, c):
@@ -304,7 +323,7 @@
     unit = call(unit_kernel, shape((2 * w_out.shape[0], wide), bf16), [VMEM] * 2)(chunk_b, chunk_a)
     y1 = moved(unit, along)
     rim = lax.ppermute(rim, ("y", "x"), [(i, i + 1) for i in range(NY * NX - 1)])
-    before, totals = call(row_kernel, (shape((HD, HD), f32), shape((NY, HD, HD), bf16)), [VMEM])(row_states)
+    before, totals = call(row_kernel, (shape((HD, HD), f32), shape((NY, HD, HD), bf16)), [VMEM], nbytes=0)(row_states)
     totals = lax.all_to_all(totals, "y", 0, 0, tiled=True)
     y2 = moved(y1, along)
     e1 = moved(y1, across)
@@ -326,10 +345,8 @@
     mixed = lax.all_to_all(mixed, "z", 0, 0, tiled=True)
     y4 = moved(y3, along)
     e3 = moved(y3, across)
-    given, kept = call(
-        project_kernel, (shape((HD, wide), bf16), shape((HD, wide), f32)),
-        [VMEM] * (1 + NY),
-    )(mixed, unit, y1, y2, y3, y4, e1, e2, e3)
+    early = call(early_kernel, shape((2 * HD, wide), f32), [VMEM] * 7)(mixed, unit, y1, y2, y3, e1, e2)
+    given, kept = call(late_kernel, (shape((HD, wide), bf16), shape((HD, wide), f32)), [VMEM] * 4)(mixed, early, y4, e3)
     taken = lax.ppermute(given, "c", [(0, 1), (1, 0)])
     return call(add_kernel, shape((HD, wide), bf16), [VMEM] * 2)(kept, taken)
 

time: 104 us -> 102 us (0.981)
  waiting for transfers between devices: 26.1 us -> 23.6 us
    ppermute x9, waiting for transfers between devices: 14.9 us -> 12.5 us  [moved(): return lax.ppermute(shard, AXES, pairs)]
    pallas_call x2 -> x3, Pallas kernels: 2.63 us -> 2.8 us  [the longest x1 2.33 us: layer(): call(early_kernel, shape((2 * HD, wide), f32), [VMEM] * 7)]
  transfers between devices with their start and end apart: 14 -> 14, of which waited for: 9 -> 8; matrix products, arithmetic and copies ran while one was open for 0% -> 0% of each run, Pallas kernels for 9% -> 12%
where the time goes in v6:
time: 102 us; the launch traced here: 101 us
  starting transfers between devices  62.1 us (61%)
  waiting for transfers between devices  23.6 us (23%)
  Pallas kernels  13.5 us (13%)
  local copies, waits for them, and re-layouts  1.75 us (2%)
    ppermute x9, starting transfers between devices, moved(): return lax.ppermute(shard, AXES, pairs)  32.3 us
    ppermute x9, waiting for transfers between devices, moved(): return lax.ppermute(shard, AXES, pairs)  12.5 us
    ppermute x1, starting transfers between devices, layer(): taken = lax.ppermute(given, 'c', [(0, 1), (1, 0)])  9.73 us
    all_to_all x1, starting transfers between devices, layer(): mixed = lax.all_to_all(mixed, 'z', 0, 0, tiled=True)  7.42 us
    all_to_all x1, starting transfers between devices, layer(): row_states = lax.all_to_all(states, 'x', 0, 0, tiled=True)  5.63 us
    all_to_all x1, waiting for transfers between devices, layer(): totals = lax.all_to_all(totals, 'y', 0, 0, tiled=True)  5.59 us
    all_to_all x1, starting transfers between devices, layer(): totals = lax.all_to_all(totals, 'y', 0, 0, tiled=True)  5.12 us
    pallas_call x1, Pallas kernels, layer(): call(outer_kernel, shape((NZ, rows // NZ, HD), bf16), [VMEM] * 8, out_spe...  4.01 us
  transfers between devices with their start and end apart: 14, of which 8 were waited for; matrix products, arithmetic and copies ran while one was open for 0% of the time, Pallas kernels for 12%

profile of v6, /device:TPU:7, one launch (start us, length us, event | category | flops | bytes accessed | tf_op | source)
XLA Modules:
  0.0 101.2 jit_solution(11767802359076363590)
XLA Ops:
  0.0 0.0 copy-start
  0.0 0.0 copy-start.1
  0.0 0.0 copy-start.2
  0.0 3.2 %collective-permute-start.1 = (bf16[64,2048]{1,0:T(8,128)(2,1)}, bf16[64,2048]{1,0:T(8,128)(2,1)S(1)}, u32[]{:S(2)}, u32[]{:S(2)}) collective-permute-start(bf16[64,2048]{1,0:T(8,128)(2,1)} %param.7), channel_id=1, source_target_pairs={{1,0},{33,1},{3,2},{35,3},{5,4},{37,5},{7,6},{39,7},{9,8},{41,9},{... | collective-permute-start | bytes 786440 | tf_op jit(solution)/shard_map/ppermute | solution.py:275
  3.2 7.0 %collective-permute-start.2 = (bf16[64,2048]{1,0:T(8,128)(2,1)}, bf16[64,2048]{1,0:T(8,128)(2,1)S(1)}, u32[]{:S(2)}, u32[]{:S(2)}) collective-permute-start(bf16[64,2048]{1,0:T(8,128)(2,1)} %param.7), channel_id=1, source_target_pairs={{17,0},{49,1},{19,2},{51,3},{21,4},{53,5},{23,6},{55,7},{25,8},{57... | collective-permute-start | bytes 786440 | tf_op jit(solution)/shard_map/ppermute | solution.py:275
  10.2 0.0 collective-permute-done.1.first_ref
  10.2 3.6 %collective-permute-done.2.second_ref = bf16[64,2048]{1,0:T(8,128)(2,1)S(1)} collective-permute-done((bf16[64,2048]{1,0:T(8,128)(2,1)}, bf16[64,2048]{1,0:T(8,128)(2,1)S(1)}, u32[]{:S(2)}, u32[]{:S(2)}) %collective-permute-start.2) | collective-permute-done | bytes 262176 | tf_op jit(solution)/shard_map/ppermute | solution.py:275
  13.8 0.1 shard_map.50.refs_0_
  13.9 2.7 %collective-permute-start.3 = (bf16[128,2048]{1,0:T(8,128)(2,1)S(1)}, bf16[128,2048]{1,0:T(8,128)(2,1)S(1)}, u32[]{:S(2)}, u32[]{:S(2)}) collective-permute-start(bf16[128,2048]{1,0:T(8,128)(2,1)S(1)} %shard_map.50.refs_0_), channel_id=1, source_target_pairs={{64,0},{449,1},{66,2},{451,3},{68,4},{453,5},{70,6},{455,7},{72,8}... | collective-permute-start | bytes 1572872 | tf_op jit(solution)/shard_map/ppermute | solution.py:275
  16.5 2.9 %shard_map.46 = (f32[4,128,128]{2,1,0:T(8,128)}, f32[8,128,128]{2,1,0:T(8,128)}, bf16[2,1024,128]{2,1,0:T(8,128)(2,1)}) custom-call(bf16[2048,128]{1,0:T(8,128)(2,1)} %k_ref.3, bf16[2048,128]{1,0:T(8,128)(2,1)} %v_ref.3), custom_call_target="tpu_custom_call" | custom-call | flops 1 | bytes 67108864 | tf_op jit(solution)/shard_map/pallas_call | solution.py:313
  19.4 5.6 %all-to-all-start = ((f32[4,128,128]{2,1,0:T(8,128)}), f32[4,128,128]{2,1,0:T(8,128)S(1)}, u32[]{:S(2)}, u32[]{:S(2)}) async-start(f32[4,128,128]{2,1,0:T(8,128)} %get-tuple-element.16), calls=%async_computation | async-start | bytes 524288 | tf_op jit(solution)/shard_map/all_to_all | solution.py:322
  25.0 0.0 collective-permute-done.3.refs_1_
  25.0 4.6 %collective-permute-start.4 = (bf16[128,2048]{1,0:T(8,128)(2,1)S(1)}, bf16[128,2048]{1,0:T(8,128)(2,1)}, u32[]{:S(2)}, u32[]{:S(2)}) collective-permute-start(bf16[128,2048]{1,0:T(8,128)(2,1)S(1)} %collective-permute-done.3.refs_1_), channel_id=1, source_target_pairs={{64,0},{449,1},{66,2},{451,3},{68,4},{453,5},{70,6},{455,7},{72,8}... | collective-permute-start | bytes 1572872 | tf_op jit(solution)/shard_map/ppermute | solution.py:275
  29.6 1.9 %collective-permute-start = (bf16[2,1024,128]{2,1,0:T(8,128)(2,1)}, bf16[2,1024,128]{2,1,0:T(8,128)(2,1)S(1)}, u32[]{:S(2)}, u32[]{:S(2)}) collective-permute-start(bf16[2,1024,128]{2,1,0:T(8,128)(2,1)} %get-tuple-element.14), channel_id=1, source_target_pairs={{0,16},{16,32},{32,48},{48,64},{64,80},{80,96},{96,112},{112,128},... | collective-permute-start | bytes 1572872 | tf_op jit(solution)/shard_map/ppermute | solution.py:325
  31.6 0.0 all-to-all-done.states_ref
  31.6 0.0 copy-start.4
  31.6 0.7 copy-done.4
  32.3 5.1 %all-to-all-start.1 = ((bf16[8,128,128]{2,1,0:T(8,128)(2,1)}), bf16[8,128,128]{2,1,0:T(8,128)(2,1)S(1)}, u32[]{:S(2)}, u32[]{:S(2)}) async-start(bf16[8,128,128]{2,1,0:T(8,128)(2,1)} %copy-done.4), calls=%async_computation.1 | async-start | bytes 524288 | tf_op jit(solution)/shard_map/all_to_all | solution.py:327
  37.4 0.0 collective-permute-done.4.refs_2_
  37.4 4.6 %collective-permute-start.5 = (bf16[128,2048]{1,0:T(8,128)(2,1)}, bf16[128,2048]{1,0:T(8,128)(2,1)}, u32[]{:S(2)}, u32[]{:S(2)}) collective-permute-start(bf16[128,2048]{1,0:T(8,128)(2,1)} %collective-permute-done.4.refs_2_), channel_id=1, source_target_pairs={{64,0},{449,1},{66,2},{451,3},{68,4},{453,5},{70,6},{455,7},{72,8}... | collective-permute-start | bytes 1572872 | tf_op jit(solution)/shard_map/ppermute | solution.py:275
  42.0 3.0 %collective-permute-done.rim_hbm = bf16[2,1024,128]{2,1,0:T(8,128)(2,1)S(1)} collective-permute-done((bf16[2,1024,128]{2,1,0:T(8,128)(2,1)}, bf16[2,1024,128]{2,1,0:T(8,128)(2,1)S(1)}, u32[]{:S(2)}, u32[]{:S(2)}) %collective-permute-start) | collective-permute-done | bytes 524320 | tf_op jit(solution)/shard_map/ppermute | solution.py:325
  45.0 5.6 %all-to-all-done.1.totals_ref = bf16[8,128,128]{2,1,0:T(8,128)(2,1)S(1)} async-done(((bf16[8,128,128]{2,1,0:T(8,128)(2,1)}), bf16[8,128,128]{2,1,0:T(8,128)(2,1)S(1)}, u32[]{:S(2)}, u32[]{:S(2)}) %all-to-all-start.1) | async-done | bytes 262176 | tf_op jit(solution)/shard_map/all_to_all | solution.py:327
  50.6 0.0 copy-done
  50.6 0.0 copy-done.1
  50.6 0.0 copy-done.2
  50.6 0.0 copy-start.3
  50.6 1.0 %copy-done.3 = f32[8,128,128]{2,1,0:T(8,128)S(1)} copy-done((f32[8,128,128]{2,1,0:T(8,128)S(1)}, f32[8,128,128]{2,1,0:T(8,128)}, u32[]{:S(2)}) %copy-start.3) | copy-done | bytes 524312
  51.6 2.9 %shard_map.48 = (bf16[4,256,128]{2,1,0:T(8,128)(2,1)S(1)}, bf16[2,1024,128]{2,1,0:T(8,128)(2,1)S(1)}) custom-call(bf16[2048,128]{1,0:T(8,128)(2,1)S(1)} %copy-done.2, bf16[2048,128]{1,0:T(8,128)(2,1)S(1)} %copy-done, bf16[2048,128]{1,0:T(8,128)(2,1)S(1)} %copy-done.1, bf16[2,1024,128]{2,1,0:T(8,128)(2,1)S(1)} %collective-permute-done.rim_hbm, ...), custom_call_target="tpu_custom_call" | custom-call | flops 1 | bytes 67108864 | tf_op jit(solution)/shard_map/pallas_call | solution.py:331
  54.5 4.0 %shard_map.49 = bf16[8,256,128]{2,1,0:T(8,128)(2,1)} custom-call(bf16[2048,128]{1,0:T(8,128)(2,1)S(1)} %copy-done.2, bf16[2048,128]{1,0:T(8,128)(2,1)S(1)} %copy-done, bf16[2048,128]{1,0:T(8,128)(2,1)S(1)} %copy-done.1, bf16[2,1024,128]{2,1,0:T(8,128)(2,1)S(1)} %get-tuple-element.19.rim_ref, f32[8,128,128]{2,1,0:T(8,128)S(1)} %copy-done.3, ...), custom_call_target="tpu_custom_call" | custom-call | flops 1 | bytes 67108864 | tf_op jit(solution)/shard_map/pallas_call | solution.py:339
  58.5 7.4 %all-to-all-start.2 = ((bf16[8,256,128]{2,1,0:T(8,128)(2,1)}), bf16[8,256,128]{2,1,0:T(8,128)(2,1)S(1)}, u32[]{:S(2)}, u32[]{:S(2)}) async-start(bf16[8,256,128]{2,1,0:T(8,128)(2,1)} %shard_map.49), calls=%async_computation.2 | async-start | bytes 1048576 | tf_op jit(solution)/shard_map/all_to_all | solution.py:345
  66.0 1.9 %collective-permute-start.6 = (bf16[128,2048]{1,0:T(8,128)(2,1)S(1)}, bf16[128,2048]{1,0:T(8,128)(2,1)S(1)}, u32[]{:S(2)}, u32[]{:S(2)}) collective-permute-start(bf16[128,2048]{1,0:T(8,128)(2,1)S(1)} %collective-permute-done.3.refs_1_), channel_id=1, source_target_pairs={{16,0},{49,1},{18,2},{51,3},{20,4},{53,5},{22,6},{55,7},{24,8},{57... | collective-permute-start | bytes 1572872 | tf_op jit(solution)/shard_map/ppermute | solution.py:275
  67.9 4.6 %collective-permute-start.7 = (bf16[128,2048]{1,0:T(8,128)(2,1)}, bf16[128,2048]{1,0:T(8,128)(2,1)}, u32[]{:S(2)}, u32[]{:S(2)}) collective-permute-start(bf16[128,2048]{1,0:T(8,128)(2,1)} %collective-permute-done.4.refs_2_), channel_id=1, source_target_pairs={{16,0},{49,1},{18,2},{51,3},{20,4},{53,5},{22,6},{55,7},{24,8},{57... | collective-permute-start | bytes 1572872 | tf_op jit(solution)/shard_map/ppermute | solution.py:275
  72.5 0.0 collective-permute-done.5.refs_3_
  72.5 1.9 %collective-permute-start.8 = (bf16[128,2048]{1,0:T(8,128)(2,1)}, bf16[128,2048]{1,0:T(8,128)(2,1)S(1)}, u32[]{:S(2)}, u32[]{:S(2)}) collective-permute-start(bf16[128,2048]{1,0:T(8,128)(2,1)} %collective-permute-done.5.refs_3_), channel_id=1, source_target_pairs={{64,0},{449,1},{66,2},{451,3},{68,4},{453,5},{70,6},{455,7},{72,8}... | collective-permute-start | bytes 1572872 | tf_op jit(solution)/shard_map/ppermute | solution.py:275
  74.4 1.9 %collective-permute-start.9 = (bf16[128,2048]{1,0:T(8,128)(2,1)}, bf16[128,2048]{1,0:T(8,128)(2,1)S(1)}, u32[]{:S(2)}, u32[]{:S(2)}) collective-permute-start(bf16[128,2048]{1,0:T(8,128)(2,1)} %collective-permute-done.5.refs_3_), channel_id=1, source_target_pairs={{16,0},{49,1},{18,2},{51,3},{20,4},{53,5},{22,6},{55,7},{24,8},{57... | collective-permute-start | bytes 1572872 | tf_op jit(solution)/shard_map/ppermute | solution.py:275
  76.3 0.8 collective-permute-done.6.refs_4_
  77.1 1.0 %all-to-all-done.2.mixed_ref = bf16[8,256,128]{2,1,0:T(8,128)(2,1)S(1)} async-done(((bf16[8,256,128]{2,1,0:T(8,128)(2,1)}), bf16[8,256,128]{2,1,0:T(8,128)(2,1)S(1)}, u32[]{:S(2)}, u32[]{:S(2)}) %all-to-all-start.2) | async-done | bytes 524320 | tf_op jit(solution)/shard_map/all_to_all | solution.py:345
  78.1 4.9 %collective-permute-done.7.refs_5_ = bf16[128,2048]{1,0:T(8,128)(2,1)} collective-permute-done((bf16[128,2048]{1,0:T(8,128)(2,1)}, bf16[128,2048]{1,0:T(8,128)(2,1)}, u32[]{:S(2)}, u32[]{:S(2)}) %collective-permute-start.7) | collective-permute-done | bytes 524320 | tf_op jit(solution)/shard_map/ppermute | solution.py:275
  83.0 2.3 %shard_map.51.early_ref = f32[256,2048]{1,0:T(8,128)S(1)} custom-call(bf16[8,256,128]{2,1,0:T(8,128)(2,1)S(1)} %all-to-all-done.2.mixed_ref, bf16[128,2048]{1,0:T(8,128)(2,1)S(1)} %shard_map.50.refs_0_, bf16[128,2048]{1,0:T(8,128)(2,1)S(1)} %collective-permute-done.3.refs_1_, bf16[128,2048]{1,0:T(8,128)(2,1)} %collective-permute-done.4.refs_2_, ...), custom_call_target="tpu_custom_call" | custom-call | flops 1 | bytes 67108864 | tf_op jit(solution)/shard_map/pallas_call | solution.py:348
  85.3 0.0 collective-permute-done.8.refs_0_
  85.3 3.3 %collective-permute-done.9.refs_1_ = bf16[128,2048]{1,0:T(8,128)(2,1)S(1)} collective-permute-done((bf16[128,2048]{1,0:T(8,128)(2,1)}, bf16[128,2048]{1,0:T(8,128)(2,1)S(1)}, u32[]{:S(2)}, u32[]{:S(2)}) %collective-permute-start.9) | collective-permute-done | bytes 524320 | tf_op jit(solution)/shard_map/ppermute | solution.py:275
  88.6 0.4 shard_map.52
  89.1 9.7 %collective-permute-start.10 = (bf16[128,2048]{1,0:T(8,128)(2,1)S(1)}, bf16[128,2048]{1,0:T(8,128)(2,1)S(1)}, u32[]{:S(2)}, u32[]{:S(2)}) collective-permute-start(bf16[128,2048]{1,0:T(8,128)(2,1)S(1)} %get-tuple-element.22), channel_id=1, source_target_pairs={{0,1},{1,0},{2,3},{3,2},{4,5},{5,4},{6,7},{7,6},{8,9},{9,8},{10,11... | collective-permute-start | bytes 1572872 | tf_op jit(solution)/shard_map/ppermute | solution.py:350
  98.8 1.5 %collective-permute-done.10.taken_ref = bf16[128,2048]{1,0:T(8,128)(2,1)S(1)} collective-permute-done((bf16[128,2048]{1,0:T(8,128)(2,1)S(1)}, bf16[128,2048]{1,0:T(8,128)(2,1)S(1)}, u32[]{:S(2)}, u32[]{:S(2)}) %collective-permute-start.10) | collective-permute-done | bytes 524320 | tf_op jit(solution)/shard_map/ppermute | solution.py:350
  100.3 0.9 shard_map.53
  (1 shorter events, 0.0 us)
Async XLA Ops:
  0.0 50.6 %copy-start = (bf16[2048,128]{1,0:T(8,128)(2,1)S(1)}, bf16[2048,128]{1,0:T(8,128)(2,1)}, u32[]{:S(2)}) copy-start(bf16[2048,128]{1,0:T(8,128)(2,1)} %k_ref.3) | copy-start | bytes 1572868
  0.0 50.6 %copy-start.1 = (bf16[2048,128]{1,0:T(8,128)(2,1)S(1)}, bf16[2048,128]{1,0:T(8,128)(2,1)}, u32[]{:S(2)}) copy-start(bf16[2048,128]{1,0:T(8,128)(2,1)} %v_ref.3) | copy-start | bytes 1572868
  0.0 50.6 %copy-start.2 = (bf16[2048,128]{1,0:T(8,128)(2,1)S(1)}, bf16[2048,128]{1,0:T(8,128)(2,1)}, u32[]{:S(2)}) copy-start(bf16[2048,128]{1,0:T(8,128)(2,1)} %q_ref.3) | copy-start | bytes 1572868
  0.0 10.2 %collective-permute-start.1 = (bf16[64,2048]{1,0:T(8,128)(2,1)}, bf16[64,2048]{1,0:T(8,128)(2,1)S(1)}, u32[]{:S(2)}, u32[]{:S(2)}) collective-permute-start(bf16[64,2048]{1,0:T(8,128)(2,1)} %param.7), channel_id=1, source_target_pairs={{1,0},{33,1},{3,2},{35,3},{5,4},{37,5},{7,6},{39,7},{9,8},{41,9},{... | collective-permute-start | bytes 786440 | tf_op jit(solution)/shard_map/ppermute | solution.py:275
  3.2 10.6 %collective-permute-start.2 = (bf16[64,2048]{1,0:T(8,128)(2,1)}, bf16[64,2048]{1,0:T(8,128)(2,1)S(1)}, u32[]{:S(2)}, u32[]{:S(2)}) collective-permute-start(bf16[64,2048]{1,0:T(8,128)(2,1)} %param.7), channel_id=1, source_target_pairs={{17,0},{49,1},{19,2},{51,3},{21,4},{53,5},{23,6},{55,7},{25,8},{57... | collective-permute-start | bytes 786440 | tf_op jit(solution)/shard_map/ppermute | solution.py:275
  13.9 11.2 %collective-permute-start.3 = (bf16[128,2048]{1,0:T(8,128)(2,1)S(1)}, bf16[128,2048]{1,0:T(8,128)(2,1)S(1)}, u32[]{:S(2)}, u32[]{:S(2)}) collective-permute-start(bf16[128,2048]{1,0:T(8,128)(2,1)S(1)} %shard_map.50.refs_0_), channel_id=1, source_target_pairs={{64,0},{449,1},{66,2},{451,3},{68,4},{453,5},{70,6},{455,7},{72,8}... | collective-permute-start | bytes 1572872 | tf_op jit(solution)/shard_map/ppermute | solution.py:275
  19.4 12.1 %all-to-all-start = ((f32[4,128,128]{2,1,0:T(8,128)}), f32[4,128,128]{2,1,0:T(8,128)S(1)}, u32[]{:S(2)}, u32[]{:S(2)}) async-start(f32[4,128,128]{2,1,0:T(8,128)} %get-tuple-element.16), calls=%async_computation | async-start | bytes 524288 | tf_op jit(solution)/shard_map/all_to_all | solution.py:322
  25.0 12.4 %collective-permute-start.4 = (bf16[128,2048]{1,0:T(8,128)(2,1)S(1)}, bf16[128,2048]{1,0:T(8,128)(2,1)}, u32[]{:S(2)}, u32[]{:S(2)}) collective-permute-start(bf16[128,2048]{1,0:T(8,128)(2,1)S(1)} %collective-permute-done.3.refs_1_), channel_id=1, source_target_pairs={{64,0},{449,1},{66,2},{451,3},{68,4},{453,5},{70,6},{455,7},{72,8}... | collective-permute-start | bytes 1572872 | tf_op jit(solution)/shard_map/ppermute | solution.py:275
  29.6 15.4 %collective-permute-start = (bf16[2,1024,128]{2,1,0:T(8,128)(2,1)}, bf16[2,1024,128]{2,1,0:T(8,128)(2,1)S(1)}, u32[]{:S(2)}, u32[]{:S(2)}) collective-permute-start(bf16[2,1024,128]{2,1,0:T(8,128)(2,1)} %get-tuple-element.14), channel_id=1, source_target_pairs={{0,16},{16,32},{32,48},{48,64},{64,80},{80,96},{96,112},{112,128},... | collective-permute-start | bytes 1572872 | tf_op jit(solution)/shard_map/ppermute | solution.py:325
  31.6 0.7 copy-start.4
  32.3 18.3 %all-to-all-start.1 = ((bf16[8,128,128]{2,1,0:T(8,128)(2,1)}), bf16[8,128,128]{2,1,0:T(8,128)(2,1)S(1)}, u32[]{:S(2)}, u32[]{:S(2)}) async-start(bf16[8,128,128]{2,1,0:T(8,128)(2,1)} %copy-done.4), calls=%async_computation.1 | async-start | bytes 524288 | tf_op jit(solution)/shard_map/all_to_all | solution.py:327
  37.4 35.0 %collective-permute-start.5 = (bf16[128,2048]{1,0:T(8,128)(2,1)}, bf16[128,2048]{1,0:T(8,128)(2,1)}, u32[]{:S(2)}, u32[]{:S(2)}) collective-permute-start(bf16[128,2048]{1,0:T(8,128)(2,1)} %collective-permute-done.4.refs_2_), channel_id=1, source_target_pairs={{64,0},{449,1},{66,2},{451,3},{68,4},{453,5},{70,6},{455,7},{72,8}... | collective-permute-start | bytes 1572872 | tf_op jit(solution)/shard_map/ppermute | solution.py:275
  50.6 1.0 %copy-start.3 = (f32[8,128,128]{2,1,0:T(8,128)S(1)}, f32[8,128,128]{2,1,0:T(8,128)}, u32[]{:S(2)}) copy-start(f32[8,128,128]{2,1,0:T(8,128)} %get-tuple-element.15.within_ref) | copy-start | bytes 1572868
  58.5 19.6 %all-to-all-start.2 = ((bf16[8,256,128]{2,1,0:T(8,128)(2,1)}), bf16[8,256,128]{2,1,0:T(8,128)(2,1)S(1)}, u32[]{:S(2)}, u32[]{:S(2)}) async-start(bf16[8,256,128]{2,1,0:T(8,128)(2,1)} %shard_map.49), calls=%async_computation.2 | async-start | bytes 1048576 | tf_op jit(solution)/shard_map/all_to_all | solution.py:345
  66.0 11.1 %collective-permute-start.6 = (bf16[128,2048]{1,0:T(8,128)(2,1)S(1)}, bf16[128,2048]{1,0:T(8,128)(2,1)S(1)}, u32[]{:S(2)}, u32[]{:S(2)}) collective-permute-start(bf16[128,2048]{1,0:T(8,128)(2,1)S(1)} %collective-permute-done.3.refs_1_), channel_id=1, source_target_pairs={{16,0},{49,1},{18,2},{51,3},{20,4},{53,5},{22,6},{55,7},{24,8},{57... | collective-permute-start | bytes 1572872 | tf_op jit(solution)/shard_map/ppermute | solution.py:275
  67.9 15.1 %collective-permute-start.7 = (bf16[128,2048]{1,0:T(8,128)(2,1)}, bf16[128,2048]{1,0:T(8,128)(2,1)}, u32[]{:S(2)}, u32[]{:S(2)}) collective-permute-start(bf16[128,2048]{1,0:T(8,128)(2,1)} %collective-permute-done.4.refs_2_), channel_id=1, source_target_pairs={{16,0},{49,1},{18,2},{51,3},{20,4},{53,5},{22,6},{55,7},{24,8},{57... | collective-permute-start | bytes 1572872 | tf_op jit(solution)/shard_map/ppermute | solution.py:275
  72.5 12.9 %collective-permute-start.8 = (bf16[128,2048]{1,0:T(8,128)(2,1)}, bf16[128,2048]{1,0:T(8,128)(2,1)S(1)}, u32[]{:S(2)}, u32[]{:S(2)}) collective-permute-start(bf16[128,2048]{1,0:T(8,128)(2,1)} %collective-permute-done.5.refs_3_), channel_id=1, source_target_pairs={{64,0},{449,1},{66,2},{451,3},{68,4},{453,5},{70,6},{455,7},{72,8}... | collective-permute-start | bytes 1572872 | tf_op jit(solution)/shard_map/ppermute | solution.py:275
  74.4 14.2 %collective-permute-start.9 = (bf16[128,2048]{1,0:T(8,128)(2,1)}, bf16[128,2048]{1,0:T(8,128)(2,1)S(1)}, u32[]{:S(2)}, u32[]{:S(2)}) collective-permute-start(bf16[128,2048]{1,0:T(8,128)(2,1)} %collective-permute-done.5.refs_3_), channel_id=1, source_target_pairs={{16,0},{49,1},{18,2},{51,3},{20,4},{53,5},{22,6},{55,7},{24,8},{57... | collective-permute-start | bytes 1572872 | tf_op jit(solution)/shard_map/ppermute | solution.py:275
  89.1 11.3 %collective-permute-start.10 = (bf16[128,2048]{1,0:T(8,128)(2,1)S(1)}, bf16[128,2048]{1,0:T(8,128)(2,1)S(1)}, u32[]{:S(2)}, u32[]{:S(2)}) collective-permute-start(bf16[128,2048]{1,0:T(8,128)(2,1)S(1)} %get-tuple-element.22), channel_id=1, source_target_pairs={{0,1},{1,0},{2,3},{3,2},{4,5},{5,4},{6,7},{7,6},{8,9},{9,8},{10,11... | collective-permute-start | bytes 1572872 | tf_op jit(solution)/shard_map/ppermute | solution.py:350
